TPU v7x, 256 devices: a whole 4x4x8 slice. The times are simulated.
256 devices in a mesh: batch: 4 (over z_lo, core), row: 4 (over x), col: 16 (over y, z_hi).
Axes of the slice: x: 4, y: 4, z: 8 (z_hi: 4, z_lo: 2; z = z_hi * 2 + z_lo), core: 2. Of those that a mesh axis runs over, the one named last changes fastest.
Arguments:
- embeddings: bfloat16 [512, 128, 512], P('batch', 'col', 'row'), may hold values from -170 to 170
- projection: bfloat16 [512, 32], replicated, may hold values from -0.25 to 0.25
- w_in: bfloat16 [16384, 2048], P('row', 'col'), may hold values from -0.046875 to 0.046875
- bias: float32 [2048], P('col'), may hold values from -3 to 3
- w_out: bfloat16 [2048, 128, 512], P(None, 'col', 'row'), may hold values from -0.125 to 0.125
- cotangent: bfloat16 [512, 128, 512], P('batch', 'col', 'row'), may hold values from -0.1796875 to 0.1796875
Outputs:
- mixed: bfloat16 [512, 128, 512], P('batch', 'col', 'row')
- grad_out: float32 [2048, 128, 512], P('batch', 'col', 'row')
- grad_in: float32 [16384, 2048], P('row', 'col')
- grad_bias: float32 [2048], P('col')
- grad_proj: float32 [512, 32], P('row')
All inputs are finite; a program needn't handle non-finite values.
Results may differ from a plain program's by a relative error of at most 0.006.
Values may be sent and summed in bfloat16 or wider, within the bound.
A program may use at most 128 MiB of HBM per device.

v0:
```python
import jax
import jax.numpy as jnp
from jax import lax
from jax.sharding import PartitionSpec as P

epsilon = 1e-06


def copy_for_each(array, axis):
    size = lax.axis_size(axis)
    return lax.all_to_all(
        jnp.broadcast_to(array[None], (size, *array.shape)), axis, 0, 0, tiled=True
    )


def of_everyone(array, axis):
    everything = copy_for_each(array, axis)
    return jnp.sum(everything, axis=0)


def joined_along(tiles, dim):
    tiles = jnp.moveaxis(tiles, 0, dim)
    lengths = tiles.shape
    return tiles.reshape(*lengths[:dim], lengths[dim] * lengths[dim + 1], *lengths[dim + 2 :])


def gathered_copies(array, axis, dim):
    return joined_along(copy_for_each(array, axis), dim)


def cut_along(array, dim, size):
    lengths = array.shape
    tiles = array.reshape(*lengths[:dim], size, lengths[dim] // size, *lengths[dim + 1 :])
    return jnp.moveaxis(tiles, dim, 0)


def sent_and_summed(array, axis, dim):
    size = lax.axis_size(axis)
    tiles = lax.all_to_all(cut_along(array, dim, size), axis, 0, 0, tiled=True)
    return jnp.sum(tiles, axis=0)


def in_one_piece(arrays, axis, dim, along):
    both = jnp.concatenate(arrays, axis=along)
    whole, at, gathered = (lax.all_gather(both, axis, axis=dim, tiled=True), 0, [])
    for a in arrays:
        gathered.append(lax.slice_in_dim(whole, at, at + a.shape[along], axis=along))
        at += a.shape[along]
    return tuple(gathered)


def filled_up(lines, size):
    spare = -lines.shape[0] % size
    if not spare:
        return lines
    return jnp.concatenate([lines, jnp.zeros((spare, *lines.shape[1:]), lines.dtype)])


def sum_by_parts(array, axis):
    lines = array.reshape(-1, *array.shape[1:][-1:])
    padded = filled_up(lines, lax.axis_size(axis))
    own = lax.psum_scatter(padded, axis, scatter_dimension=0, tiled=True)
    whole = lax.all_gather(own, axis, axis=0, tiled=True)
    return whole[: len(lines)].reshape(array.shape)


def contract_first(left, right):
    return lax.dot_general(
        left, right, (((0,), (0,)), ((), ())), preferred_element_type=jnp.float32
    )


def contract_last(left, right):
    return lax.dot_general(
        left, right, (((1,), (1,)), ((), ())), preferred_element_type=jnp.float32
    )


def local(embeddings, projection, w_in, bias, w_out, cotangent):
    highest = lax.Precision.HIGHEST
    tok_rows, feat_local, emb_local = embeddings.shape
    rank_cols = projection.shape[1]
    row_count = lax.axis_size("row")
    row_place = lax.axis_index("row")
    emb_float = embeddings.astype(jnp.float32)
    own_proj = lax.dynamic_slice_in_dim(projection, row_place * emb_local, emb_local, 0)
    folded = of_everyone(
        jnp.einsum("bde,ek->bdk", embeddings, own_proj, preferred_element_type=jnp.float32), "row"
    )
    partial_value = jnp.einsum("bde,bdk->bek", emb_float, folded, precision=highest)
    interact = lax.psum(partial_value, "col")
    feature_count = emb_local * row_count * rank_cols
    square_sum = of_everyone(jnp.sum(interact * interact, axis=(1, 2)), "row")
    inv_rms = lax.rsqrt(square_sum / feature_count + epsilon)[:, None, None]
    normed = interact * inv_rms
    activated = normed.astype(jnp.bfloat16).reshape(tok_rows, emb_local * rank_cols)
    preact = of_everyone(jnp.dot(activated, w_in, preferred_element_type=jnp.float32), "row") + bias
    hidden = jax.nn.silu(preact).astype(jnp.bfloat16)
    hidden_all = gathered_copies(hidden, "col", 1)
    flat_out = w_out.reshape(w_out.shape[0], feat_local * emb_local)
    mixed = (
        jnp.dot(hidden_all, flat_out, preferred_element_type=jnp.float32)
        .astype(jnp.bfloat16)
        .reshape(tok_rows, feat_local, emb_local)
    )
    cot_rows = cotangent.reshape(tok_rows, feat_local * emb_local)
    d_cols = sent_and_summed(contract_last(cot_rows, flat_out), "col", 1)
    d_hidden = of_everyone(d_cols, "row")
    sigmoid_pre = jax.nn.sigmoid(preact)
    d_preact = d_hidden * sigmoid_pre * (1.0 + preact * (1.0 - sigmoid_pre))
    d_pre_b = d_preact.astype(jnp.bfloat16)
    per_batch = w_out.shape[0] // lax.axis_size("batch")
    every_hidden, every_cot = in_one_piece((hidden_all, cot_rows), "batch", 0, 1)
    own_hidden = lax.dynamic_slice_in_dim(
        every_hidden, lax.axis_index("batch") * per_batch, per_batch, 1
    )
    grad_flat = contract_first(own_hidden, every_cot)
    grad_out = grad_flat.reshape(per_batch, feat_local, emb_local)
    grad_in, grad_bias = lax.psum(
        (contract_first(activated, d_pre_b), jnp.sum(d_preact, axis=0)), "batch"
    )
    d_act = sum_by_parts(contract_last(d_pre_b, w_in), "col").reshape(
        tok_rows, emb_local, rank_cols
    )
    inner_term = of_everyone(jnp.sum(d_act * normed, axis=(1, 2)), "row") / feature_count
    d_inter = (inv_rms * (d_act - normed * inner_term[:, None, None])).astype(jnp.bfloat16)
    back_fold = of_everyone(
        jnp.einsum("bek,bde->bdk", d_inter, embeddings, preferred_element_type=jnp.float32), "row"
    )
    grad_proj = of_everyone(
        jnp.einsum("bde,bdk->ek", emb_float, back_fold, precision=highest), ("batch", "col")
    )
    return (mixed, grad_out, grad_in, grad_bias, grad_proj)


def solution(mesh):
    placed = (
        P("batch", "col", "row"),
        P(),
        P("row", "col"),
        P("col"),
        P(None, "col", "row"),
        P("batch", "col", "row"),
    )
    return jax.shard_map(
        local,
        mesh=mesh,
        in_specs=placed,
        out_specs=(
            P("batch", "col", "row"),
            P("batch", "col", "row"),
            P("row", "col"),
            P("col"),
            P("row", None),
        ),
        check_vma=False,
    )
```

profile of v0, /device:TPU:1, one launch (start us, length us, event | category | flops | bytes accessed | tf_op | source)
XLA Modules:
  0.0 535.5 jit_solution(8240638500809765838)
XLA Ops:
  9.3 4.8 all-to-all-start
  14.4 7.4 %dot_general.47 = bf16[16,128,1024]{2,1,0:T(8,128)(2,1)} reshape(bf16[2048,8,128]{2,1,0:T(8,128)(2,1)} %param.10) | data formatting | bytes 8388608 | tf_op jit(solution)/shard_map/dot_general | solution.py:74
  22.1 3.2 convolution_bitcast_fusion.1
  25.3 4.7 convolution_bitcast_fusion.2
  30.0 11.6 %all-to-all-start.4 = ((f32[16,128,128]{2,1,0:T(8,128)}), f32[16,128,128]{2,1,0:T(8,128)}, u32[]{:S(2)}, u32[]{:S(2)}) async-start(f32[16,128,128]{2,1,0:T(8,128)} %convolution_bitcast_fusion.2), calls=%async_computation.4 | async-start | bytes 2097152 | tf_op jit(solution)/shard_map/all_to_all | solution.py:39
  41.6 172.1 %all-reduce.3.cloned.1.call-done = f32[128,128,32]{1,2,0:T(8,128)} async-done(((f32[128,128,32]{1,2,0:T(8,128)}), f32[128,128,32]{1,2,0:T(8,128)}) %all-reduce.3.cloned.1.call-update) | async-done | bytes 2097168 | tf_op jit(solution)/shard_map/psum | solution.py:91
  213.7 2.8 multiply_reduce_fusion.1
  217.0 3.3 all-to-all-start.1
  221.6 2.8 all-to-all-done.1
  225.1 4.0 all-to-all-start.5
  230.4 3.3 copy.58
  236.1 4.2 all-to-all-start.2
  241.3 5.8 %all-to-all-done.2 = f32[4,128,128]{2,1,0:T(8,128)} async-done(((f32[4,128,128]{2,1,0:T(8,128)}), f32[4,128,128]{2,1,0:T(8,128)}, u32[]{:S(2)}, u32[]{:S(2)}) %all-to-all-start.2) | async-done | bytes 262176 | tf_op jit(solution)/shard_map/all_to_all | solution.py:11
  249.6 1.8 fusion.15
  251.4 95.4 %reduce-scatter.2.cloned.1.call-done = f32[8,4096]{1,0:T(8,128)} async-done(((f32[128,4096]{1,0:T(8,128)}), f32[8,4096]{1,0:T(8,128)}) %reduce-scatter.2.cloned.1.call-update) | async-done | bytes 131088 | tf_op jit(solution)/shard_map/reduce_scatter | solution.py:62
  347.1 23.1 %all_to_all.47 = bf16[16,128,128]{1,2,0:T(8,128)(2,1)S(1)} all-to-all(bf16[16,128,128]{1,2,0:T(8,128)(2,1)S(1)} %broadcast_in_dim.19), channel_id=1, replica_groups=mesh['batch'=4,'row'=4,'col'=16] {'col'}, dimensions={0} | all-to-all | bytes 1048576 | tf_op jit(solution)/shard_map/all_to_all | solution.py:11
  371.0 1.9 pad_maximum_fusion
  372.9 34.7 %all-gather.5.cloned.1.call-done = f32[128,4096]{1,0:T(8,128)} async-done(((f32[8,4096]{1,0:T(8,128)}), f32[128,4096]{1,0:T(8,128)}) %all-gather.5.cloned.1.call-update) | async-done | bytes 2097168 | tf_op jit(solution)/shard_map/all_gather | solution.py:63
  407.6 2.9 copy.62
  410.5 3.4 copy.65
  413.9 3.5 multiply_reduce_fusion
  417.3 8.2 %all_to_all.48 = f32[4,1,128]{2,1,0:T(1,128)S(1)} all-to-all(f32[4,1,128]{2,1,0:T(1,128)S(1)} %broadcast_in_dim.21), channel_id=1, replica_groups=mesh['batch'=4,'row'=4,'col'=16] {'row'}, dimensions={0} | all-to-all | bytes 4096 | tf_op jit(solution)/shard_map/all_to_all | solution.py:11
  425.5 3.1 convolution_bitcast_fusion.3
  430.8 3.5 all-to-all-start.7
  436.2 5.1 all-to-all-done.7
  442.6 10.9 %all-to-all-start.8 = ((f32[64,128,32]{1,2,0:T(8,128)}), f32[64,128,32]{1,2,0:T(8,128)S(1)}, u32[]{:S(2)}, u32[]{:S(2)}) async-start(f32[64,128,32]{1,2,0:T(8,128)} %broadcast_in_dim.23), calls=%async_computation.9 | async-start | bytes 2097152 | tf_op jit(solution)/shard_map/all_to_all | solution.py:11
  453.6 33.7 %psum.23 = f32[128]{0:T(128)} all-reduce(f32[128]{0:T(128)S(1)} %get-tuple-element.5), channel_id=1, replica_groups=mesh['batch'=4,'row'=4,'col'=16] {'batch'}, use_global_device_ids=true, to_apply=%region_9.10 | all-reduce | flops 128 | bytes 1024 | tf_op jit(solution)/shard_map/psum | solution.py:119
  487.3 3.0 fusion.6
  492.6 2.0 convolution_bitcast_fusion
  494.6 1.8 copy.72
  497.1 28.8 %all-reduce.5.cloned.1.call-done = f32[4096,128]{1,0:T(8,128)} async-done(((f32[4096,128]{1,0:T(8,128)}), f32[4096,128]{1,0:T(8,128)}) %all-reduce.5.cloned.1.call-update) | async-done | bytes 2097168 | tf_op jit(solution)/shard_map/psum | solution.py:119
  525.9 3.0 copy.87
  (64 shorter events, 22.0 us)
Async XLA Ops:
  7.2 226.5 %copy-start = (bf16[4096,128]{1,0:T(8,128)(2,1)S(1)}, bf16[4096,128]{1,0:T(8,128)(2,1)}, u32[]{:S(2)}) copy-start(bf16[4096,128]{1,0:T(8,128)(2,1)} %param.8) | copy-start | bytes 3145732
  7.2 7.0 %copy-start.7 = (bf16[128,8,128]{2,1,0:T(8,128)(2,1)S(1)}, bf16[128,8,128]{2,1,0:T(8,128)(2,1)}, u32[]{:S(2)}) copy-start(bf16[128,8,128]{2,1,0:T(8,128)(2,1)} %param.11) | copy-start | bytes 786436
  9.3 12.5 %all-to-all-start = ((f32[4,128,8,32]{1,3,2,0:T(8,128)}), f32[4,128,8,32]{1,3,2,0:T(8,128)S(1)}, u32[]{:S(2)}, u32[]{:S(2)}) async-start(f32[4,128,8,32]{1,3,2,0:T(8,128)} %broadcast_in_dim.16), calls=%async_computation | async-start | bytes 1048576 | tf_op jit(solution)/shard_map/all_to_all | solution.py:11
  14.2 199.5 %all-reduce.3.cloned.1.call-start = ((), (), s32[]{:S(2)}) async-start(), calls=%async_computation.10 | async-start | bytes 4194304 | tf_op jit(solution)/shard_map/psum | solution.py:91
  14.4 10.9 %copy-start.4 = (bf16[128,8,128]{0,2,1:T(8,128)(2,1)}, bf16[128,8,128]{0,2,1:T(8,128)(2,1)S(1)}, u32[]{:S(2)}) copy-start(bf16[128,8,128]{0,2,1:T(8,128)(2,1)S(1)} %copy.60) | copy-start | bytes 786436
  14.4 7.7 %copy-start.3 = (bf16[128,8,128]{2,1,0:T(8,128)(2,1)S(1)}, bf16[128,8,128]{2,1,0:T(8,128)(2,1)}, u32[]{:S(2)}) copy-start(bf16[128,8,128]{2,1,0:T(8,128)(2,1)} %param.6) | copy-start | bytes 786436
  30.0 186.4 %all-to-all-start.4 = ((f32[16,128,128]{2,1,0:T(8,128)}), f32[16,128,128]{2,1,0:T(8,128)}, u32[]{:S(2)}, u32[]{:S(2)}) async-start(f32[16,128,128]{2,1,0:T(8,128)} %convolution_bitcast_fusion.2), calls=%async_computation.4 | async-start | bytes 2097152 | tf_op jit(solution)/shard_map/all_to_all | solution.py:39
  213.7 15.5 %copy-start.1 = (f32[128,128,32]{1,2,0:T(8,128)S(1)}, f32[128,128,32]{1,2,0:T(8,128)}, u32[]{:S(2)}) copy-start(f32[128,128,32]{1,2,0:T(8,128)} %all-reduce.3.cloned.1.call-done) | copy-start | bytes 6291460
  217.0 7.4 %all-to-all-start.1 = ((f32[4,1,128]{2,1,0:T(1,128)}), f32[4,1,128]{2,1,0:T(1,128)S(1)}, u32[]{:S(2)}, u32[]{:S(2)}) async-start(f32[4,1,128]{2,1,0:T(1,128)} %broadcast_in_dim.17), calls=%async_computation.1 | async-start | bytes 4096 | tf_op jit(solution)/shard_map/all_to_all | solution.py:11
  225.1 10.3 %all-to-all-start.5 = ((f32[4,128,128]{2,1,0:T(8,128)}), f32[4,128,128]{2,1,0:T(8,128)}, u32[]{:S(2)}, u32[]{:S(2)}) async-start(f32[4,128,128]{2,1,0:T(8,128)} %broadcast_in_dim.20), calls=%async_computation.5 | async-start | bytes 524288 | tf_op jit(solution)/shard_map/all_to_all | solution.py:11
  233.7 15.0 %copy-start.8 = (f32[128]{0:T(128)S(1)}, f32[128]{0:T(128)}, u32[]{:S(2)}) copy-start(f32[128]{0:T(128)} %param.9) | copy-start | bytes 1540
  236.1 10.9 %all-to-all-start.2 = ((f32[4,128,128]{2,1,0:T(8,128)}), f32[4,128,128]{2,1,0:T(8,128)}, u32[]{:S(2)}, u32[]{:S(2)}) async-start(f32[4,128,128]{2,1,0:T(8,128)} %broadcast_in_dim.18), calls=%async_computation.2 | async-start | bytes 524288 | tf_op jit(solution)/shard_map/all_to_all | solution.py:11
  240.3 106.5 %reduce-scatter.2.cloned.1.call-start = ((), (), s32[]{:S(2)}) async-start(), calls=%async_computation.13 | async-start | bytes 2228224 | tf_op jit(solution)/shard_map/reduce_scatter | solution.py:62
  251.4 156.3 %all-gather.5.cloned.1.call-start = ((), (), s32[]{:S(2)}) async-start(), calls=%async_computation.14 | async-start | bytes 2228224 | tf_op jit(solution)/shard_map/all_gather | solution.py:63
  346.9 144.2 %all-gather.3.cloned.1.call-start = ((), (), s32[]{:S(2)}) async-start(), calls=%async_computation.11 | async-start | bytes 3932160 | tf_op jit(solution)/shard_map/all_gather | solution.py:45
  370.2 0.8 copy-start.5
  428.7 5.7 %copy-start.2 = (bf16[128,128,32]{0,2,1:T(8,128)(2,1)S(1)}, bf16[128,128,32]{0,2,1:T(8,128)(2,1)}, u32[]{:S(2)}) copy-start(bf16[128,128,32]{0,2,1:T(8,128)(2,1)} %copy.58) | copy-start | bytes 3145732
  430.8 10.4 %all-to-all-start.7 = ((f32[4,128,8,32]{1,3,2,0:T(8,128)}), f32[4,128,8,32]{1,3,2,0:T(8,128)S(1)}, u32[]{:S(2)}, u32[]{:S(2)}) async-start(f32[4,128,8,32]{1,3,2,0:T(8,128)} %broadcast_in_dim.22), calls=%async_computation.8 | async-start | bytes 1048576 | tf_op jit(solution)/shard_map/all_to_all | solution.py:11
  434.3 91.6 %all-reduce.5.cloned.1.call-start = ((), (), s32[]{:S(2)}) async-start(), calls=%async_computation.12 | async-start | bytes 4194304 | tf_op jit(solution)/shard_map/psum | solution.py:119
  436.1 51.2 %copy-start.6 = (bf16[16,128,128]{1,2,0:T(8,128)(2,1)S(1)}, bf16[16,128,128]{1,2,0:T(8,128)(2,1)}, u32[]{:S(2)}) copy-start(bf16[16,128,128]{1,2,0:T(8,128)(2,1)} %copy-done.5) | copy-start | bytes 1572868
  442.6 53.8 %all-to-all-start.8 = ((f32[64,128,32]{1,2,0:T(8,128)}), f32[64,128,32]{1,2,0:T(8,128)S(1)}, u32[]{:S(2)}, u32[]{:S(2)}) async-start(f32[64,128,32]{1,2,0:T(8,128)} %broadcast_in_dim.23), calls=%async_computation.9 | async-start | bytes 2097152 | tf_op jit(solution)/shard_map/all_to_all | solution.py:11
  491.1 1.6 slice-start
Sparse Core Ops, SparseCore 0:
  25.4 188.1 all-reduce.2
  251.5 95.3 reduce-scatter.1
  349.3 58.3 all-gather.4
  409.3 39.9 all-gather.2
  452.4 73.5 all-reduce.4
where the time goes:
time: 537 us; the launch traced here: 536 us
  waiting for transfers between devices  345 us (64%)
  blocking collectives  65 us (12%)
  starting transfers between devices  42.5 us (8%)
  local copies, waits for them, and re-layouts  31.8 us (6%)
  matrix products  22.6 us (4%)
  other arithmetic  14.9 us (3%)
  between operations  14 us (3%)
    psum x1, waiting for transfers between devices, local(): interact = lax.psum(partial_value, 'col')  172 us
    reduce_scatter x1, waiting for transfers between devices, sum_by_parts(): own = lax.psum_scatter(padded, axis, scatter_dimension=0, tiled=True)  95.4 us
    all_gather x1, waiting for transfers between devices, sum_by_parts(): whole = lax.all_gather(own, axis, axis=0, tiled=True)  34.7 us
    psum x1, blocking collectives, local(): lax.psum((contract_first(activated, d_pre_b), jnp.sum(d_preact, axis=0)),...  33.7 us
    all_to_all x2, blocking collectives, copy_for_each(): lax.all_to_all(jnp.broadcast_to(array[None], (size, *array.shape)), axis,...  31.3 us
    all_to_all x6, starting transfers between devices, copy_for_each(): lax.all_to_all(jnp.broadcast_to(array[None], (size, *array.shape)), axis,...  30.8 us
    psum x1, waiting for transfers between devices, local(): lax.psum((contract_first(activated, d_pre_b), jnp.sum(d_preact, axis=0)),...  28.8 us
    all_to_all x6, waiting for transfers between devices, copy_for_each(): lax.all_to_all(jnp.broadcast_to(array[None], (size, *array.shape)), axis,...  13.6 us
  transfers between devices with their start and end apart: 12, of which 7 were waited for; matrix products, arithmetic and copies ran while one was open for 10% of the time, Pallas kernels for 0%

commit v1 on v0

v1 whole, which is shorter than its diff:
```python
import jax
import jax.numpy as jnp
from jax import lax
from jax.sharding import PartitionSpec as P

epsilon = 1e-06
bf16 = jnp.bfloat16
f32 = jnp.float32


def swap(tiles, axis):
    return lax.all_to_all(tiles, axis, 0, 0, tiled=True)


def everyone(array, axis):
    size = lax.axis_size(axis)
    return swap(jnp.broadcast_to(array[None], (size, *array.shape)), axis)


def contract_last(left, right):
    return lax.dot_general(left, right, (((1,), (1,)), ((), ())), preferred_element_type=f32)


def contract_first(left, right):
    return lax.dot_general(left, right, (((0,), (0,)), ((), ())), preferred_element_type=f32)


def summed(tiles):
    return jnp.sum(tiles.astype(f32), axis=0)


def local(embeddings, projection, w_in, bias, w_out, cotangent):
    highest = lax.Precision.HIGHEST
    toks, feat, embs = embeddings.shape
    rank = projection.shape[1]
    rows, cols, batches = lax.axis_size("row"), lax.axis_size("col"), lax.axis_size("batch")
    own = toks // (rows * cols)
    hid = w_out.shape[0]
    hid_local = w_in.shape[1]
    flat_out = w_out.reshape(hid, feat * embs)
    cot_rows = cotangent.reshape(toks, feat * embs)
    partial = contract_last(cot_rows, flat_out).astype(bf16)
    partial = jnp.moveaxis(partial.reshape(toks, cols, hid_local), 1, 0)
    d_cols = summed(swap(partial, "col"))
    d_hidden = jnp.sum(everyone(d_cols, "row"), axis=0)
    every_cot = everyone(cot_rows, "batch")
    emb = swap(embeddings.reshape(cols * rows, own, feat, embs), ("col", "row"))
    emb = emb.reshape(cols, rows, own, feat, embs).transpose(2, 0, 3, 1, 4)
    emb = emb.reshape(own, cols * feat, rows * embs)
    emb_float = emb.astype(f32)
    folded = jnp.einsum("bde,ek->bdk", emb, projection, preferred_element_type=f32)
    interact = jnp.einsum("bde,bdk->bek", emb_float, folded, precision=highest)
    count = rows * embs * rank
    inv_rms = lax.rsqrt(jnp.sum(interact * interact, axis=(1, 2)) / count + epsilon)[:, None, None]
    normed = interact * inv_rms
    activated = normed.astype(bf16).reshape(own, rows, embs * rank)
    act = swap(jnp.moveaxis(activated, 1, 0), "row").reshape(rows * own, embs * rank)
    act = everyone(act, "col").reshape(toks, embs * rank)
    pre = jnp.dot(act, w_in, preferred_element_type=f32)
    preact = jnp.sum(everyone(pre, "row"), axis=0) + bias
    hidden = jax.nn.silu(preact).astype(bf16)
    sig = jax.nn.sigmoid(preact)
    d_preact = d_hidden * sig * (1.0 + preact * (1.0 - sig))
    d_pre_b = d_preact.astype(bf16)
    d_part = contract_last(d_pre_b, w_in).astype(bf16).reshape(cols, rows * own, embs * rank)
    d_rows = summed(swap(d_part, "col")).astype(bf16)
    d_act = swap(d_rows.reshape(rows, own, embs * rank), "row").astype(f32)
    d_act = jnp.moveaxis(d_act, 0, 1).reshape(own, rows * embs, rank)
    inner = (jnp.sum(d_act * normed, axis=(1, 2)) / count)[:, None, None]
    d_inter = (inv_rms * (d_act - normed * inner)).astype(bf16)
    back_fold = jnp.einsum("bek,bde->bdk", d_inter, emb, preferred_element_type=f32)
    part_proj = jnp.einsum("bde,bdk->ek", emb_float, back_fold, precision=highest)
    part_proj = jnp.sum(swap(part_proj.reshape(rows, embs, rank), "row"), axis=0)
    everywhere = ("batch", "col")
    group = batches * cols
    share = jnp.sum(swap(part_proj.reshape(group, -1), everywhere), axis=0)
    grad_proj = everyone(share, everywhere).reshape(embs, rank)
    hidden_all = everyone(hidden, "col")
    mixed = jnp.dot(
        jnp.moveaxis(hidden_all, 0, 1).reshape(toks, hid), flat_out, preferred_element_type=f32
    )
    mixed = mixed.astype(bf16).reshape(toks, feat, embs)
    by_batch = hidden_all.reshape(batches, cols // batches, toks, hid_local)
    own_hidden = swap(by_batch, "batch")
    own_hidden = own_hidden.transpose(0, 2, 1, 3).reshape(batches * toks, hid // batches)
    grad_out = contract_first(own_hidden, every_cot.reshape(batches * toks, feat * embs))
    grad_out = grad_out.reshape(hid // batches, feat, embs)
    in_part = contract_first(act, d_pre_b).astype(bf16)
    quarter = summed(swap(in_part.reshape(batches, -1, hid_local), "batch")).astype(bf16)
    grad_in = everyone(quarter, "batch").astype(f32).reshape(embs * rank, hid_local)
    grad_bias = jnp.sum(everyone(jnp.sum(d_preact, axis=0), "batch"), axis=0)
    return (mixed, grad_out, grad_in, grad_bias, grad_proj)


def solution(mesh):
    placed = (
        P("batch", "col", "row"),
        P(),
        P("row", "col"),
        P("col"),
        P(None, "col", "row"),
        P("batch", "col", "row"),
    )
    return jax.shard_map(
        local,
        mesh=mesh,
        in_specs=placed,
        out_specs=(
            P("batch", "col", "row"),
            P("batch", "col", "row"),
            P("row", "col"),
            P("col"),
            P("row", None),
        ),
        check_vma=False,
    )
```

time: 537 us -> 305 us (0.57)
  waiting for transfers between devices: 345 us -> 103 us
  starting transfers between devices: 42.5 us -> 96.8 us
  blocking collectives: 65 us -> 41.8 us
  between operations: 14 us -> 0.84 us
  matrix products: 22.6 us -> 15.3 us
    psum x2 -> x0, waiting for transfers between devices: 201 us -> none  [the longest x1 172 us: local(): interact = lax.psum(partial_value, 'col')]
    reduce_scatter x1 -> x0, waiting for transfers between devices: 95.4 us -> none  [sum_by_parts(): own = lax.psum_scatter(padded, axis, scatter_dimension=0, tiled=True)]
    all_to_all x7 -> x15, waiting for transfers between devices: 13.6 us -> 103 us  [swap(): return lax.all_to_all(tiles, axis, 0, 0, tiled=True)]
    all_to_all x7 -> x15, starting transfers between devices: 42.4 us -> 96.8 us  [swap(): return lax.all_to_all(tiles, axis, 0, 0, tiled=True)]
    all_gather x2 -> x0, waiting for transfers between devices: 34.7 us -> none  [the longest x1 34.7 us: sum_by_parts(): whole = lax.all_gather(own, axis, axis=0, tiled=True)]
    psum x1 -> x0, blocking collectives: 33.7 us -> none  [local(): lax.psum((contract_first(activated, d_pre_b), jnp.sum(d_preact, axis=0)),...]
    all_to_all x2, blocking collectives: 31.3 us -> 41.8 us  [swap(): return lax.all_to_all(tiles, axis, 0, 0, tiled=True)]
    dot_general x2 -> x1, local copies, waits for them, and re-layouts: 8.72 us -> 1.49 us  [contract_first(): lax.dot_general(left, right, (((0,), (0,)), ((), ())), preferred_element_...]
  transfers between devices with their start and end apart: 12 -> 15, of which waited for: 7 -> 12; matrix products, arithmetic and copies ran while one was open for 10% -> 16% of each run, Pallas kernels for 0% -> 0%
where the time goes in v1:
time: 305 us; the launch traced here: 303 us
  waiting for transfers between devices  103 us (34%)
  starting transfers between devices  96.8 us (32%)
  blocking collectives  41.8 us (14%)
  local copies, waits for them, and re-layouts  33.3 us (11%)
  matrix products  15.3 us (5%)
  other arithmetic  12 us (4%)
    all_to_all x15, waiting for transfers between devices, swap(): return lax.all_to_all(tiles, axis, 0, 0, tiled=True)  103 us
    all_to_all x15, starting transfers between devices, swap(): return lax.all_to_all(tiles, axis, 0, 0, tiled=True)  96.8 us
    all_to_all x2, blocking collectives, swap(): return lax.all_to_all(tiles, axis, 0, 0, tiled=True)  41.8 us
    broadcast_in_dim x9, local copies, waits for them, and re-layouts, everyone(): return swap(jnp.broadcast_to(array[None], (size, *array.shape)), axis)  6.92 us
  transfers between devices with their start and end apart: 15, of which 12 were waited for; matrix products, arithmetic and copies ran while one was open for 16% of the time, Pallas kernels for 0%

profile of v1, /device:TPU:1, one launch (start us, length us, event | category | flops | bytes accessed | tf_op | source)
XLA Modules:
  0.0 302.6 jit_solution(10908157120233566869)
XLA Ops:
  0.6 15.2 %all-to-all-start = ((bf16[64,2,8,128]{3,2,1,0:T(8,128)(2,1)}), bf16[64,2,8,128]{3,2,1,0:T(8,128)(2,1)S(1)}, u32[]{:S(2)}, u32[]{:S(2)}) async-start(bf16[64,2,8,128]{3,2,1,0:T(8,128)(2,1)} %bitcast.109), calls=%async_computation | async-start | bytes 524288 | tf_op jit(solution)/shard_map/all_to_all | solution.py:12
  17.1 11.9 %all-to-all-done = bf16[64,2,8,128]{3,2,1,0:T(8,128)(2,1)S(1)} async-done(((bf16[64,2,8,128]{3,2,1,0:T(8,128)(2,1)}), bf16[64,2,8,128]{3,2,1,0:T(8,128)(2,1)S(1)}, u32[]{:S(2)}, u32[]{:S(2)}) %all-to-all-start) | async-done | bytes 262176 | tf_op jit(solution)/shard_map/all_to_all | solution.py:12
  31.5 3.3 %all-to-all-start.1 = ((bf16[4,2,4096]{2,1,0:T(2,128)(2,1)}), bf16[4,2,4096]{2,1,0:T(2,128)(2,1)S(1)}, u32[]{:S(2)}, u32[]{:S(2)}) async-start(bf16[4,2,4096]{2,1,0:T(2,128)(2,1)} %copy.102), calls=%async_computation.1 | async-start | bytes 131072 | tf_op jit(solution)/shard_map/all_to_all | solution.py:12
  34.8 3.7 %fusion.12 = bf16[16,16,8,128]{3,2,1,0:T(8,128)(2,1)S(1)} fusion(bf16[128,8,128]{0,2,1:T(8,128)(2,1)S(1)} %copy.122, bf16[2048,8,128]{2,1,0:T(8,128)(2,1)} %param.10), kind=kOutput, calls=%fused_computation.10 | convolution fusion | flops 537133056 | bytes 4980736 | tf_op jit(solution)/shard_map/dot_general | solution.py:21
  39.4 3.7 %all-to-all-start.7 = ((bf16[16,128,128]{2,1,0:T(8,128)(2,1)}), bf16[16,128,128]{2,1,0:T(8,128)(2,1)S(1)}, u32[]{:S(2)}, u32[]{:S(2)}) async-start(bf16[16,128,128]{2,1,0:T(8,128)(2,1)} %bitcast.97), calls=%async_computation.7 | async-start | bytes 1048576 | tf_op jit(solution)/shard_map/all_to_all | solution.py:12
  43.2 12.7 %all-to-all-done.7 = bf16[16,128,128]{2,1,0:T(8,128)(2,1)S(1)} async-done(((bf16[16,128,128]{2,1,0:T(8,128)(2,1)}), bf16[16,128,128]{2,1,0:T(8,128)(2,1)S(1)}, u32[]{:S(2)}, u32[]{:S(2)}) %all-to-all-start.7) | async-done | bytes 524320 | tf_op jit(solution)/shard_map/all_to_all | solution.py:12
  56.9 4.2 %all-to-all-start.2 = ((bf16[16,8,4096]{2,1,0:T(8,128)(2,1)}), bf16[16,8,4096]{2,1,0:T(8,128)(2,1)S(1)}, u32[]{:S(2)}, u32[]{:S(2)}) async-start(bf16[16,8,4096]{2,1,0:T(8,128)(2,1)} %broadcast_in_dim.21), calls=%async_computation.2 | async-start | bytes 2097152 | tf_op jit(solution)/shard_map/all_to_all | solution.py:12
  61.2 17.5 %all-to-all-done.2 = bf16[16,8,4096]{2,1,0:T(8,128)(2,1)S(1)} async-done(((bf16[16,8,4096]{2,1,0:T(8,128)(2,1)}), bf16[16,8,4096]{2,1,0:T(8,128)(2,1)S(1)}, u32[]{:S(2)}, u32[]{:S(2)}) %all-to-all-start.2) | async-done | bytes 1048608 | tf_op jit(solution)/shard_map/all_to_all | solution.py:12
  79.4 6.7 %all-to-all-start.8 = ((f32[4,128,128]{2,1,0:T(8,128)}), f32[4,128,128]{2,1,0:T(8,128)S(1)}, u32[]{:S(2)}, u32[]{:S(2)}) async-start(f32[4,128,128]{2,1,0:T(8,128)} %broadcast_in_dim.26), calls=%async_computation.8 | async-start | bytes 524288 | tf_op jit(solution)/shard_map/all_to_all | solution.py:12
  86.5 5.1 %all-to-all-done.8 = f32[4,128,128]{2,1,0:T(8,128)S(1)} async-done(((f32[4,128,128]{2,1,0:T(8,128)}), f32[4,128,128]{2,1,0:T(8,128)S(1)}, u32[]{:S(2)}, u32[]{:S(2)}) %all-to-all-start.8) | async-done | bytes 262176 | tf_op jit(solution)/shard_map/all_to_all | solution.py:12
  91.6 8.6 %all_to_all.91 = f32[4,128,128]{2,1,0:T(8,128)} all-to-all(f32[4,128,128]{2,1,0:T(8,128)S(1)} %broadcast_in_dim.22), channel_id=1, replica_groups=mesh['batch'=4,'row'=4,'col'=16] {'row'}, dimensions={0} | all-to-all | bytes 524288 | tf_op jit(solution)/shard_map/all_to_all | solution.py:12
  101.3 17.8 %all-to-all-start.6 = ((bf16[4,128,1024]{1,2,0:T(8,128)(2,1)}), bf16[4,128,1024]{1,2,0:T(8,128)(2,1)S(1)}, u32[]{:S(2)}, u32[]{:S(2)}) async-start(bf16[4,128,1024]{1,2,0:T(8,128)(2,1)} %broadcast_in_dim.25), calls=%async_computation.6 | async-start | bytes 2097152 | tf_op jit(solution)/shard_map/all_to_all | solution.py:12
  125.9 6.5 %all-to-all-done.6 = bf16[4,128,1024]{1,2,0:T(8,128)(2,1)S(1)} async-done(((bf16[4,128,1024]{1,2,0:T(8,128)(2,1)}), bf16[4,128,1024]{1,2,0:T(8,128)(2,1)S(1)}, u32[]{:S(2)}, u32[]{:S(2)}) %all-to-all-start.6) | async-done | bytes 1048608 | tf_op jit(solution)/shard_map/all_to_all | solution.py:12
  132.4 33.2 %all_to_all.92 = bf16[16,8,4096]{2,1,0:T(8,128)(2,1)} all-to-all(bf16[16,8,4096]{2,1,0:T(8,128)(2,1)} %fusion), channel_id=1, replica_groups=mesh['batch'=4,'row'=4,'col'=16] {'col'}, dimensions={0} | all-to-all | bytes 2097152 | tf_op jit(solution)/shard_map/all_to_all | solution.py:12
  166.2 5.6 %all-to-all-start.11 = ((f32[4,1,128]{2,1,0:T(1,128)}), f32[4,1,128]{2,1,0:T(1,128)S(1)}, u32[]{:S(2)}, u32[]{:S(2)}) async-start(f32[4,1,128]{2,1,0:T(1,128)} %broadcast_in_dim.28), calls=%async_computation.11 | async-start | bytes 4096 | tf_op jit(solution)/shard_map/all_to_all | solution.py:12
  175.4 3.9 %all-to-all-start.13 = ((bf16[4,2,4096]{2,1,0:T(2,128)(2,1)}), bf16[4,2,4096]{2,1,0:T(2,128)(2,1)}, u32[]{:S(2)}, u32[]{:S(2)}) async-start(bf16[4,2,4096]{2,1,0:T(2,128)(2,1)} %reshape.146), calls=%async_computation.13 | async-start | bytes 131072 | tf_op jit(solution)/shard_map/all_to_all | solution.py:12
  180.8 3.1 %all-to-all-done.13 = bf16[4,2,4096]{2,1,0:T(2,128)(2,1)} async-done(((bf16[4,2,4096]{2,1,0:T(2,128)(2,1)}), bf16[4,2,4096]{2,1,0:T(2,128)(2,1)}, u32[]{:S(2)}, u32[]{:S(2)}) %all-to-all-start.13) | async-done | bytes 65568 | tf_op jit(solution)/shard_map/all_to_all | solution.py:12
  185.5 4.3 %all-to-all-start.4 = ((bf16[16,128,128]{1,2,0:T(8,128)(2,1)}), bf16[16,128,128]{1,2,0:T(8,128)(2,1)}, u32[]{:S(2)}, u32[]{:S(2)}) async-start(bf16[16,128,128]{1,2,0:T(8,128)(2,1)} %broadcast_in_dim.23), calls=%async_computation.4 | async-start | bytes 1048576 | tf_op jit(solution)/shard_map/all_to_all | solution.py:12
  198.3 6.9 %all-to-all-done.4 = bf16[16,128,128]{1,2,0:T(8,128)(2,1)} async-done(((bf16[16,128,128]{1,2,0:T(8,128)(2,1)}), bf16[16,128,128]{1,2,0:T(8,128)(2,1)}, u32[]{:S(2)}, u32[]{:S(2)}) %all-to-all-start.4) | async-done | bytes 524320 | tf_op jit(solution)/shard_map/all_to_all | solution.py:12
  205.2 3.3 %all-to-all-start.14 = ((f32[4,128,32]{1,2,0:T(8,128)}), f32[4,128,32]{1,2,0:T(8,128)S(1)}, u32[]{:S(2)}, u32[]{:S(2)}) async-start(f32[4,128,32]{1,2,0:T(8,128)} %bitcast.98), calls=%async_computation.14 | async-start | bytes 131072 | tf_op jit(solution)/shard_map/all_to_all | solution.py:12
  210.7 2.2 all-to-all-done.14
  212.9 9.8 %all-to-all-start.9 = ((bf16[4,1024,128]{2,1,0:T(8,128)(2,1)}), bf16[4,1024,128]{2,1,0:T(8,128)(2,1)S(1)}, u32[]{:S(2)}, u32[]{:S(2)}) async-start(bf16[4,1024,128]{2,1,0:T(8,128)(2,1)} %bitcast.104), calls=%async_computation.9 | async-start | bytes 2097152 | tf_op jit(solution)/shard_map/all_to_all | solution.py:12
  223.5 12.7 %all-to-all-done.9 = bf16[4,1024,128]{2,1,0:T(8,128)(2,1)S(1)} async-done(((bf16[4,1024,128]{2,1,0:T(8,128)(2,1)}), bf16[4,1024,128]{2,1,0:T(8,128)(2,1)S(1)}, u32[]{:S(2)}, u32[]{:S(2)}) %all-to-all-start.9) | async-done | bytes 1048608 | tf_op jit(solution)/shard_map/all_to_all | solution.py:12
  236.2 5.1 %all-to-all-start.15 = ((f32[64,1,64]{2,1,0:T(1,128)}), f32[64,1,64]{2,1,0:T(1,128)S(1)}, u32[]{:S(2)}, u32[]{:S(2)}) async-start(f32[64,1,64]{2,1,0:T(1,128)} %bitcast.28), calls=%async_computation.15 | async-start | bytes 65536 | tf_op jit(solution)/shard_map/all_to_all | solution.py:12
  243.4 7.2 %all-to-all-done.15 = f32[64,1,64]{2,1,0:T(1,128)S(1)} async-done(((f32[64,1,64]{2,1,0:T(1,128)}), f32[64,1,64]{2,1,0:T(1,128)S(1)}, u32[]{:S(2)}, u32[]{:S(2)}) %all-to-all-start.15) | async-done | bytes 16416 | tf_op jit(solution)/shard_map/all_to_all | solution.py:12
  250.6 4.7 %all-to-all-start.5 = ((bf16[4,4,128,128]{3,2,1,0:T(8,128)(2,1)}), bf16[4,4,128,128]{3,2,1,0:T(8,128)(2,1)}, u32[]{:S(2)}, u32[]{:S(2)}) async-start(bf16[4,4,128,128]{3,2,1,0:T(8,128)(2,1)} %bitcast.106), calls=%async_computation.5 | async-start | bytes 1048576 | tf_op jit(solution)/shard_map/all_to_all | solution.py:12
  255.3 7.9 %all-to-all-done.5 = bf16[4,4,128,128]{3,2,1,0:T(8,128)(2,1)} async-done(((bf16[4,4,128,128]{3,2,1,0:T(8,128)(2,1)}), bf16[4,4,128,128]{3,2,1,0:T(8,128)(2,1)}, u32[]{:S(2)}, u32[]{:S(2)}) %all-to-all-start.5) | async-done | bytes 524320 | tf_op jit(solution)/shard_map/all_to_all | solution.py:12
  263.8 5.1 %all-to-all-start.16 = ((f32[64,1,64]{2,1,0:T(1,128)}), f32[64,1,64]{2,1,0:T(1,128)S(1)}, u32[]{:S(2)}, u32[]{:S(2)}) async-start(f32[64,1,64]{2,1,0:T(1,128)} %broadcast_in_dim.29), calls=%async_computation.16 | async-start | bytes 65536 | tf_op jit(solution)/shard_map/all_to_all | solution.py:12
  269.2 9.0 %all-to-all-done.16 = f32[64,1,64]{2,1,0:T(1,128)S(1)} async-done(((f32[64,1,64]{2,1,0:T(1,128)}), f32[64,1,64]{2,1,0:T(1,128)S(1)}, u32[]{:S(2)}, u32[]{:S(2)}) %all-to-all-start.16) | async-done | bytes 16416 | tf_op jit(solution)/shard_map/all_to_all | solution.py:12
  279.3 4.1 %all-to-all-start.10 = ((bf16[4,1024,128]{2,1,0:T(8,128)(2,1)}), bf16[4,1024,128]{2,1,0:T(8,128)(2,1)S(1)}, u32[]{:S(2)}, u32[]{:S(2)}) async-start(bf16[4,1024,128]{2,1,0:T(8,128)(2,1)} %broadcast_in_dim.27), calls=%async_computation.10 | async-start | bytes 2097152 | tf_op jit(solution)/shard_map/all_to_all | solution.py:12
  286.7 3.1 %fusion.18 = bf16[16,8,8,128]{3,1,2,0:T(8,128)(2,1)S(1)} fusion(bf16[128,2048]{0,1:T(8,128)(2,1)} %bitcast.9, bf16[256,8,8,128]{3,2,1,0:T(8,128)(2,1)} %bitcast.112), kind=kOutput, calls=%fused_computation.12 | convolution fusion | flops 537001984 | bytes 4980736 | tf_op jit(solution)/shard_map/dot_general | solution.py:79
  296.5 2.5 copy.120
  (71 shorter events, 51.2 us)
Async XLA Ops:
  0.6 85.4 %copy-start = (bf16[4096,128]{1,0:T(8,128)(2,1)S(1)}, bf16[4096,128]{1,0:T(8,128)(2,1)}, u32[]{:S(2)}) copy-start(bf16[4096,128]{1,0:T(8,128)(2,1)} %param.8) | copy-start | bytes 3145732
  0.6 28.3 %all-to-all-start = ((bf16[64,2,8,128]{3,2,1,0:T(8,128)(2,1)}), bf16[64,2,8,128]{3,2,1,0:T(8,128)(2,1)S(1)}, u32[]{:S(2)}, u32[]{:S(2)}) async-start(bf16[64,2,8,128]{3,2,1,0:T(8,128)(2,1)} %bitcast.109), calls=%async_computation | async-start | bytes 524288 | tf_op jit(solution)/shard_map/all_to_all | solution.py:12
  31.5 7.9 %all-to-all-start.1 = ((bf16[4,2,4096]{2,1,0:T(2,128)(2,1)}), bf16[4,2,4096]{2,1,0:T(2,128)(2,1)S(1)}, u32[]{:S(2)}, u32[]{:S(2)}) async-start(bf16[4,2,4096]{2,1,0:T(2,128)(2,1)} %copy.102), calls=%async_computation.1 | async-start | bytes 131072 | tf_op jit(solution)/shard_map/all_to_all | solution.py:12
  39.4 16.4 %all-to-all-start.7 = ((bf16[16,128,128]{2,1,0:T(8,128)(2,1)}), bf16[16,128,128]{2,1,0:T(8,128)(2,1)S(1)}, u32[]{:S(2)}, u32[]{:S(2)}) async-start(bf16[16,128,128]{2,1,0:T(8,128)(2,1)} %bitcast.97), calls=%async_computation.7 | async-start | bytes 1048576 | tf_op jit(solution)/shard_map/all_to_all | solution.py:12
  56.9 21.7 %all-to-all-start.2 = ((bf16[16,8,4096]{2,1,0:T(8,128)(2,1)}), bf16[16,8,4096]{2,1,0:T(8,128)(2,1)S(1)}, u32[]{:S(2)}, u32[]{:S(2)}) async-start(bf16[16,8,4096]{2,1,0:T(8,128)(2,1)} %broadcast_in_dim.21), calls=%async_computation.2 | async-start | bytes 2097152 | tf_op jit(solution)/shard_map/all_to_all | solution.py:12
  61.1 61.3 %copy-start.5 = (f32[128]{0:T(128)S(1)}, f32[128]{0:T(128)}, u32[]{:S(2)}) copy-start(f32[128]{0:T(128)} %param.9) | copy-start | bytes 1540
  79.4 12.2 %all-to-all-start.8 = ((f32[4,128,128]{2,1,0:T(8,128)}), f32[4,128,128]{2,1,0:T(8,128)S(1)}, u32[]{:S(2)}, u32[]{:S(2)}) async-start(f32[4,128,128]{2,1,0:T(8,128)} %broadcast_in_dim.26), calls=%async_computation.8 | async-start | bytes 524288 | tf_op jit(solution)/shard_map/all_to_all | solution.py:12
  91.6 9.7 %copy-start.3 = (f32[4,128,128]{2,1,0:T(8,128)}, f32[4,128,128]{2,1,0:T(8,128)S(1)}, u32[]{:S(2)}) copy-start(f32[4,128,128]{2,1,0:T(8,128)S(1)} %all-to-all-done.8) | copy-start | bytes 786436
  101.3 31.1 %all-to-all-start.6 = ((bf16[4,128,1024]{1,2,0:T(8,128)(2,1)}), bf16[4,128,1024]{1,2,0:T(8,128)(2,1)S(1)}, u32[]{:S(2)}, u32[]{:S(2)}) async-start(bf16[4,128,1024]{1,2,0:T(8,128)(2,1)} %broadcast_in_dim.25), calls=%async_computation.6 | async-start | bytes 2097152 | tf_op jit(solution)/shard_map/all_to_all | solution.py:12
  123.9 0.6 copy-start.4
  132.4 78.3 %copy-start.1 = (bf16[4,128,1024]{1,2,0:T(8,128)(2,1)}, bf16[4,128,1024]{1,2,0:T(8,128)(2,1)S(1)}, u32[]{:S(2)}) copy-start(bf16[4,128,1024]{1,2,0:T(8,128)(2,1)S(1)} %all-to-all-done.6) | copy-start | bytes 3145732
  166.2 9.2 %all-to-all-start.11 = ((f32[4,1,128]{2,1,0:T(1,128)}), f32[4,1,128]{2,1,0:T(1,128)S(1)}, u32[]{:S(2)}, u32[]{:S(2)}) async-start(f32[4,1,128]{2,1,0:T(1,128)} %broadcast_in_dim.28), calls=%async_computation.11 | async-start | bytes 4096 | tf_op jit(solution)/shard_map/all_to_all | solution.py:12
  175.4 8.4 %all-to-all-start.13 = ((bf16[4,2,4096]{2,1,0:T(2,128)(2,1)}), bf16[4,2,4096]{2,1,0:T(2,128)(2,1)}, u32[]{:S(2)}, u32[]{:S(2)}) async-start(bf16[4,2,4096]{2,1,0:T(2,128)(2,1)} %reshape.146), calls=%async_computation.13 | async-start | bytes 131072 | tf_op jit(solution)/shard_map/all_to_all | solution.py:12
  185.5 19.7 %all-to-all-start.4 = ((bf16[16,128,128]{1,2,0:T(8,128)(2,1)}), bf16[16,128,128]{1,2,0:T(8,128)(2,1)}, u32[]{:S(2)}, u32[]{:S(2)}) async-start(bf16[16,128,128]{1,2,0:T(8,128)(2,1)} %broadcast_in_dim.23), calls=%async_computation.4 | async-start | bytes 1048576 | tf_op jit(solution)/shard_map/all_to_all | solution.py:12
  205.2 7.7 %all-to-all-start.14 = ((f32[4,128,32]{1,2,0:T(8,128)}), f32[4,128,32]{1,2,0:T(8,128)S(1)}, u32[]{:S(2)}, u32[]{:S(2)}) async-start(f32[4,128,32]{1,2,0:T(8,128)} %bitcast.98), calls=%async_computation.14 | async-start | bytes 131072 | tf_op jit(solution)/shard_map/all_to_all | solution.py:12
  212.9 70.5 %copy-start.2 = (bf16[4,128,1024]{1,2,0:T(8,128)(2,1)S(1)}, bf16[4,128,1024]{1,2,0:T(8,128)(2,1)}, u32[]{:S(2)}) copy-start(bf16[4,128,1024]{1,2,0:T(8,128)(2,1)} %copy-done.1) | copy-start | bytes 3145732
  212.9 23.3 %all-to-all-start.9 = ((bf16[4,1024,128]{2,1,0:T(8,128)(2,1)}), bf16[4,1024,128]{2,1,0:T(8,128)(2,1)S(1)}, u32[]{:S(2)}, u32[]{:S(2)}) async-start(bf16[4,1024,128]{2,1,0:T(8,128)(2,1)} %bitcast.104), calls=%async_computation.9 | async-start | bytes 2097152 | tf_op jit(solution)/shard_map/all_to_all | solution.py:12
  236.2 14.4 %all-to-all-start.15 = ((f32[64,1,64]{2,1,0:T(1,128)}), f32[64,1,64]{2,1,0:T(1,128)S(1)}, u32[]{:S(2)}, u32[]{:S(2)}) async-start(f32[64,1,64]{2,1,0:T(1,128)} %bitcast.28), calls=%async_computation.15 | async-start | bytes 65536 | tf_op jit(solution)/shard_map/all_to_all | solution.py:12
  250.6 12.7 %all-to-all-start.5 = ((bf16[4,4,128,128]{3,2,1,0:T(8,128)(2,1)}), bf16[4,4,128,128]{3,2,1,0:T(8,128)(2,1)}, u32[]{:S(2)}, u32[]{:S(2)}) async-start(bf16[4,4,128,128]{3,2,1,0:T(8,128)(2,1)} %bitcast.106), calls=%async_computation.5 | async-start | bytes 1048576 | tf_op jit(solution)/shard_map/all_to_all | solution.py:12
  263.8 14.4 %all-to-all-start.16 = ((f32[64,1,64]{2,1,0:T(1,128)}), f32[64,1,64]{2,1,0:T(1,128)S(1)}, u32[]{:S(2)}, u32[]{:S(2)}) async-start(f32[64,1,64]{2,1,0:T(1,128)} %broadcast_in_dim.29), calls=%async_computation.16 | async-start | bytes 65536 | tf_op jit(solution)/shard_map/all_to_all | solution.py:12
  279.3 21.7 %all-to-all-start.10 = ((bf16[4,1024,128]{2,1,0:T(8,128)(2,1)}), bf16[4,1024,128]{2,1,0:T(8,128)(2,1)S(1)}, u32[]{:S(2)}, u32[]{:S(2)}) async-start(bf16[4,1024,128]{2,1,0:T(8,128)(2,1)} %broadcast_in_dim.27), calls=%async_computation.10 | async-start | bytes 2097152 | tf_op jit(solution)/shard_map/all_to_all | solution.py:12

commit v2 on v1

--- a/solution.py
+++ b/solution.py
@@ -1,11 +1,18 @@
+import functools
+
 import jax
 import jax.numpy as jnp
 from jax import lax
+from jax.experimental import pallas as pl
+from jax.experimental.pallas import tpu as pltpu
 from jax.sharding import PartitionSpec as P
 
 epsilon = 1e-06
 bf16 = jnp.bfloat16
 f32 = jnp.float32
+MESH = pl.DeviceIdType.MESH
+VMEM = pltpu.VMEM
+DMA = pltpu.SemaphoreType.DMA
 
 
 def swap(tiles, axis):
@@ -25,8 +32,233 @@
     return lax.dot_general(left, right, (((0,), (0,)), ((), ())), preferred_element_type=f32)
 
 
+def dot(left, right):
+    return jnp.dot(left, right, preferred_element_type=f32)
+
+
 def summed(tiles):
     return jnp.sum(tiles.astype(f32), axis=0)
+
+
+def send(src, dst, send_sem, recv_sem, **place):
+    copy = pltpu.make_async_remote_copy(
+        src_ref=src, dst_ref=dst, send_sem=send_sem, recv_sem=recv_sem,
+        device_id=place, device_id_type=MESH,
+    )
+    copy.start()
+
+
+def arrived(ref, sem):
+    pltpu.make_async_copy(ref, ref, sem).wait()
+
+
+def split(value):
+    high = value.astype(bf16)
+    return high, (value - high.astype(f32)).astype(bf16)
+
+
+def places():
+    me = {axis: lax.axis_index(axis) for axis in ("batch", "row", "col")}
+    i, r, c = me["batch"], me["row"], me["col"]
+    y = c // 4
+    z = c - y * 4
+    sibling = i + 1 - 2 * lax.rem(i, 2)
+    across = lax.rem(i + 2, 4)
+    return i, r, c, y, z, sibling, across
+
+
+def forward_kernel(
+    emb, proj, w_in, bias, d_part, cot,
+    gathered, hidden, d_pre, d_pre_b, normed, inv, own_emb, every_cot,
+    folds, to_row, from_row, d_y, d_z_out, d_z, d_x, pre_x,
+    emb_send, emb_recv, row_send, row_recv, gather_send, gather_recv,
+    dy_send, dy_recv, dz_send, dz_recv, dx_send, dx_recv, pre_send, pre_recv,
+    cot_send, cot_recv, own_sem,
+):
+    i, r, c, y, z, sibling, across = places()
+    me = c * 4 + r
+    barrier = pltpu.get_barrier_semaphore()
+
+    def greet(k, _):
+        peer = lax.rem(me + k, 64)
+        pl.semaphore_signal(
+            barrier, inc=1, device_id={"col": peer // 4, "row": lax.rem(peer, 4)},
+            device_id_type=MESH,
+        )
+        return 0
+
+    lax.fori_loop(1, 64, greet, 0)
+    for other in (sibling, across):
+        pl.semaphore_signal(barrier, inc=1, device_id={"batch": other}, device_id_type=MESH)
+    pl.semaphore_wait(barrier, 65)
+
+    def give(k, _):
+        peer = lax.rem(me + k, 64)
+        send(
+            emb.at[peer], own_emb.at[r, :, c], emb_send, emb_recv,
+            col=peer // 4, row=lax.rem(peer, 4),
+        )
+        return 0
+
+    keep = pltpu.make_async_copy(emb.at[me], own_emb.at[r, :, c], emb_recv)
+    keep.start()
+    lax.fori_loop(1, 64, give, 0)
+    for k in (1, 2, 3):
+        to = lax.rem(y + k, 4)
+        send(
+            d_part.at[:, pl.ds(pl.multiple_of(to * 512, 512), 512)], d_y.at[y],
+            dy_send, dy_recv.at[y], col=to * 4 + z,
+        )
+    lanes = lax.broadcasted_iota(jnp.int32, (32, 128), 1)
+    ranks = lax.broadcasted_iota(jnp.int32, (32, 128), 0)
+    spread = (lax.rem(lanes, 32) == ranks).astype(f32).astype(bf16)
+    wide = dot(proj[...], spread).astype(bf16)
+    block = lax.broadcasted_iota(jnp.int32, (128, 128), 1) // 32
+    at = lax.broadcasted_iota(jnp.int32, (256, 256), 0)
+    of = lax.broadcasted_iota(jnp.int32, (256, 256), 1)
+    source = lax.rem(at, 8) // 2 * 64 + lax.rem(at, 2) * 32 + at // 8
+    order = (of == source).astype(f32).astype(bf16)
+    arrived(own_emb, emb_recv)
+    for s in range(2):
+        tiles = [own_emb[q, s].reshape(128, 128) for q in range(4)]
+        folded = sum(dot(tiles[q], wide[q * 128 : (q + 1) * 128]) for q in range(4))
+        high, low = split(folded)
+        for q in range(4):
+            folds[q * 128 : (q + 1) * 128, :] = contract_first(tiles[q], high) + contract_first(
+                tiles[q], low
+            )
+        inter = jnp.zeros((128, 128), f32)
+        for j in range(4):
+            inter = jnp.where(block == j, folds[pl.ds(j, 128, stride=4), :], inter)
+        total = jnp.sum(jnp.sum(inter * inter, axis=0, keepdims=True), axis=1, keepdims=True)
+        scale = lax.rsqrt(total / (512 * 32) + epsilon)
+        norm = inter * scale
+        normed[s] = norm
+        inv[s] = jnp.broadcast_to(scale, (8, 128))
+        for q in range(4):
+            to_row[q, s] = norm[q * 32 : (q + 1) * 32].astype(bf16)
+    from_row[r] = to_row[r]
+    for k in (1, 2, 3):
+        to = lax.rem(r + k, 4)
+        send(to_row.at[to], from_row.at[r], row_send, row_recv.at[r], row=to)
+    for k in (1, 2, 3):
+        f = lax.rem(y + k, 4)
+        arrived(d_y.at[f], dy_recv.at[f])
+    d_y[y] = d_part[:, pl.ds(pl.multiple_of(y * 512, 512), 512)]
+    for q in range(4):
+        part = d_y[0, :, q * 128 : (q + 1) * 128].astype(f32)
+        for f in (1, 2, 3):
+            part = part + d_y[f, :, q * 128 : (q + 1) * 128].astype(f32)
+        d_z_out[q] = part.astype(bf16)
+    d_z[z] = d_z_out[z]
+    for k in (1, 2, 3):
+        to = lax.rem(z + k, 4)
+        send(d_z_out.at[to], d_z.at[z], dz_send, dz_recv.at[z], col=y * 4 + to)
+    for k in (1, 2, 3):
+        f = lax.rem(r + k, 4)
+        arrived(from_row.at[f], row_recv.at[f])
+    rows = dot(order, from_row[...].reshape(256, 128))
+    gathered[:, c] = rows.reshape(32, 8, 128).astype(bf16)
+    for k in (1, 2, 3):
+        to = lax.rem(z + k, 4)
+        send(gathered.at[:, c], gathered.at[:, c], gather_send, gather_recv.at[c], col=y * 4 + to)
+    for k in (1, 2, 3):
+        to = lax.rem(y + k, 4)
+        send(gathered.at[:, c], gathered.at[:, c], gather_send, gather_recv.at[c], col=to * 4 + z)
+    for m in (1, 2, 3):
+        slot = y * 4 + lax.rem(z + m, 4)
+        arrived(gathered.at[:, slot], gather_recv.at[slot])
+        for k in (1, 2, 3):
+            to = lax.rem(y + k, 4)
+            send(
+                gathered.at[:, slot], gathered.at[:, slot], gather_send, gather_recv.at[slot],
+                col=to * 4 + z,
+            )
+    mine = pltpu.make_async_copy(cot, every_cot.at[i], own_sem)
+    mine.start()
+    send(cot, every_cot.at[i], cot_send, cot_recv.at[i], batch=sibling)
+    send(cot, every_cot.at[i], cot_send, cot_recv.at[i], batch=across)
+    for k in (1, 2, 3):
+        f = lax.rem(z + k, 4)
+        arrived(d_z.at[f], dz_recv.at[f])
+    d_x[r] = sum(d_z[f].astype(f32) for f in range(4))
+    for k in (1, 2, 3):
+        to = lax.rem(r + k, 4)
+        send(d_x.at[r], d_x.at[r], dx_send, dx_recv.at[r], row=to)
+    for m in (1, 2, 3):
+        for k in range(4):
+            slot = lax.rem(y + m, 4) * 4 + k
+            arrived(gathered.at[:, slot], gather_recv.at[slot])
+    pre = jnp.zeros((128, 128), f32)
+    for e in range(32):
+        pre = pre + dot(gathered[e].reshape(128, 128), w_in[e])
+    pre_x[r] = pre
+    for k in (1, 2, 3):
+        to = lax.rem(r + k, 4)
+        send(pre_x.at[r], pre_x.at[r], pre_send, pre_recv.at[r], row=to)
+    arrived(every_cot.at[across], cot_recv.at[across])
+    send(every_cot.at[across], every_cot.at[across], cot_send, cot_recv.at[across], batch=sibling)
+    for k in (1, 2, 3):
+        f = lax.rem(r + k, 4)
+        arrived(d_x.at[f], dx_recv.at[f])
+    d_hidden = (d_x[0] + d_x[1]) + (d_x[2] + d_x[3])
+    for k in (1, 2, 3):
+        f = lax.rem(r + k, 4)
+        arrived(pre_x.at[f], pre_recv.at[f])
+    preact = (pre_x[0] + pre_x[1]) + (pre_x[2] + pre_x[3]) + bias[...]
+    sig = 1.0 / (1.0 + jnp.exp(-preact))
+    hidden[...] = (preact * sig).astype(bf16)
+    d_value = d_hidden * sig * (1.0 + preact * (1.0 - sig))
+    d_pre[...] = d_value
+    d_pre_b[...] = d_value.astype(bf16)
+    diagonal = lax.rem(sibling + 2, 4)
+    arrived(every_cot.at[sibling], cot_recv.at[sibling])
+    arrived(every_cot.at[diagonal], cot_recv.at[diagonal])
+    mine.wait()
+    arrived(emb.at[pl.ds(0, 63)], emb_send)
+    arrived(d_y.at[pl.ds(0, 3)], dy_send)
+    arrived(d_z.at[pl.ds(0, 3)], dz_send)
+    arrived(d_x.at[pl.ds(0, 3)], dx_send)
+    arrived(pre_x.at[pl.ds(0, 3)], pre_send)
+    arrived(from_row.at[pl.ds(0, 3)], row_send)
+    arrived(every_cot.at[pl.ds(0, 3)], cot_send)
+    arrived(gathered.at[:, pl.ds(0, 15)], gather_send)
+
+
+def forward(emb, proj, w_in, bias, d_part, cot):
+    out = jax.ShapeDtypeStruct
+    return pl.pallas_call(
+        forward_kernel,
+        out_shape=(
+            out((32, 16, 8, 128), bf16),
+            out((128, 128), bf16),
+            out((128, 128), f32),
+            out((128, 128), bf16),
+            out((2, 128, 128), f32),
+            out((2, 8, 128), f32),
+            out((4, 2, 16, 8, 128), bf16),
+            out((4, 128, 1024), bf16),
+        ),
+        in_specs=[pl.BlockSpec(memory_space=VMEM)] * 6,
+        out_specs=[pl.BlockSpec(memory_space=VMEM)] * 8,
+        scratch_shapes=[
+            VMEM((512, 128), f32),
+            VMEM((4, 2, 32, 128), bf16),
+            VMEM((4, 2, 32, 128), bf16),
+            VMEM((4, 128, 512), bf16),
+            VMEM((4, 128, 128), bf16),
+            VMEM((4, 128, 128), bf16),
+            VMEM((4, 128, 128), f32),
+            VMEM((4, 128, 128), f32),
+            DMA, DMA, DMA, DMA((4,)), DMA, DMA((16,)),
+            DMA, DMA((4,)), DMA, DMA((4,)), DMA, DMA((4,)), DMA, DMA((4,)),
+            DMA, DMA((4,)), DMA,
+        ],
+        compiler_params=pltpu.CompilerParams(
+            collective_id=0, has_side_effects=True, vmem_limit_bytes=48 << 20
+        ),
+        name="forward",
+    )(emb, proj, w_in, bias, d_part, cot)
 
 
 def local(embeddings, projection, w_in, bias, w_out, cotangent):
@@ -37,31 +269,20 @@
     own = toks // (rows * cols)
     hid = w_out.shape[0]
     hid_local = w_in.shape[1]
+    count = rows * embs * rank
     flat_out = w_out.reshape(hid, feat * embs)
     cot_rows = cotangent.reshape(toks, feat * embs)
-    partial = contract_last(cot_rows, flat_out).astype(bf16)
-    partial = jnp.moveaxis(partial.reshape(toks, cols, hid_local), 1, 0)
-    d_cols = summed(swap(partial, "col"))
-    d_hidden = jnp.sum(everyone(d_cols, "row"), axis=0)
-    every_cot = everyone(cot_rows, "batch")
-    emb = swap(embeddings.reshape(cols * rows, own, feat, embs), ("col", "row"))
-    emb = emb.reshape(cols, rows, own, feat, embs).transpose(2, 0, 3, 1, 4)
+    d_part = contract_last(cot_rows, flat_out).astype(bf16)
+    act, hidden, d_preact, d_pre_b, normed, inv, own_emb, every_cot = forward(
+        embeddings.reshape(64, own, feat, embs), projection, w_in.reshape(32, 128, hid_local),
+        bias.reshape(1, hid_local), d_part, cot_rows,
+    )
+    act = jnp.moveaxis(act.reshape(32, toks, 128), 1, 0).reshape(toks, embs * rank)
+    emb = own_emb.reshape(rows, own, cols * feat, embs).transpose(1, 2, 0, 3)
     emb = emb.reshape(own, cols * feat, rows * embs)
     emb_float = emb.astype(f32)
-    folded = jnp.einsum("bde,ek->bdk", emb, projection, preferred_element_type=f32)
-    interact = jnp.einsum("bde,bdk->bek", emb_float, folded, precision=highest)
-    count = rows * embs * rank
-    inv_rms = lax.rsqrt(jnp.sum(interact * interact, axis=(1, 2)) / count + epsilon)[:, None, None]
-    normed = interact * inv_rms
-    activated = normed.astype(bf16).reshape(own, rows, embs * rank)
-    act = swap(jnp.moveaxis(activated, 1, 0), "row").reshape(rows * own, embs * rank)
-    act = everyone(act, "col").reshape(toks, embs * rank)
-    pre = jnp.dot(act, w_in, preferred_element_type=f32)
-    preact = jnp.sum(everyone(pre, "row"), axis=0) + bias
-    hidden = jax.nn.silu(preact).astype(bf16)
-    sig = jax.nn.sigmoid(preact)
-    d_preact = d_hidden * sig * (1.0 + preact * (1.0 - sig))
-    d_pre_b = d_preact.astype(bf16)
+    normed = normed.reshape(own, rows * embs, rank)
+    inv_rms = inv[:, :1, :1]
     d_part = contract_last(d_pre_b, w_in).astype(bf16).reshape(cols, rows * own, embs * rank)
     d_rows = summed(swap(d_part, "col")).astype(bf16)
     d_act = swap(d_rows.reshape(rows, own, embs * rank), "row").astype(f32)

time: 305 us -> 223 us (0.73)
  Pallas kernels: 0 us -> 50.2 us
  starting transfers between devices: 96.8 us -> 52.8 us
  blocking collectives: 41.8 us -> 0 us
  waiting for transfers between devices: 103 us -> 79.6 us
  local copies, waits for them, and re-layouts: 33.3 us -> 20 us
  other arithmetic: 12 us -> 5.75 us
    pallas_call x0 -> x1, Pallas kernels: none -> 50.2 us  [forward(): pl.pallas_call(forward_kernel, out_shape=(out((32, 16, 8, 128), bf16), ou...]
    all_to_all x15 -> x10, starting transfers between devices: 96.8 us -> 52.8 us  [swap(): return lax.all_to_all(tiles, axis, 0, 0, tiled=True)]
    all_to_all x2 -> x0, blocking collectives: 41.8 us -> none  [swap(): return lax.all_to_all(tiles, axis, 0, 0, tiled=True)]
    all_to_all x15 -> x10, waiting for transfers between devices: 103 us -> 79.6 us  [swap(): return lax.all_to_all(tiles, axis, 0, 0, tiled=True)]
    reshape x3 -> x1, local copies, waits for them, and re-layouts: 4.49 us -> 1.08 us  [local(): d_act = jnp.moveaxis(d_act, 0, 1).reshape(own, rows * embs, rank)]
    reduce_sum x2 -> x0, other arithmetic: 3.2 us -> none  [the longest x1 1.6 us: local(): d_hidden = jnp.sum(everyone(d_cols, 'row'), axis=0)]
    broadcast_in_dim x9 -> x4, local copies, waits for them, and re-layouts: 6.92 us -> 4.02 us  [everyone(): return swap(jnp.broadcast_to(array[None], (size, *array.shape)), axis)]
    unnamed x16 -> x21, local copies, waits for them, and re-layouts: 5.75 us -> 6.7 us
  transfers between devices with their start and end apart: 15 -> 10, of which waited for: 12 -> 10; matrix products, arithmetic and copies ran while one was open for 16% -> 11% of each run, Pallas kernels for 0% -> 0%
where the time goes in v2:
time: 223 us; the launch traced here: 222 us
  waiting for transfers between devices  79.6 us (36%)
  starting transfers between devices  52.8 us (24%)
  Pallas kernels  50.2 us (23%)
  local copies, waits for them, and re-layouts  20 us (9%)
  matrix products  12.7 us (6%)
  other arithmetic  5.75 us (3%)
    all_to_all x10, waiting for transfers between devices, swap(): return lax.all_to_all(tiles, axis, 0, 0, tiled=True)  79.6 us
    all_to_all x10, starting transfers between devices, swap(): return lax.all_to_all(tiles, axis, 0, 0, tiled=True)  52.8 us
    pallas_call x1, Pallas kernels, forward(): pl.pallas_call(forward_kernel, out_shape=(out((32, 16, 8, 128), bf16), ou...  50.2 us
    unnamed x21, local copies, waits for them, and re-layouts  6.7 us
    dot_general x2, matrix products, contract_last(): lax.dot_general(left, right, (((1,), (1,)), ((), ())), preferred_element_...  5.21 us
  transfers between devices with their start and end apart: 10, of which 10 were waited for; matrix products, arithmetic and copies ran while one was open for 11% of the time, Pallas kernels for 0%

profile of v2, /device:TPU:1, one launch (start us, length us, event | category | flops | bytes accessed | tf_op | source)
XLA Modules:
  0.0 221.9 jit_solution(1356916518862939967)
XLA Ops:
  2.7 3.8 %fusion.9.d_part = bf16[128,2048]{1,0:T(8,128)(2,1)S(1)} fusion(bf16[2048,8,128]{2,1,0:T(8,128)(2,1)} %param.10, bf16[128,8,128]{2,1,0:T(8,128)(2,1)} %param.11), kind=kOutput, calls=%fused_computation.9 | convolution fusion | flops 537133056 | bytes 4980736 | tf_op jit(solution)/shard_map/dot_general | solution.py:28
  6.5 50.2 %forward.1 = (bf16[32,16,8,128]{3,2,1,0:T(8,128)(2,1)S(1)}, bf16[128,128]{1,0:T(8,128)(2,1)S(1)}, f32[128,128]{1,0:T(8,128)S(1)}, bf16[128,128]{1,0:T(8,128)(2,1...) custom-call(bf16[64,2,8,128]{3,2,1,0:T(8,128)(2,1)S(1)} %bitcast.78,, ...), custom_call_target="tpu_custom_call" | custom-call | tf_op jit(solution)/shard_map/forward/pallas_call | solution.py:230
  57.4 1.4 fusion
  58.8 4.5 %all-to-all-start.5 = ((bf16[16,8,4096]{2,1,0:T(8,128)(2,1)}), bf16[16,8,4096]{2,1,0:T(8,128)(2,1)}, u32[]{:S(2)}, u32[]{:S(2)}) async-start(bf16[16,8,4096]{2,1,0:T(8,128)(2,1)} %fusion), calls=%async_computation.5 | async-start | bytes 2097152 | tf_op jit(solution)/shard_map/all_to_all | solution.py:19
  63.3 22.0 %all-to-all-done.5 = bf16[16,8,4096]{2,1,0:T(8,128)(2,1)} async-done(((bf16[16,8,4096]{2,1,0:T(8,128)(2,1)}), bf16[16,8,4096]{2,1,0:T(8,128)(2,1)}, u32[]{:S(2)}, u32[]{:S(2)}) %all-to-all-start.5) | async-done | bytes 1048608 | tf_op jit(solution)/shard_map/all_to_all | solution.py:19
  86.0 12.8 %all-to-all-start.4 = ((f32[4,1,128]{2,1,0:T(1,128)}), f32[4,1,128]{2,1,0:T(1,128)S(1)}, u32[]{:S(2)}, u32[]{:S(2)}) async-start(f32[4,1,128]{2,1,0:T(1,128)} %broadcast_in_dim.10), calls=%async_computation.4 | async-start | bytes 4096 | tf_op jit(solution)/shard_map/all_to_all | solution.py:19
  98.8 1.4 reduce_sum.72
  101.8 3.3 %all-to-all-start.6 = ((bf16[4,2,4096]{2,1,0:T(2,128)(2,1)}), bf16[4,2,4096]{2,1,0:T(2,128)(2,1)S(1)}, u32[]{:S(2)}, u32[]{:S(2)}) async-start(bf16[4,2,4096]{2,1,0:T(2,128)(2,1)} %reshape.123), calls=%async_computation.6 | async-start | bytes 131072 | tf_op jit(solution)/shard_map/all_to_all | solution.py:19
  108.4 1.1 all-to-all-done.6
  109.5 1.7 broadcast_in_dim.8
  111.2 3.6 %all-to-all-start = ((bf16[16,128,128]{1,2,0:T(8,128)(2,1)}), bf16[16,128,128]{1,2,0:T(8,128)(2,1)S(1)}, u32[]{:S(2)}, u32[]{:S(2)}) async-start(bf16[16,128,128]{1,2,0:T(8,128)(2,1)} %broadcast_in_dim.8), calls=%async_computation | async-start | bytes 1048576 | tf_op jit(solution)/shard_map/all_to_all | solution.py:19
  115.6 1.1 reshape.124
  116.7 1.2 fusion.22
  117.8 1.3 convolution_bitcast_fusion.1
  120.1 12.1 %all-to-all-done = bf16[16,128,128]{1,2,0:T(8,128)(2,1)S(1)} async-done(((bf16[16,128,128]{1,2,0:T(8,128)(2,1)}), bf16[16,128,128]{1,2,0:T(8,128)(2,1)S(1)}, u32[]{:S(2)}, u32[]{:S(2)}) %all-to-all-start) | async-done | bytes 524320 | tf_op jit(solution)/shard_map/all_to_all | solution.py:19
  132.2 3.3 %all-to-all-start.7 = ((f32[4,128,32]{1,2,0:T(8,128)}), f32[4,128,32]{1,2,0:T(8,128)S(1)}, u32[]{:S(2)}, u32[]{:S(2)}) async-start(f32[4,128,32]{1,2,0:T(8,128)} %convolution_bitcast_fusion), calls=%async_computation.7 | async-start | bytes 131072 | tf_op jit(solution)/shard_map/all_to_all | solution.py:19
  135.5 1.4 convolution_convert_fusion.1
  136.9 3.0 %all-to-all-done.7 = f32[4,128,32]{1,2,0:T(8,128)S(1)} async-done(((f32[4,128,32]{1,2,0:T(8,128)}), f32[4,128,32]{1,2,0:T(8,128)S(1)}, u32[]{:S(2)}, u32[]{:S(2)}) %all-to-all-start.7) | async-done | bytes 65568 | tf_op jit(solution)/shard_map/all_to_all | solution.py:19
  140.0 7.0 %all-to-all-start.2 = ((bf16[4,1024,128]{2,1,0:T(8,128)(2,1)}), bf16[4,1024,128]{2,1,0:T(8,128)(2,1)S(1)}, u32[]{:S(2)}, u32[]{:S(2)}) async-start(bf16[4,1024,128]{2,1,0:T(8,128)(2,1)} %bitcast.14), calls=%async_computation.2 | async-start | bytes 2097152 | tf_op jit(solution)/shard_map/all_to_all | solution.py:19
  147.8 12.7 %all-to-all-done.2 = bf16[4,1024,128]{2,1,0:T(8,128)(2,1)S(1)} async-done(((bf16[4,1024,128]{2,1,0:T(8,128)(2,1)}), bf16[4,1024,128]{2,1,0:T(8,128)(2,1)S(1)}, u32[]{:S(2)}, u32[]{:S(2)}) %all-to-all-start.2) | async-done | bytes 1048608 | tf_op jit(solution)/shard_map/all_to_all | solution.py:19
  160.4 5.1 %all-to-all-start.8 = ((f32[64,1,64]{2,1,0:T(1,128)}), f32[64,1,64]{2,1,0:T(1,128)S(1)}, u32[]{:S(2)}, u32[]{:S(2)}) async-start(f32[64,1,64]{2,1,0:T(1,128)} %bitcast.28), calls=%async_computation.8 | async-start | bytes 65536 | tf_op jit(solution)/shard_map/all_to_all | solution.py:19
  166.6 8.2 %all-to-all-done.8 = f32[64,1,64]{2,1,0:T(1,128)S(1)} async-done(((f32[64,1,64]{2,1,0:T(1,128)}), f32[64,1,64]{2,1,0:T(1,128)S(1)}, u32[]{:S(2)}, u32[]{:S(2)}) %all-to-all-start.8) | async-done | bytes 16416 | tf_op jit(solution)/shard_map/all_to_all | solution.py:19
  174.8 4.0 %all-to-all-start.1 = ((bf16[4,4,128,128]{3,2,1,0:T(8,128)(2,1)}), bf16[4,4,128,128]{3,2,1,0:T(8,128)(2,1)S(1)}, u32[]{:S(2)}, u32[]{:S(2)}) async-start(bf16[4,4,128,128]{3,2,1,0:T(8,128)(2,1)} %bitcast.86), calls=%async_computation.1 | async-start | bytes 1048576 | tf_op jit(solution)/shard_map/all_to_all | solution.py:19
  178.9 7.8 %all-to-all-done.1 = bf16[4,4,128,128]{3,2,1,0:T(8,128)(2,1)S(1)} async-done(((bf16[4,4,128,128]{3,2,1,0:T(8,128)(2,1)}), bf16[4,4,128,128]{3,2,1,0:T(8,128)(2,1)S(1)}, u32[]{:S(2)}, u32[]{:S(2)}) %all-to-all-start.1) | async-done | bytes 524320 | tf_op jit(solution)/shard_map/all_to_all | solution.py:19
  187.4 5.1 %all-to-all-start.9 = ((f32[64,1,64]{2,1,0:T(1,128)}), f32[64,1,64]{2,1,0:T(1,128)S(1)}, u32[]{:S(2)}, u32[]{:S(2)}) async-start(f32[64,1,64]{2,1,0:T(1,128)} %broadcast_in_dim.11), calls=%async_computation.9 | async-start | bytes 65536 | tf_op jit(solution)/shard_map/all_to_all | solution.py:19
  192.7 9.0 %all-to-all-done.9 = f32[64,1,64]{2,1,0:T(1,128)S(1)} async-done(((f32[64,1,64]{2,1,0:T(1,128)}), f32[64,1,64]{2,1,0:T(1,128)S(1)}, u32[]{:S(2)}, u32[]{:S(2)}) %all-to-all-start.9) | async-done | bytes 16416 | tf_op jit(solution)/shard_map/all_to_all | solution.py:19
  201.7 1.1 broadcast_in_dim.9
  202.8 4.1 %all-to-all-start.3 = ((bf16[4,1024,128]{2,1,0:T(8,128)(2,1)}), bf16[4,1024,128]{2,1,0:T(8,128)(2,1)S(1)}, u32[]{:S(2)}, u32[]{:S(2)}) async-start(bf16[4,1024,128]{2,1,0:T(8,128)(2,1)} %broadcast_in_dim.9), calls=%async_computation.3 | async-start | bytes 2097152 | tf_op jit(solution)/shard_map/all_to_all | solution.py:19
  208.0 3.1 %fusion.15 = bf16[16,8,8,128]{3,1,2,0:T(8,128)(2,1)S(1)} fusion(bf16[128,2048]{0,1:T(8,128)(2,1)} %bitcast.84, bf16[256,8,8,128]{3,2,1,0:T(8,128)(2,1)} %bitcast.90), kind=kOutput, calls=%fused_computation.11 | convolution fusion | flops 537001984 | bytes 4980736 | tf_op jit(solution)/shard_map/dot_general | solution.py:300
  213.1 2.5 %copy.80 = f32[512,8,128]{2,1,0:T(8,128)} copy(f32[512,8,128]{2,0,1:T(8,128)S(1)} %fusion.23) | data formatting | bytes 4194304
  217.7 2.7 %all-to-all-done.3 = bf16[4,1024,128]{2,1,0:T(8,128)(2,1)S(1)} async-done(((bf16[4,1024,128]{2,1,0:T(8,128)(2,1)}), bf16[4,1024,128]{2,1,0:T(8,128)(2,1)S(1)}, u32[]{:S(2)}, u32[]{:S(2)}) %all-to-all-start.3) | async-done | bytes 1048608 | tf_op jit(solution)/shard_map/all_to_all | solution.py:19
  220.4 1.5 bitcast_convert_fusion
  (49 shorter events, 18.0 us)
Async XLA Ops:
  0.6 5.9 %copy-start = (bf16[4096,128]{1,0:T(8,128)(2,1)S(1)}, bf16[4096,128]{1,0:T(8,128)(2,1)}, u32[]{:S(2)}) copy-start(bf16[4096,128]{1,0:T(8,128)(2,1)} %param.8) | copy-start | bytes 3145732
  0.6 5.9 %copy-start.4 = (f32[128]{0:T(128)S(1)}, f32[128]{0:T(128)}, u32[]{:S(2)}) copy-start(f32[128]{0:T(128)} %param.9) | copy-start | bytes 1540
  1.6 4.9 %copy-start.1 = (bf16[128,8,128]{2,1,0:T(8,128)(2,1)S(1)}, bf16[128,8,128]{2,1,0:T(8,128)(2,1)}, u32[]{:S(2)}) copy-start(bf16[128,8,128]{2,1,0:T(8,128)(2,1)} %param.6) | copy-start | bytes 786436
  56.7 0.7 copy-start.2
  58.8 48.8 %copy-start.3 = (bf16[4,2,16,8,128]{4,3,2,1,0:T(8,128)(2,1)S(1)}, bf16[4,2,16,8,128]{4,3,2,1,0:T(8,128)(2,1)}, u32[]{:S(2)}) copy-start(bf16[4,2,16,8,128]{4,3,2,1,0:T(8,128)(2,1)} %copy-done.2) | copy-start | bytes 786436
  58.8 26.6 %all-to-all-start.5 = ((bf16[16,8,4096]{2,1,0:T(8,128)(2,1)}), bf16[16,8,4096]{2,1,0:T(8,128)(2,1)}, u32[]{:S(2)}, u32[]{:S(2)}) async-start(bf16[16,8,4096]{2,1,0:T(8,128)(2,1)} %fusion), calls=%async_computation.5 | async-start | bytes 2097152 | tf_op jit(solution)/shard_map/all_to_all | solution.py:19
  86.0 15.8 %all-to-all-start.4 = ((f32[4,1,128]{2,1,0:T(1,128)}), f32[4,1,128]{2,1,0:T(1,128)S(1)}, u32[]{:S(2)}, u32[]{:S(2)}) async-start(f32[4,1,128]{2,1,0:T(1,128)} %broadcast_in_dim.10), calls=%async_computation.4 | async-start | bytes 4096 | tf_op jit(solution)/shard_map/all_to_all | solution.py:19
  101.8 7.7 %all-to-all-start.6 = ((bf16[4,2,4096]{2,1,0:T(2,128)(2,1)}), bf16[4,2,4096]{2,1,0:T(2,128)(2,1)S(1)}, u32[]{:S(2)}, u32[]{:S(2)}) async-start(bf16[4,2,4096]{2,1,0:T(2,128)(2,1)} %reshape.123), calls=%async_computation.6 | async-start | bytes 131072 | tf_op jit(solution)/shard_map/all_to_all | solution.py:19
  111.2 21.0 %all-to-all-start = ((bf16[16,128,128]{1,2,0:T(8,128)(2,1)}), bf16[16,128,128]{1,2,0:T(8,128)(2,1)S(1)}, u32[]{:S(2)}, u32[]{:S(2)}) async-start(bf16[16,128,128]{1,2,0:T(8,128)(2,1)} %broadcast_in_dim.8), calls=%async_computation | async-start | bytes 1048576 | tf_op jit(solution)/shard_map/all_to_all | solution.py:19
  132.2 70.6 %copy-start.5 = (bf16[16,128,128]{1,2,0:T(8,128)(2,1)}, bf16[16,128,128]{1,2,0:T(8,128)(2,1)S(1)}, u32[]{:S(2)}) copy-start(bf16[16,128,128]{1,2,0:T(8,128)(2,1)S(1)} %all-to-all-done) | copy-start | bytes 1572868
  132.2 7.7 %all-to-all-start.7 = ((f32[4,128,32]{1,2,0:T(8,128)}), f32[4,128,32]{1,2,0:T(8,128)S(1)}, u32[]{:S(2)}, u32[]{:S(2)}) async-start(f32[4,128,32]{1,2,0:T(8,128)} %convolution_bitcast_fusion), calls=%async_computation.7 | async-start | bytes 131072 | tf_op jit(solution)/shard_map/all_to_all | solution.py:19
  140.0 20.5 %all-to-all-start.2 = ((bf16[4,1024,128]{2,1,0:T(8,128)(2,1)}), bf16[4,1024,128]{2,1,0:T(8,128)(2,1)S(1)}, u32[]{:S(2)}, u32[]{:S(2)}) async-start(bf16[4,1024,128]{2,1,0:T(8,128)(2,1)} %bitcast.14), calls=%async_computation.2 | async-start | bytes 2097152 | tf_op jit(solution)/shard_map/all_to_all | solution.py:19
  160.4 14.4 %all-to-all-start.8 = ((f32[64,1,64]{2,1,0:T(1,128)}), f32[64,1,64]{2,1,0:T(1,128)S(1)}, u32[]{:S(2)}, u32[]{:S(2)}) async-start(f32[64,1,64]{2,1,0:T(1,128)} %bitcast.28), calls=%async_computation.8 | async-start | bytes 65536 | tf_op jit(solution)/shard_map/all_to_all | solution.py:19
  174.8 11.9 %all-to-all-start.1 = ((bf16[4,4,128,128]{3,2,1,0:T(8,128)(2,1)}), bf16[4,4,128,128]{3,2,1,0:T(8,128)(2,1)S(1)}, u32[]{:S(2)}, u32[]{:S(2)}) async-start(bf16[4,4,128,128]{3,2,1,0:T(8,128)(2,1)} %bitcast.86), calls=%async_computation.1 | async-start | bytes 1048576 | tf_op jit(solution)/shard_map/all_to_all | solution.py:19
  186.7 16.1 %copy-start.6 = (bf16[4,4,128,128]{3,2,1,0:T(8,128)(2,1)}, bf16[4,4,128,128]{3,2,1,0:T(8,128)(2,1)S(1)}, u32[]{:S(2)}) copy-start(bf16[4,4,128,128]{3,2,1,0:T(8,128)(2,1)S(1)} %all-to-all-done.1) | copy-start | bytes 1572868
  187.4 14.4 %all-to-all-start.9 = ((f32[64,1,64]{2,1,0:T(1,128)}), f32[64,1,64]{2,1,0:T(1,128)S(1)}, u32[]{:S(2)}, u32[]{:S(2)}) async-start(f32[64,1,64]{2,1,0:T(1,128)} %broadcast_in_dim.11), calls=%async_computation.9 | async-start | bytes 65536 | tf_op jit(solution)/shard_map/all_to_all | solution.py:19
  202.8 17.6 %all-to-all-start.3 = ((bf16[4,1024,128]{2,1,0:T(8,128)(2,1)}), bf16[4,1024,128]{2,1,0:T(8,128)(2,1)S(1)}, u32[]{:S(2)}, u32[]{:S(2)}) async-start(bf16[4,1024,128]{2,1,0:T(8,128)(2,1)} %broadcast_in_dim.9), calls=%async_computation.3 | async-start | bytes 2097152 | tf_op jit(solution)/shard_map/all_to_all | solution.py:19
  207.5 4.4 %copy-start.7 = (bf16[4,4,128,128]{3,2,1,0:T(8,128)(2,1)S(1)}, bf16[4,4,128,128]{3,2,1,0:T(8,128)(2,1)}, u32[]{:S(2)}) copy-start(bf16[4,4,128,128]{3,2,1,0:T(8,128)(2,1)} %copy-done.6) | copy-start | bytes 1572868

commit v3 on v2

--- a/solution.py
+++ b/solution.py
@@ -15,15 +15,6 @@
 DMA = pltpu.SemaphoreType.DMA
 
 
-def swap(tiles, axis):
-    return lax.all_to_all(tiles, axis, 0, 0, tiled=True)
-
-
-def everyone(array, axis):
-    size = lax.axis_size(axis)
-    return swap(jnp.broadcast_to(array[None], (size, *array.shape)), axis)
-
-
 def contract_last(left, right):
     return lax.dot_general(left, right, (((1,), (1,)), ((), ())), preferred_element_type=f32)
 
@@ -34,10 +25,6 @@
 
 def dot(left, right):
     return jnp.dot(left, right, preferred_element_type=f32)
-
-
-def summed(tiles):
-    return jnp.sum(tiles.astype(f32), axis=0)
 
 
 def send(src, dst, send_sem, recv_sem, **place):
@@ -261,56 +248,271 @@
     )(emb, proj, w_in, bias, d_part, cot)
 
 
+def lanes_of(slot, size=128):
+    return pl.ds(pl.multiple_of(slot * size, size), size)
+
+
+def backward_kernel(
+    hidden, d_pre_b, d_pre, w_in, gathered, normed, inv, own_emb,
+    hidden_all, own_hidden, grad_in, grad_proj, grad_bias,
+    d_act, d_y, d_z_out, d_z, d_row_out, d_row, spread, acts, d_all, bias_all,
+    proj_out, proj_x, proj_y, proj_z, proj_b,
+    h_send, h_recv, oh_send, oh_recv, dy_send, dy_recv, dz_send, dz_recv, row_send, row_recv,
+    acts_send, acts_recv, all_send, all_recv, in_send, in_recv, bias_send, bias_recv,
+    px_send, px_recv, py_send, py_recv, pz_send, pz_recv, pb_send, pb_recv, own_sem,
+):
+    i, r, c, y, z, sibling, across = places()
+    barrier = pltpu.get_barrier_semaphore()
+    for k in (1, 2, 3):
+        for place in (
+            {"row": lax.rem(r + k, 4)},
+            {"col": lax.rem(y + k, 4) * 4 + z},
+            {"col": y * 4 + lax.rem(z + k, 4)},
+            {"batch": lax.rem(i + k, 4)},
+        ):
+            pl.semaphore_signal(barrier, inc=1, device_id=place, device_id_type=MESH)
+    pl.semaphore_wait(barrier, 12)
+    mine = pltpu.make_async_copy(gathered.at[pl.ds(8 * i, 8)], acts.at[i], own_sem)
+    mine.start()
+    for k in (1, 2, 3):
+        to = lax.rem(z + k, 4)
+        send(hidden, hidden_all.at[:, lanes_of(c)], h_send, h_recv.at[c], col=y * 4 + to)
+    for half in range(2):
+        for e in range(16):
+            part = contract_last(d_pre_b[...], w_in[half * 16 + e])
+            d_act[half, e] = part.reshape(16, 8, 128).astype(bf16)
+        for k in (1, 2, 3):
+            to = lax.rem(y + k, 4)
+            send(
+                d_act.at[half, :, pl.ds(4 * to, 4)], d_y.at[half, y],
+                dy_send, dy_recv.at[half, y], col=to * 4 + z,
+            )
+    for k in (1, 2, 3):
+        to = lax.rem(y + k, 4)
+        send(hidden, hidden_all.at[:, lanes_of(c)], h_send, h_recv.at[c], col=to * 4 + z)
+    hidden_all[:, lanes_of(c)] = hidden[...]
+    bias_all[i] = jnp.broadcast_to(jnp.sum(d_pre[...], axis=0, keepdims=True), (8, 128))
+    d_all[i] = d_pre_b[...]
+    for k in (1, 2, 3):
+        to = lax.rem(i + k, 4)
+        send(d_pre_b, d_all.at[i], all_send, all_recv.at[i], batch=to)
+        send(bias_all.at[i], bias_all.at[i], bias_send, bias_recv.at[i], batch=to)
+        send(gathered.at[pl.ds(8 * to, 8)], acts.at[i], acts_send, acts_recv.at[i], batch=to)
+    for m in (1, 2, 3):
+        slot = y * 4 + lax.rem(z + m, 4)
+        arrived(hidden_all.at[:, lanes_of(slot)], h_recv.at[slot])
+        for k in (1, 2, 3):
+            to = lax.rem(y + k, 4)
+            send(
+                hidden_all.at[:, lanes_of(slot)], hidden_all.at[:, lanes_of(slot)],
+                h_send, h_recv.at[slot], col=to * 4 + z,
+            )
+    at = lax.broadcasted_iota(jnp.int32, (256, 256), 0)
+    of = lax.broadcasted_iota(jnp.int32, (256, 256), 1)
+    source = lax.rem(at, 8) // 2 * 64 + lax.rem(at, 2) * 32 + at // 8
+    order = (of == source).astype(f32).astype(bf16)
+    for half in range(2):
+        d_y[half, y] = d_act[half, :, pl.ds(4 * y, 4)]
+        for k in (1, 2, 3):
+            f = lax.rem(y + k, 4)
+            arrived(d_y.at[half, f], dy_recv.at[half, f])
+        for q in range(4):
+            part = d_y[half, 0, :, q].astype(f32)
+            for f in (1, 2, 3):
+                part = part + d_y[half, f, :, q].astype(f32)
+            d_z_out[half, q] = part.astype(bf16)
+        d_z[half, z] = d_z_out[half, z]
+        for k in (1, 2, 3):
+            to = lax.rem(z + k, 4)
+            send(
+                d_z_out.at[half, to], d_z.at[half, z], dz_send, dz_recv.at[half, z],
+                col=y * 4 + to,
+            )
+    for m in (1, 2, 3):
+        for k in range(4):
+            slot = lax.rem(y + m, 4) * 4 + k
+            arrived(hidden_all.at[:, lanes_of(slot)], h_recv.at[slot])
+    for k in (1, 2, 3):
+        to = lax.rem(i + k, 4)
+        send(
+            hidden_all.at[:, lanes_of(to, 512)], own_hidden.at[i], oh_send, oh_recv.at[i],
+            batch=to,
+        )
+    own_hidden[i] = hidden_all[:, lanes_of(i, 512)]
+    mine.wait()
+    for k in (1, 2, 3):
+        f = lax.rem(i + k, 4)
+        arrived(d_all.at[f], all_recv.at[f])
+        arrived(acts.at[f], acts_recv.at[f])
+    for e in range(8):
+        part = contract_first(acts[0, e].reshape(128, 128), d_all[0])
+        for f in (1, 2, 3):
+            part = part + contract_first(acts[f, e].reshape(128, 128), d_all[f])
+        grad_in[i, e] = part.astype(bf16)
+    send(grad_in.at[i], grad_in.at[i], in_send, in_recv.at[i], batch=sibling)
+    send(grad_in.at[i], grad_in.at[i], in_send, in_recv.at[i], batch=across)
+    for half in range(2):
+        for k in (1, 2, 3):
+            f = lax.rem(z + k, 4)
+            arrived(d_z.at[half, f], dz_recv.at[half, f])
+    total = jnp.concatenate(
+        [
+            sum(d_z[half, f].astype(f32) for f in range(4)).reshape(128, 128)
+            for half in range(2)
+        ],
+        axis=0,
+    )
+    high, low = split(total)
+    d_row_out[...] = (contract_first(order, high) + contract_first(order, low)).reshape(
+        4, 2, 32, 128
+    )
+    d_row[r] = d_row_out[r]
+    for k in (1, 2, 3):
+        to = lax.rem(r + k, 4)
+        send(d_row_out.at[to], d_row.at[r], row_send, row_recv.at[r], row=to)
+    block = lax.broadcasted_iota(jnp.int32, (128, 128), 1) // 32
+    for k in (1, 2, 3):
+        f = lax.rem(r + k, 4)
+        arrived(d_row.at[f], row_recv.at[f])
+    for s in range(2):
+        grad = d_row[:, s].reshape(128, 128)
+        norm = normed[s]
+        inner = jnp.sum(jnp.sum(grad * norm, axis=0, keepdims=True), axis=1, keepdims=True)
+        d_inter = (inv[s, 0:1, :] * (grad - norm * (inner / (512 * 32)))).astype(bf16).astype(f32)
+        for j in range(4):
+            spread[pl.ds(j, 128, stride=4), :] = jnp.where(block == j, d_inter, 0.0)
+        tiles = [own_emb[q, s].reshape(128, 128) for q in range(4)]
+        fold = sum(
+            dot(tiles[q], spread[q * 128 : (q + 1) * 128, :].astype(bf16)) for q in range(4)
+        )
+        fold = fold + pltpu.roll(fold, 32, 1)
+        fold = fold + pltpu.roll(fold, 64, 1)
+        high, low = split(fold)
+        for q in range(4):
+            part = contract_first(high, tiles[q])[:32] + contract_first(low, tiles[q])[:32]
+            if s == 0:
+                proj_out[q] = part
+            else:
+                proj_out[q] += part
+    proj_x[r] = proj_out[r]
+    for k in (1, 2, 3):
+        to = lax.rem(r + k, 4)
+        send(proj_out.at[to], proj_x.at[r], px_send, px_recv.at[r], row=to)
+    for k in (1, 2, 3):
+        f = lax.rem(r + k, 4)
+        arrived(proj_x.at[f], px_recv.at[f])
+    proj_y[y] = (proj_x[0] + proj_x[1]) + (proj_x[2] + proj_x[3])
+    for k in (1, 2, 3):
+        to = lax.rem(y + k, 4)
+        send(proj_y.at[y], proj_y.at[y], py_send, py_recv.at[y], col=to * 4 + z)
+    for k in (1, 2, 3):
+        f = lax.rem(y + k, 4)
+        arrived(proj_y.at[f], py_recv.at[f])
+    proj_z[z] = (proj_y[0] + proj_y[1]) + (proj_y[2] + proj_y[3])
+    for k in (1, 2, 3):
+        to = lax.rem(z + k, 4)
+        send(proj_z.at[z], proj_z.at[z], pz_send, pz_recv.at[z], col=y * 4 + to)
+    arrived(grad_in.at[across], in_recv.at[across])
+    send(grad_in.at[across], grad_in.at[across], in_send, in_recv.at[across], batch=sibling)
+    for k in (1, 2, 3):
+        f = lax.rem(z + k, 4)
+        arrived(proj_z.at[f], pz_recv.at[f])
+    proj_b[i] = (proj_z[0] + proj_z[1]) + (proj_z[2] + proj_z[3])
+    for k in (1, 2, 3):
+        to = lax.rem(i + k, 4)
+        send(proj_b.at[i], proj_b.at[i], pb_send, pb_recv.at[i], batch=to)
+    for k in (1, 2, 3):
+        f = lax.rem(i + k, 4)
+        arrived(bias_all.at[f], bias_recv.at[f])
+        arrived(own_hidden.at[f], oh_recv.at[f])
+    grad_bias[...] = (bias_all[0] + bias_all[1]) + (bias_all[2] + bias_all[3])
+    for k in (1, 2, 3):
+        f = lax.rem(i + k, 4)
+        arrived(proj_b.at[f], pb_recv.at[f])
+    grad_proj[...] = (proj_b[0] + proj_b[1]) + (proj_b[2] + proj_b[3])
+    diagonal = lax.rem(sibling + 2, 4)
+    arrived(grad_in.at[sibling], in_recv.at[sibling])
+    arrived(grad_in.at[diagonal], in_recv.at[diagonal])
+    three = pl.ds(0, 3)
+    arrived(hidden_all.at[:, pl.ds(0, 15 * 128)], h_send)
+    arrived(own_hidden.at[three], oh_send)
+    arrived(d_act.at[:, :, pl.ds(0, 12)], dy_send)
+    arrived(d_z.at[:, three], dz_send)
+    arrived(d_row.at[three], row_send)
+    arrived(acts.at[three], acts_send)
+    arrived(d_all.at[three], all_send)
+    arrived(grad_in.at[three], in_send)
+    arrived(bias_all.at[three], bias_send)
+    arrived(proj_x.at[three], px_send)
+    arrived(proj_y.at[three], py_send)
+    arrived(proj_z.at[three], pz_send)
+    arrived(proj_b.at[three], pb_send)
+
+
+def backward(hidden, d_pre_b, d_pre, w_in, gathered, normed, inv, own_emb):
+    out = jax.ShapeDtypeStruct
+    pair = [DMA, DMA((4,))]
+    return pl.pallas_call(
+        backward_kernel,
+        out_shape=(
+            out((128, 2048), bf16),
+            out((4, 128, 512), bf16),
+            out((4, 8, 128, 128), bf16),
+            out((32, 128), f32),
+            out((8, 128), f32),
+        ),
+        in_specs=[pl.BlockSpec(memory_space=VMEM)] * 8,
+        out_specs=[pl.BlockSpec(memory_space=VMEM)] * 5,
+        scratch_shapes=[
+            VMEM((2, 16, 16, 8, 128), bf16),
+            VMEM((2, 4, 16, 4, 8, 128), bf16),
+            VMEM((2, 4, 16, 8, 128), bf16),
+            VMEM((2, 4, 16, 8, 128), bf16),
+            VMEM((4, 2, 32, 128), f32),
+            VMEM((4, 2, 32, 128), f32),
+            VMEM((512, 128), f32),
+            VMEM((4, 8, 16, 8, 128), bf16),
+            VMEM((4, 128, 128), bf16),
+            VMEM((4, 8, 128), f32),
+            VMEM((4, 32, 128), f32),
+            VMEM((4, 32, 128), f32),
+            VMEM((4, 32, 128), f32),
+            VMEM((4, 32, 128), f32),
+            VMEM((4, 32, 128), f32),
+            DMA, DMA((16,)), *pair, DMA, DMA((2, 4)), DMA, DMA((2, 4)), *pair,
+            *pair, *pair, *pair, *pair,
+            *pair, *pair, *pair, *pair, DMA,
+        ],
+        compiler_params=pltpu.CompilerParams(
+            collective_id=1, has_side_effects=True, vmem_limit_bytes=48 << 20
+        ),
+        name="backward",
+    )(hidden, d_pre_b, d_pre, w_in, gathered, normed, inv, own_emb)
+
+
 def local(embeddings, projection, w_in, bias, w_out, cotangent):
-    highest = lax.Precision.HIGHEST
     toks, feat, embs = embeddings.shape
-    rank = projection.shape[1]
-    rows, cols, batches = lax.axis_size("row"), lax.axis_size("col"), lax.axis_size("batch")
-    own = toks // (rows * cols)
     hid = w_out.shape[0]
     hid_local = w_in.shape[1]
-    count = rows * embs * rank
     flat_out = w_out.reshape(hid, feat * embs)
     cot_rows = cotangent.reshape(toks, feat * embs)
     d_part = contract_last(cot_rows, flat_out).astype(bf16)
-    act, hidden, d_preact, d_pre_b, normed, inv, own_emb, every_cot = forward(
-        embeddings.reshape(64, own, feat, embs), projection, w_in.reshape(32, 128, hid_local),
+    w_tiles = w_in.reshape(32, 128, hid_local)
+    act, hidden, d_pre, d_pre_b, normed, inv, own_emb, every_cot = forward(
+        embeddings.reshape(64, 2, feat, embs), projection, w_tiles,
         bias.reshape(1, hid_local), d_part, cot_rows,
     )
-    act = jnp.moveaxis(act.reshape(32, toks, 128), 1, 0).reshape(toks, embs * rank)
-    emb = own_emb.reshape(rows, own, cols * feat, embs).transpose(1, 2, 0, 3)
-    emb = emb.reshape(own, cols * feat, rows * embs)
-    emb_float = emb.astype(f32)
-    normed = normed.reshape(own, rows * embs, rank)
-    inv_rms = inv[:, :1, :1]
-    d_part = contract_last(d_pre_b, w_in).astype(bf16).reshape(cols, rows * own, embs * rank)
-    d_rows = summed(swap(d_part, "col")).astype(bf16)
-    d_act = swap(d_rows.reshape(rows, own, embs * rank), "row").astype(f32)
-    d_act = jnp.moveaxis(d_act, 0, 1).reshape(own, rows * embs, rank)
-    inner = (jnp.sum(d_act * normed, axis=(1, 2)) / count)[:, None, None]
-    d_inter = (inv_rms * (d_act - normed * inner)).astype(bf16)
-    back_fold = jnp.einsum("bek,bde->bdk", d_inter, emb, preferred_element_type=f32)
-    part_proj = jnp.einsum("bde,bdk->ek", emb_float, back_fold, precision=highest)
-    part_proj = jnp.sum(swap(part_proj.reshape(rows, embs, rank), "row"), axis=0)
-    everywhere = ("batch", "col")
-    group = batches * cols
-    share = jnp.sum(swap(part_proj.reshape(group, -1), everywhere), axis=0)
-    grad_proj = everyone(share, everywhere).reshape(embs, rank)
-    hidden_all = everyone(hidden, "col")
-    mixed = jnp.dot(
-        jnp.moveaxis(hidden_all, 0, 1).reshape(toks, hid), flat_out, preferred_element_type=f32
-    )
+    hidden_all, own_hidden, grad_in, grad_proj, grad_bias = backward(
+        hidden, d_pre_b, d_pre, w_tiles, act, normed, inv, own_emb
+    )
+    mixed = jnp.dot(hidden_all, flat_out, preferred_element_type=f32)
     mixed = mixed.astype(bf16).reshape(toks, feat, embs)
-    by_batch = hidden_all.reshape(batches, cols // batches, toks, hid_local)
-    own_hidden = swap(by_batch, "batch")
-    own_hidden = own_hidden.transpose(0, 2, 1, 3).reshape(batches * toks, hid // batches)
-    grad_out = contract_first(own_hidden, every_cot.reshape(batches * toks, feat * embs))
-    grad_out = grad_out.reshape(hid // batches, feat, embs)
-    in_part = contract_first(act, d_pre_b).astype(bf16)
-    quarter = summed(swap(in_part.reshape(batches, -1, hid_local), "batch")).astype(bf16)
-    grad_in = everyone(quarter, "batch").astype(f32).reshape(embs * rank, hid_local)
-    grad_bias = jnp.sum(everyone(jnp.sum(d_preact, axis=0), "batch"), axis=0)
-    return (mixed, grad_out, grad_in, grad_bias, grad_proj)
+    grad_out = contract_first(
+        own_hidden.reshape(4 * toks, hid // 4), every_cot.reshape(4 * toks, feat * embs)
+    )
+    grad_out = grad_out.reshape(hid // 4, feat, embs)
+    grad_in = grad_in.astype(f32).reshape(w_in.shape)
+    return (mixed, grad_out, grad_in, grad_bias[0], grad_proj.T)
 
 
 def solution(mesh):

time: 223 us -> 118 us (0.53)
  waiting for transfers between devices: 79.6 us -> 0 us
  starting transfers between devices: 52.8 us -> 0 us
  Pallas kernels: 50.2 us -> 100 us
  local copies, waits for them, and re-layouts: 20 us -> 8.51 us
  matrix products: 12.7 us -> 6.64 us
  other arithmetic: 5.75 us -> 1.52 us
    all_to_all x10 -> x0, waiting for transfers between devices: 79.6 us -> none  [swap(): return lax.all_to_all(tiles, axis, 0, 0, tiled=True)]
    all_to_all x10 -> x0, starting transfers between devices: 52.8 us -> none  [swap(): return lax.all_to_all(tiles, axis, 0, 0, tiled=True)]
    pallas_call x0 -> x1, Pallas kernels: none -> 49.8 us  [backward(): pl.pallas_call(backward_kernel, out_shape=(out((128, 2048), bf16), out((4...]
    dot_general x3 -> x1, matrix products: 5.41 us -> 0.72 us  [local(): mixed = jnp.dot(hidden_all, flat_out, preferred_element_type=f32)]
    reshape x8 -> x0, local copies, waits for them, and re-layouts: 4.55 us -> none  [the longest x2 1.66 us: local(): normed = normed.reshape(own, rows * embs, rank)]
    broadcast_in_dim x4 -> x0, local copies, waits for them, and re-layouts: 4.02 us -> none  [everyone(): return swap(jnp.broadcast_to(array[None], (size, *array.shape)), axis)]
    reduce_sum x7 -> x0, other arithmetic: 3.45 us -> none  [the longest x2 1.64 us: summed(): return jnp.sum(tiles.astype(f32), axis=0)]
    dot_general x2 -> x1, matrix products: 5.21 us -> 3.94 us  [contract_last(): lax.dot_general(left, right, (((1,), (1,)), ((), ())), preferred_element_...]
  transfers between devices with their start and end apart: 10 -> 0, of which waited for: 10 -> 0; matrix products, arithmetic and copies ran while one was open for 11% -> 0% of each run, Pallas kernels for 0% -> 0%
where the time goes in v3:
time: 118 us; the launch traced here: 117 us
  Pallas kernels  100 us (85%)
  local copies, waits for them, and re-layouts  8.51 us (7%)
  matrix products  6.64 us (6%)
  other arithmetic  1.52 us (1%)
    pallas_call x1, Pallas kernels, forward(): pl.pallas_call(forward_kernel, out_shape=(out((32, 16, 8, 128), bf16), ou...  50.2 us
    pallas_call x1, Pallas kernels, backward(): pl.pallas_call(backward_kernel, out_shape=(out((128, 2048), bf16), out((4...  49.8 us
    unnamed x17, local copies, waits for them, and re-layouts  6.68 us
    dot_general x1, matrix products, contract_last(): lax.dot_general(left, right, (((1,), (1,)), ((), ())), preferred_element_...  3.94 us

profile of v3, /device:TPU:1, one launch (start us, length us, event | category | flops | bytes accessed | tf_op | source)
XLA Modules:
  0.0 117.4 jit_solution(16706635507604663044)
XLA Ops:
  0.6 0.0 copy-start.4
  0.6 0.0 copy-start
  0.7 0.0 copy-start.3
  0.7 1.0 copy.13.proj
  1.6 1.0 copy.39
  2.7 0.0 copy-start.5
  2.7 3.9 %fusion.8.d_part = bf16[128,2048]{1,0:T(8,128)(2,1)S(1)} fusion(bf16[2048,8,128]{2,1,0:T(8,128)(2,1)} %param.10, bf16[128,8,128]{2,1,0:T(8,128)(2,1)} %param.11), kind=kOutput, calls=%fused_computation.6 | convolution fusion | flops 537133056 | bytes 4980736 | tf_op jit(solution)/shard_map/dot_general | solution.py:19
  6.6 0.0 copy-done.4
  6.6 0.0 copy-done
  6.6 0.0 copy-done.3
  6.6 50.2 %forward.1 = (bf16[32,16,8,128]{3,2,1,0:T(8,128)(2,1)S(1)}, bf16[128,128]{1,0:T(8,128)(2,1)S(1)}, f32[128,128]{1,0:T(8,128)S(1)}, bf16[128,128]{1,0:T(8,128)(2,1...) custom-call(bf16[64,2,8,128]{3,2,1,0:T(8,128)(2,1)S(1)} %bitcast.43,, ...), custom_call_target="tpu_custom_call" | custom-call | tf_op jit(solution)/shard_map/forward/pallas_call | solution.py:217
  56.9 49.8 %backward.1 = (bf16[128,2048]{1,0:T(8,128)(2,1)S(1)}, bf16[4,128,512]{2,1,0:T(8,128)(2,1)S(1)}, bf16[4,8,128,128]{3,2,1,0:T(8,128)(2,1)S(1)}, f32[32,128]{1,0:T(8,128)S(1)}, f32[8,128]{1,0:T(8,128)S(1)}) custom-call(bf16[128,128]{1,0:T(8,128)(2,1)S(1)} %get-tuple-element.18.hidden, bf16[128,128]{1,0:T(8,128)(2,1)S(1)} %get-tuple-element.19.d_pre_b, ...), custom_call_target="tpu_custom_call" | custom-call | tf_op jit(solution)/shard_map/backward/pallas_call | solution.py:455
  106.7 0.0 copy-start.1
  106.7 0.8 copy-done.1
  107.5 0.0 copy-done.5
  107.5 0.0 copy-start.2
  107.5 0.7 fusion.14
  108.2 0.8 copy.21
  109.0 0.5 slice_bitcast_fusion
  109.5 1.3 %copy.14 = bf16[1024,512]{1,0:T(8,128)(2,1)} copy(bf16[1024,512]{0,1:T(8,128)(2,1)S(1)} %bitcast.41) | data formatting | bytes 2097152 | tf_op jit(solution)/shard_map/dot_general | solution.py:23
  110.8 0.0 copy-done.2
  110.8 2.0 %fusion.18 = f32[512,8,128]{2,0,1:T(8,128)S(1)} fusion(bf16[512,512,1]{1,0,2:T(8,128)(2,1)S(1)} %bitcast.42, bf16[8,128,512]{2,1,0:T(8,128)(2,1)} %bitcast.46), kind=kOutput, calls=%fused_computation.13 | convolution fusion | flops 536870912 | bytes 3670016 | tf_op jit(solution)/shard_map/dot_general | solution.py:23
  112.8 2.5 %copy.16 = f32[512,8,128]{2,1,0:T(8,128)} copy(f32[512,8,128]{2,0,1:T(8,128)S(1)} %fusion.18) | data formatting | bytes 4194304
  115.3 1.5 %bitcast_convert_fusion = f32[4096,128]{1,0:T(8,128)} fusion(bf16[4,8,128,128]{3,2,1,0:T(8,128)(2,1)S(1)} %get-tuple-element.28), kind=kLoop, calls=%fused_computation.9 | loop fusion | flops 524288 | bytes 3145728 | tf_op jit(solution)/shard_map/reshape | solution.py:514
  116.8 0.6 copy.41
Async XLA Ops:
  0.6 6.0 %copy-start.4 = (f32[128]{0:T(128)S(1)}, f32[128]{0:T(128)}, u32[]{:S(2)}) copy-start(f32[128]{0:T(128)} %param.9) | copy-start | bytes 1540
  0.6 6.0 %copy-start = (bf16[4096,128]{1,0:T(8,128)(2,1)S(1)}, bf16[4096,128]{1,0:T(8,128)(2,1)}, u32[]{:S(2)}) copy-start(bf16[4096,128]{1,0:T(8,128)(2,1)} %param.8) | copy-start | bytes 3145732
  0.7 6.0 %copy-start.3 = (bf16[128,8,128]{2,1,0:T(8,128)(2,1)S(1)}, bf16[128,8,128]{2,1,0:T(8,128)(2,1)}, u32[]{:S(2)}) copy-start(bf16[128,8,128]{2,1,0:T(8,128)(2,1)} %param.6) | copy-start | bytes 786436
  2.7 104.8 %copy-start.5 = (bf16[2048,8,128]{2,1,0:T(8,128)(2,1)S(1)}, bf16[2048,8,128]{2,1,0:T(8,128)(2,1)}, u32[]{:S(2)}) copy-start(bf16[2048,8,128]{2,1,0:T(8,128)(2,1)} %param.10) | copy-start | bytes 12582916
  106.7 0.8 copy-start.1
  107.5 3.3 %copy-start.2 = (bf16[4,128,512]{2,1,0:T(8,128)(2,1)S(1)}, bf16[4,128,512]{2,1,0:T(8,128)(2,1)}, u32[]{:S(2)}) copy-start(bf16[4,128,512]{2,1,0:T(8,128)(2,1)} %copy-done.1) | copy-start | bytes 1572868

commit v4 on v1

v4 whole, which is shorter than its diff:
```python
import jax
import jax.numpy as jnp
from jax import lax
from jax.experimental import pallas as pl
from jax.experimental.pallas import tpu as pltpu
from jax.sharding import PartitionSpec as P

epsilon = 1e-06
bf16 = jnp.bfloat16
f32 = jnp.float32
MESH = pl.DeviceIdType.MESH
VMEM = pltpu.VMEM
DMA = pltpu.SemaphoreType.DMA
others = (1, 2, 3)


def contract_last(left, right):
    return lax.dot_general(left, right, (((1,), (1,)), ((), ())), preferred_element_type=f32)


def contract_first(left, right):
    return lax.dot_general(left, right, (((0,), (0,)), ((), ())), preferred_element_type=f32)


def dot(left, right):
    return jnp.dot(left, right, preferred_element_type=f32)


def send(src, dst, send_sem, recv_sem, **place):
    copy = pltpu.make_async_remote_copy(
        src_ref=src, dst_ref=dst, send_sem=send_sem, recv_sem=recv_sem,
        device_id=place, device_id_type=MESH,
    )
    copy.start()


def arrived(ref, sem):
    pltpu.make_async_copy(ref, ref, sem).wait()


def split(value):
    high = value.astype(bf16)
    return high, (value - high.astype(f32)).astype(bf16)


def four(parts):
    return (parts[0] + parts[1]) + (parts[2] + parts[3])


def turn(place, k):
    return lax.rem(place + k, 4)


def lanes_of(slot, size=128):
    return pl.ds(pl.multiple_of(slot * size, size), size)


def whole_sum(value):
    return jnp.sum(jnp.sum(value, axis=0, keepdims=True), axis=1, keepdims=True)


def ordering(size, high):
    at = lax.broadcasted_iota(jnp.int32, (size, size), 0)
    of = lax.broadcasted_iota(jnp.int32, (size, size), 1)
    source = lax.rem(at, 8) // 2 * (2 * high) + lax.rem(at, 2) * high + at // 8
    return (of == source).astype(f32).astype(bf16)


def kernel(
    emb, proj, w_in_far, bias, w_out_far, cot,
    mixed, grad_out, grad_in, grad_bias, grad_proj,
    w_in, w_out, w_split, stage, every_cot, own_emb, folds, normed, inv,
    part_out, part_y, part_z_out, part_z, part_x,
    to_row, raw, gathered, pre_x, hidden, d_pre_b,
    d_act, d_y, d_z_out, d_z, acts, d_all, bias_all, hidden_all, own_hidden, hidden_t,
    proj_out, proj_x, proj_z, proj_b,
    load_in, load_out, emb_send, emb_recv, cot_send, cot_recv,
    py_send, py_recv, pz_send, pz_recv, px_send, px_recv,
    near_send, far_send, raw_recv, pre_send, pre_recv,
    h_send, h_recv, oh_send, oh_recv, dy_send, dy_recv, dz_send, dz_recv,
    acts_send, acts_recv, all_send, all_recv, in_send, in_recv, bias_send, bias_recv,
    gx_send, gx_recv, gz_send, gz_recv, gb_send, gb_recv, own_sem,
):
    i = lax.axis_index("batch")
    r = lax.axis_index("row")
    c = lax.axis_index("col")
    y = c // 4
    z = c - y * 4
    sibling = i + 1 - 2 * lax.rem(i, 2)
    across = turn(i, 2)
    diagonal = turn(sibling, 2)
    me = c * 4 + r
    three = pl.ds(0, 3)
    barrier = pltpu.get_barrier_semaphore()

    def greet(k, _):
        peer = lax.rem(me + k, 64)
        pl.semaphore_signal(
            barrier, inc=1, device_id={"col": peer // 4, "row": lax.rem(peer, 4)},
            device_id_type=MESH,
        )
        return 0

    lax.fori_loop(1, 64, greet, 0)
    for k in others:
        pl.semaphore_signal(barrier, inc=1, device_id={"batch": turn(i, k)}, device_id_type=MESH)
    take_out = pltpu.make_async_copy(w_out_far, w_out, load_out)
    take_out.start()
    take_in = pltpu.make_async_copy(w_in_far, w_in, load_in)
    take_in.start()
    stage[...] = cot[...].astype(f32).reshape(1024, 128)
    for d in range(8):
        every_cot[i, d] = stage[pl.ds(d, 128, stride=8), :].astype(bf16)
    pl.semaphore_wait(barrier, 66)

    keep = pltpu.make_async_copy(emb.at[me], own_emb.at[r, :, c], emb_recv)
    keep.start()

    def give(k, _):
        peer = lax.rem(me + k, 64)
        send(
            emb.at[peer], own_emb.at[r, :, c], emb_send, emb_recv,
            col=peer // 4, row=lax.rem(peer, 4),
        )
        return 0

    lax.fori_loop(1, 64, give, 0)

    take_out.wait()
    for k in (1, 2, 3, 0):
        to = turn(y, k)

        def divide(n, _):
            at = pl.multiple_of(to * 512 + n * 128, 128)
            stage[...] = w_out[pl.ds(at, 128)].astype(f32).reshape(1024, 128)
            for d in range(8):
                w_split[d, pl.ds(at, 128), :] = stage[pl.ds(d, 128, stride=8), :].astype(bf16)
            return 0

        lax.fori_loop(0, 4, divide, 0)
        part = jnp.zeros((128, 512), f32)
        for d in range(8):
            part = part + contract_last(every_cot[i, d], w_split[d, lanes_of(to, 512), :])
        for q in range(4):
            part_out[to, q] = part[:, q * 128 : (q + 1) * 128].astype(bf16)
        if k:
            send(part_out.at[to], part_y.at[y], py_send, py_recv.at[y], col=to * 4 + z)
        else:
            part_y[y] = part_out[y]

    lanes = lax.broadcasted_iota(jnp.int32, (32, 128), 1)
    ranks = lax.broadcasted_iota(jnp.int32, (32, 128), 0)
    repeat = (lax.rem(lanes, 32) == ranks).astype(f32).astype(bf16)
    wide = contract_first(proj[...], repeat).astype(bf16)
    block = lax.broadcasted_iota(jnp.int32, (128, 128), 1) // 32
    order = ordering(256, 32)

    def sample(s):
        return jnp.concatenate([own_emb[q, s].reshape(128, 128) for q in range(4)], axis=1)

    arrived(own_emb, emb_recv)
    for s in range(2):
        own = sample(s)
        high, low = split(dot(own, wide))
        both = contract_first(own, jnp.concatenate([high, low], axis=1))
        folds[...] = both[:, :128] + both[:, 128:]
        inter = jnp.zeros((128, 128), f32)
        for j in range(4):
            inter = jnp.where(block == j, folds[pl.ds(j, 128, stride=4), :], inter)
        scale = lax.rsqrt(whole_sum(inter * inter) / (512 * 32) + epsilon)
        norm = inter * scale
        normed[s] = norm
        inv[s] = jnp.broadcast_to(scale, (8, 128))
        for q in range(4):
            to_row[q, s] = norm[q * 32 : (q + 1) * 32].astype(bf16)
    raw[c, r] = to_row[r]
    plane = z * 4 + r

    def scatter(k, _):
        peer = lax.rem(plane + k, 16)
        to_z = peer // 4
        to_r = lax.rem(peer, 4)
        send(to_row.at[to_r], raw.at[c, r], near_send, raw_recv.at[c], col=y * 4 + to_z, row=to_r)
        return 0

    lax.fori_loop(1, 16, scatter, 0)

    for k in others:
        f = turn(y, k)
        arrived(part_y.at[f], py_recv.at[f])
    for q in range(4):
        part_z_out[q] = four([part_y[f, q].astype(f32) for f in range(4)]).astype(bf16)
    part_z[z] = part_z_out[z]
    for k in others:
        to = turn(z, k)
        send(part_z_out.at[to], part_z.at[z], pz_send, pz_recv.at[z], col=y * 4 + to)

    arrived(raw.at[c, three], raw_recv.at[c])
    for k in others:
        send(raw.at[c], raw.at[c], far_send, raw_recv.at[c], col=turn(y, k) * 4 + z)
    for m in others:
        slot = y * 4 + turn(z, m)
        arrived(raw.at[slot], raw_recv.at[slot])
        for k in others:
            send(raw.at[slot], raw.at[slot], far_send, raw_recv.at[slot], col=turn(y, k) * 4 + z)
    send(every_cot.at[i], every_cot.at[i], cot_send, cot_recv.at[i], batch=sibling)
    send(every_cot.at[i], every_cot.at[i], cot_send, cot_recv.at[i], batch=across)

    def lay(slot):
        rows = dot(order, raw[slot].reshape(256, 128))
        gathered[:, slot] = rows.reshape(32, 8, 128).astype(bf16)

    for q in range(4):
        lay(y * 4 + q)
    for k in others:
        f = turn(z, k)
        arrived(part_z.at[f], pz_recv.at[f])
    part_x[r] = four([part_z[f].astype(f32) for f in range(4)])
    for k in others:
        send(part_x.at[r], part_x.at[r], px_send, px_recv.at[r], row=turn(r, k))
    take_in.wait()
    for k in range(4):
        for m in others:
            slot = turn(y, m) * 4 + turn(z, k)
            arrived(raw.at[slot], raw_recv.at[slot])
            lay(slot)
    pre = jnp.zeros((128, 128), f32)
    for e in range(32):
        pre = pre + dot(gathered[e].reshape(128, 128), w_in[e])
    pre_x[r] = pre
    for k in others:
        send(pre_x.at[r], pre_x.at[r], pre_send, pre_recv.at[r], row=turn(r, k))
    for k in others:
        to = turn(i, k)
        send(gathered.at[pl.ds(8 * to, 8)], acts.at[i], acts_send, acts_recv.at[i], batch=to)
    mine = pltpu.make_async_copy(gathered.at[pl.ds(8 * i, 8)], acts.at[i], own_sem)
    mine.start()
    arrived(every_cot.at[across], cot_recv.at[across])
    send(every_cot.at[across], every_cot.at[across], cot_send, cot_recv.at[across], batch=sibling)
    for k in others:
        f = turn(r, k)
        arrived(part_x.at[f], px_recv.at[f])
    d_hidden = four(part_x)
    for k in others:
        f = turn(r, k)
        arrived(pre_x.at[f], pre_recv.at[f])
    preact = four(pre_x) + bias[...]
    sig = 1.0 / (1.0 + jnp.exp(-preact))
    hidden[...] = (preact * sig).astype(bf16)
    d_value = d_hidden * sig * (1.0 + preact * (1.0 - sig))
    d_pre_b[...] = d_value.astype(bf16)
    bias_all[i] = jnp.broadcast_to(jnp.sum(d_value, axis=0, keepdims=True), (8, 128))

    for k in others:
        send(hidden, hidden_all.at[:, lanes_of(c)], h_send, h_recv.at[c], col=y * 4 + turn(z, k))
    for half in range(2):
        for e in range(16):
            part = contract_last(d_pre_b[...], w_in[half * 16 + e])
            d_act[half, e] = part.reshape(16, 8, 128).astype(bf16)
        for k in others:
            to = turn(y, k)
            send(
                d_act.at[half, :, pl.ds(4 * to, 4)], d_y.at[half, y],
                dy_send, dy_recv.at[half, y], col=to * 4 + z,
            )
    for k in others:
        send(hidden, hidden_all.at[:, lanes_of(c)], h_send, h_recv.at[c], col=turn(y, k) * 4 + z)
    hidden_all[:, lanes_of(c)] = hidden[...]
    d_all[i] = d_pre_b[...]
    for k in others:
        to = turn(i, k)
        send(d_pre_b, d_all.at[i], all_send, all_recv.at[i], batch=to)
        send(bias_all.at[i], bias_all.at[i], bias_send, bias_recv.at[i], batch=to)
    for m in others:
        slot = y * 4 + turn(z, m)
        place = hidden_all.at[:, lanes_of(slot)]
        arrived(place, h_recv.at[slot])
        for k in others:
            send(place, place, h_send, h_recv.at[slot], col=turn(y, k) * 4 + z)
    undo = ordering(128, 16)
    for half in range(2):
        d_y[half, y] = d_act[half, :, pl.ds(4 * y, 4)]
        for k in others:
            f = turn(y, k)
            arrived(d_y.at[half, f], dy_recv.at[half, f])
        for q in range(4):
            part = four([d_y[half, f, :, q].astype(f32) for f in range(4)])
            rows = contract_first(undo, part.reshape(128, 128).astype(bf16))
            for g in range(4):
                d_z_out[half, q * 4 + g] = (
                    rows[g * 32 : (g + 1) * 32].reshape(2, 16, 128).astype(bf16)
                )
        d_z[half, plane] = d_z_out[half, plane]

        def hand(k, _):
            peer = lax.rem(plane + k, 16)
            send(
                d_z_out.at[half, peer], d_z.at[half, plane], dz_send, dz_recv.at[half],
                col=y * 4 + peer // 4, row=lax.rem(peer, 4),
            )
            return 0

        lax.fori_loop(1, 16, hand, 0)
    for m in others:
        for k in range(4):
            slot = turn(y, m) * 4 + k
            arrived(hidden_all.at[:, lanes_of(slot)], h_recv.at[slot])
    for k in others:
        to = turn(i, k)
        send(
            hidden_all.at[:, lanes_of(to, 512)], own_hidden.at[i], oh_send, oh_recv.at[i],
            batch=to,
        )
    own_hidden[i] = hidden_all[:, lanes_of(i, 512)]
    mine.wait()
    for k in others:
        f = turn(i, k)
        arrived(d_all.at[f], all_recv.at[f])
        arrived(acts.at[f], acts_recv.at[f])
    for e in range(8):
        part = four([contract_first(acts[f, e].reshape(128, 128), d_all[f]) for f in range(4)])
        grad_in[i, e] = part.astype(bf16)
    send(grad_in.at[i], grad_in.at[i], in_send, in_recv.at[i], batch=sibling)
    send(grad_in.at[i], grad_in.at[i], in_send, in_recv.at[i], batch=across)
    for half in range(2):
        arrived(d_z.at[half, pl.ds(0, 15)], dz_recv.at[half])
    for s in range(2):
        grad = jnp.concatenate(
            [
                four([d_z[half, q * 4 + g, s].astype(f32) for q in range(4)])
                for g in range(4)
                for half in range(2)
            ],
            axis=0,
        )
        norm = normed[s]
        inner = whole_sum(grad * norm) / (512 * 32)
        d_inter = (inv[s, 0:1, :] * (grad - norm * inner)).astype(bf16).astype(f32)
        for j in range(4):
            folds[pl.ds(j, 128, stride=4), :] = jnp.where(block == j, d_inter, 0.0)
        own = sample(s)
        fold = dot(own, folds[...].astype(bf16))
        fold = fold + pltpu.roll(fold, 32, 1)
        fold = fold + pltpu.roll(fold, 64, 1)
        high, low = split(jnp.transpose(fold)[:32])
        both = dot(jnp.concatenate([high, low], axis=0), own)
        for q in range(4):
            part = both[:32, q * 128 : (q + 1) * 128] + both[32:, q * 128 : (q + 1) * 128]
            if s == 0:
                proj_out[q] = part
            else:
                proj_out[q] += part
    flat = y * 4 + r
    proj_x[flat] = proj_out[r]

    def hand_on(k, _):
        peer = lax.rem(flat + k, 16)
        to_r = lax.rem(peer, 4)
        send(
            proj_out.at[to_r], proj_x.at[flat], gx_send, gx_recv,
            col=peer // 4 * 4 + z, row=to_r,
        )
        return 0

    lax.fori_loop(1, 16, hand_on, 0)
    for d in range(8):
        stage[pl.ds(d, 128, stride=8), :] = dot(hidden_all[...], w_split[d])
    mixed[...] = stage[...].reshape(128, 8, 128).astype(bf16)
    arrived(proj_x.at[pl.ds(0, 15)], gx_recv)
    proj_z[z] = four([four([proj_x[q * 4 + g] for g in range(4)]) for q in range(4)])
    for k in others:
        send(proj_z.at[z], proj_z.at[z], gz_send, gz_recv.at[z], col=y * 4 + turn(z, k))
    arrived(grad_in.at[across], in_recv.at[across])
    send(grad_in.at[across], grad_in.at[across], in_send, in_recv.at[across], batch=sibling)
    for k in others:
        f = turn(i, k)
        arrived(own_hidden.at[f], oh_recv.at[f])
    arrived(every_cot.at[sibling], cot_recv.at[sibling])
    arrived(every_cot.at[diagonal], cot_recv.at[diagonal])
    for f in range(4):
        hidden_t[:, f * 128 : (f + 1) * 128] = jnp.transpose(own_hidden[f])

    def outer(d):
        cots = jnp.concatenate([every_cot[f, d] for f in range(4)], axis=0)
        grad_out[pl.ds(d, 512, stride=8), :] = dot(hidden_t[...], cots)

    for d in range(4):
        outer(d)
    for k in others:
        f = turn(z, k)
        arrived(proj_z.at[f], gz_recv.at[f])
    proj_b[i] = four(proj_z)
    for k in others:
        send(proj_b.at[i], proj_b.at[i], gb_send, gb_recv.at[i], batch=turn(i, k))
    for d in range(4, 8):
        outer(d)
    for k in others:
        f = turn(i, k)
        arrived(bias_all.at[f], bias_recv.at[f])
    grad_bias[...] = four(bias_all)
    for k in others:
        f = turn(i, k)
        arrived(proj_b.at[f], gb_recv.at[f])
    grad_proj[...] = four(proj_b)
    arrived(grad_in.at[sibling], in_recv.at[sibling])
    arrived(grad_in.at[diagonal], in_recv.at[diagonal])
    arrived(emb.at[pl.ds(0, 63)], emb_send)
    arrived(every_cot.at[three], cot_send)
    arrived(part_y.at[three], py_send)
    arrived(part_z.at[three], pz_send)
    arrived(part_x.at[three], px_send)
    arrived(raw.at[pl.ds(0, 15), 0], near_send)
    arrived(raw.at[pl.ds(0, 12)], far_send)
    arrived(pre_x.at[three], pre_send)
    arrived(hidden_all.at[:, pl.ds(0, 15 * 128)], h_send)
    arrived(own_hidden.at[three], oh_send)
    arrived(d_act.at[:, :, pl.ds(0, 12)], dy_send)
    arrived(d_z.at[:, pl.ds(0, 15)], dz_send)
    arrived(acts.at[three], acts_send)
    arrived(d_all.at[three], all_send)
    arrived(grad_in.at[three], in_send)
    arrived(bias_all.at[three], bias_send)
    arrived(proj_x.at[pl.ds(0, 15)], gx_send)
    arrived(proj_z.at[three], gz_send)
    arrived(proj_b.at[three], gb_send)


def everything(emb, proj, w_in, bias, w_out, cot):
    out = jax.ShapeDtypeStruct
    pair = [DMA, DMA((4,))]
    far = pl.BlockSpec(memory_space=pltpu.HBM)
    near = pl.BlockSpec(memory_space=VMEM)
    return pl.pallas_call(
        kernel,
        out_shape=(
            out((128, 8, 128), bf16),
            out((4096, 128), f32),
            out((4, 8, 128, 128), bf16),
            out((8, 128), f32),
            out((32, 128), f32),
        ),
        in_specs=[far, near, far, near, far, near],
        out_specs=[near] * 5,
        scratch_shapes=[
            VMEM((32, 128, 128), bf16),
            VMEM((2048, 8, 128), bf16),
            VMEM((8, 2048, 128), bf16),
            VMEM((1024, 128), f32),
            VMEM((4, 8, 128, 128), bf16),
            VMEM((4, 2, 16, 8, 128), bf16),
            VMEM((512, 128), f32),
            VMEM((2, 128, 128), f32),
            VMEM((2, 8, 128), f32),
            VMEM((4, 4, 128, 128), bf16),
            VMEM((4, 4, 128, 128), bf16),
            VMEM((4, 128, 128), bf16),
            VMEM((4, 128, 128), bf16),
            VMEM((4, 128, 128), f32),
            VMEM((4, 2, 32, 128), bf16),
            VMEM((16, 4, 2, 32, 128), bf16),
            VMEM((32, 16, 8, 128), bf16),
            VMEM((4, 128, 128), f32),
            VMEM((128, 128), bf16),
            VMEM((128, 128), bf16),
            VMEM((2, 16, 16, 8, 128), bf16),
            VMEM((2, 4, 16, 4, 8, 128), bf16),
            VMEM((2, 16, 2, 16, 128), bf16),
            VMEM((2, 16, 2, 16, 128), bf16),
            VMEM((4, 8, 16, 8, 128), bf16),
            VMEM((4, 128, 128), bf16),
            VMEM((4, 8, 128), f32),
            VMEM((128, 2048), bf16),
            VMEM((4, 128, 512), bf16),
            VMEM((512, 512), bf16),
            VMEM((4, 32, 128), f32),
            VMEM((16, 32, 128), f32),
            VMEM((4, 32, 128), f32),
            VMEM((4, 32, 128), f32),
            DMA, DMA, DMA, DMA, *pair,
            *pair, *pair, *pair,
            DMA, DMA, DMA((16,)), *pair,
            DMA, DMA((16,)), *pair, DMA, DMA((2, 4)), DMA, DMA((2,)),
            *pair, *pair, *pair, *pair,
            DMA, DMA, *pair, *pair, DMA,
        ],
        compiler_params=pltpu.CompilerParams(
            collective_id=0, has_side_effects=True, vmem_limit_bytes=49 << 20
        ),
        name="block",
    )(emb, proj, w_in, bias, w_out, cot)


def local(embeddings, projection, w_in, bias, w_out, cotangent):
    mixed, grad_out, grad_in, grad_bias, grad_proj = everything(
        embeddings.reshape(64, 2, 8, 128), projection.T, w_in.reshape(32, 128, 128),
        bias.reshape(1, 128), w_out, cotangent,
    )
    return (
        mixed, grad_out.reshape(512, 8, 128), grad_in.astype(f32).reshape(4096, 128),
        grad_bias[0], grad_proj.T,
    )


def solution(mesh):
    placed = (
        P("batch", "col", "row"),
        P(),
        P("row", "col"),
        P("col"),
        P(None, "col", "row"),
        P("batch", "col", "row"),
    )
    return jax.shard_map(
        local,
        mesh=mesh,
        in_specs=placed,
        out_specs=(
            P("batch", "col", "row"),
            P("batch", "col", "row"),
            P("row", "col"),
            P("col"),
            P("row", None),
        ),
        check_vma=False,
    )
```

time: 305 us -> 95.8 us (0.31)
  waiting for transfers between devices: 103 us -> 0 us
  starting transfers between devices: 96.8 us -> 0 us
  Pallas kernels: 0 us -> 85.7 us
  blocking collectives: 41.8 us -> 0 us
  local copies, waits for them, and re-layouts: 33.3 us -> 7.67 us
  matrix products: 15.3 us -> 0 us
  other arithmetic: 12 us -> 1.52 us
    all_to_all x15 -> x0, waiting for transfers between devices: 103 us -> none  [swap(): return lax.all_to_all(tiles, axis, 0, 0, tiled=True)]
    all_to_all x15 -> x0, starting transfers between devices: 96.8 us -> none  [swap(): return lax.all_to_all(tiles, axis, 0, 0, tiled=True)]
    pallas_call x0 -> x1, Pallas kernels: none -> 85.7 us  [everything(): pl.pallas_call(kernel, out_shape=(out((128, 8, 128), bf16), out((4096, 12...]
    all_to_all x2 -> x0, blocking collectives: 41.8 us -> none  [swap(): return lax.all_to_all(tiles, axis, 0, 0, tiled=True)]
    dot_general x10 -> x0, matrix products: 15.3 us -> none  [the longest x2 5.12 us: contract_last(): lax.dot_general(left, right, (((1,), (1,)), ((), ())), preferred_element_...]
    reshape x9 -> x0, local copies, waits for them, and re-layouts: 9.99 us -> none  [the longest x3 4.49 us: local(): d_act = jnp.moveaxis(d_act, 0, 1).reshape(own, rows * embs, rank)]
    reduce_sum x10 -> x0, other arithmetic: 8.8 us -> none  [the longest x3 2.36 us: summed(): return jnp.sum(tiles.astype(f32), axis=0)]
    broadcast_in_dim x9 -> x0, local copies, waits for them, and re-layouts: 6.92 us -> none  [everyone(): return swap(jnp.broadcast_to(array[None], (size, *array.shape)), axis)]
  transfers between devices with their start and end apart: 15 -> 0, of which waited for: 12 -> 0; matrix products, arithmetic and copies ran while one was open for 16% -> 0% of each run, Pallas kernels for 0% -> 0%
where the time goes in v4:
time: 95.8 us; the launch traced here: 95.5 us
  Pallas kernels  85.7 us (89%)
  local copies, waits for them, and re-layouts  7.67 us (8%)
  other arithmetic  1.52 us (2%)
    pallas_call x1, Pallas kernels, everything(): pl.pallas_call(kernel, out_shape=(out((128, 8, 128), bf16), out((4096, 12...  85.7 us
    unnamed x13, local copies, waits for them, and re-layouts  7.15 us

profile of v4, /device:TPU:1, one launch (start us, length us, event | category | flops | bytes accessed | tf_op | source)
XLA Modules:
  0.0 95.5 jit_solution(13452358551756930496)
XLA Ops:
  0.6 0.0 copy-start
  0.6 1.2 %copy-done = bf16[4096,128]{1,0:T(8,128)(2,1)S(1)} copy-done((bf16[4096,128]{1,0:T(8,128)(2,1)S(1)}, bf16[4096,128]{1,0:T(8,128)(2,1)}, u32[]{:S(2)}) %copy-start) | copy-done | bytes 1048600
  1.9 0.0 copy-start.1
  1.9 0.9 copy-done.1
  2.8 0.0 copy-start.2
  2.8 0.9 copy-done.2
  3.8 0.0 copy-start.3
  3.8 0.8 copy-done.3
  4.5 0.0 copy-start.4
  4.5 0.7 copy-done.4
  5.2 85.7 %block.1 = (bf16[128,8,128]{2,1,0:T(8,128)(2,1)S(1)}, f32[4096,128]{1,0:T(8,128)S(1)}, bf16[4,8,128,128]{3,2,1,0:T(8,128)(2,1)S(1)}, f32[8,128]{1,0:T(8,128)S(1)}, f32[32,128]{1,0:T(8,128)S(1)}) custom-call(bf16[64,2,8,128]{3,2,1,0:T(8,128)(2,1)S(1)} %bitcast.13, bf16[32,512]{1,0:T(8,128)(2,1)S(1)} %bitcast.14, bf16[32,128,128]{2,1,0:T(8,128)(2,1)S(1)} %bitcast.12, ...), custom_call_target="tpu_custom_call" | custom-call | tf_op jit(solution)/shard_map/block/pallas_call | solution.py:433
  90.9 0.5 slice_bitcast_fusion
  91.4 1.5 %bitcast_convert_fusion = f32[4096,128]{1,0:T(8,128)} fusion(bf16[4,8,128,128]{3,2,1,0:T(8,128)(2,1)S(1)} %get-tuple-element.12), kind=kLoop, calls=%fused_computation | loop fusion | flops 524288 | bytes 3145728 | tf_op jit(solution)/shard_map/reshape | solution.py:499
  92.9 0.7 copy.14
  93.6 1.3 %copy.15 = f32[512,8,128]{2,1,0:T(8,128)} copy(f32[512,8,128]{2,1,0:T(8,128)S(1)} %bitcast.11) | data formatting | bytes 4194304
  94.9 0.6 copy.16
Async XLA Ops:
  0.6 1.2 %copy-start = (bf16[4096,128]{1,0:T(8,128)(2,1)S(1)}, bf16[4096,128]{1,0:T(8,128)(2,1)}, u32[]{:S(2)}) copy-start(bf16[4096,128]{1,0:T(8,128)(2,1)} %param.8) | copy-start | bytes 3145732
  1.9 0.9 copy-start.1
  2.8 0.9 copy-start.2
  3.8 0.8 copy-start.3
  4.5 0.7 copy-start.4

commit v5 on v4

--- a/solution.py
+++ b/solution.py
@@ -67,19 +67,19 @@
 
 
 def kernel(
-    emb, proj, w_in_far, bias, w_out_far, cot,
+    emb, proj_far, w_in_far, bias_far, w_out_far, cot_far,
     mixed, grad_out, grad_in, grad_bias, grad_proj,
-    w_in, w_out, w_split, stage, every_cot, own_emb, folds, normed, inv,
+    proj, w_in, bias, w_out, cot, w_split, stage, every_cot, own_emb, folds, normed, inv,
     part_out, part_y, part_z_out, part_z, part_x,
     to_row, raw, gathered, pre_x, hidden, d_pre_b,
-    d_act, d_y, d_z_out, d_z, acts, d_all, bias_all, hidden_all, own_hidden, hidden_t,
+    d_act, d_y, d_z_out, d_z, in_part, in_near, in_both, bias_all, hidden_all, own_hidden, hidden_t,
     proj_out, proj_x, proj_z, proj_b,
-    load_in, load_out, emb_send, emb_recv, cot_send, cot_recv,
+    load_in, load_out, load_cot, load_proj, load_bias, emb_send, emb_recv, cot_send, cot_recv,
     py_send, py_recv, pz_send, pz_recv, px_send, px_recv,
     near_send, far_send, raw_recv, pre_send, pre_recv,
     h_send, h_recv, oh_send, oh_recv, dy_send, dy_recv, dz_send, dz_recv,
-    acts_send, acts_recv, all_send, all_recv, in_send, in_recv, bias_send, bias_recv,
-    gx_send, gx_recv, gz_send, gz_recv, gb_send, gb_recv, own_sem,
+    near_in_send, near_in_recv, both_send, both_recv, in_send, in_recv, bias_send, bias_recv,
+    gx_send, gx_recv, gz_send, gz_recv, gb_send, gb_recv,
 ):
     i = lax.axis_index("batch")
     r = lax.axis_index("row")
@@ -104,13 +104,48 @@
     lax.fori_loop(1, 64, greet, 0)
     for k in others:
         pl.semaphore_signal(barrier, inc=1, device_id={"batch": turn(i, k)}, device_id_type=MESH)
-    take_out = pltpu.make_async_copy(w_out_far, w_out, load_out)
-    take_out.start()
+    take_cot = pltpu.make_async_copy(cot_far, cot, load_cot)
+    take_cot.start()
+    take_out = []
+    for k in (1, 2, 3, 0):
+        at = lanes_of(turn(y, k), 512)
+        take_out.append(pltpu.make_async_copy(w_out_far.at[at], w_out.at[at], load_out.at[k]))
+        take_out[-1].start()
+    take_proj = pltpu.make_async_copy(proj_far, proj, load_proj)
+    take_proj.start()
+    take_bias = pltpu.make_async_copy(bias_far, bias, load_bias)
+    take_bias.start()
     take_in = pltpu.make_async_copy(w_in_far, w_in, load_in)
     take_in.start()
+    take_cot.wait()
     stage[...] = cot[...].astype(f32).reshape(1024, 128)
     for d in range(8):
         every_cot[i, d] = stage[pl.ds(d, 128, stride=8), :].astype(bf16)
+
+    def from_output(k):
+        to = turn(y, k)
+
+        def divide(n, _):
+            at = pl.multiple_of(to * 512 + n * 128, 128)
+            stage[...] = w_out[pl.ds(at, 128)].astype(f32).reshape(1024, 128)
+            for d in range(8):
+                w_split[d, pl.ds(at, 128), :] = stage[pl.ds(d, 128, stride=8), :].astype(bf16)
+            return 0
+
+        lax.fori_loop(0, 4, divide, 0)
+        part = jnp.zeros((128, 512), f32)
+        for d in range(8):
+            part = part + contract_last(every_cot[i, d], w_split[d, lanes_of(to, 512), :])
+        for q in range(4):
+            part_out[to, q] = part[:, q * 128 : (q + 1) * 128].astype(bf16)
+
+    def share_output(k):
+        to = turn(y, k)
+        send(part_out.at[to], part_y.at[y], py_send, py_recv.at[y], col=to * 4 + z)
+
+    for n in (0, 1):
+        take_out[n].wait()
+        from_output(n + 1)
     pl.semaphore_wait(barrier, 66)
 
     keep = pltpu.make_async_copy(emb.at[me], own_emb.at[r, :, c], emb_recv)
@@ -125,29 +160,16 @@
         return 0
 
     lax.fori_loop(1, 64, give, 0)
-
-    take_out.wait()
-    for k in (1, 2, 3, 0):
-        to = turn(y, k)
-
-        def divide(n, _):
-            at = pl.multiple_of(to * 512 + n * 128, 128)
-            stage[...] = w_out[pl.ds(at, 128)].astype(f32).reshape(1024, 128)
-            for d in range(8):
-                w_split[d, pl.ds(at, 128), :] = stage[pl.ds(d, 128, stride=8), :].astype(bf16)
-            return 0
-
-        lax.fori_loop(0, 4, divide, 0)
-        part = jnp.zeros((128, 512), f32)
-        for d in range(8):
-            part = part + contract_last(every_cot[i, d], w_split[d, lanes_of(to, 512), :])
-        for q in range(4):
-            part_out[to, q] = part[:, q * 128 : (q + 1) * 128].astype(bf16)
-        if k:
-            send(part_out.at[to], part_y.at[y], py_send, py_recv.at[y], col=to * 4 + z)
-        else:
-            part_y[y] = part_out[y]
-
+    share_output(1)
+    share_output(2)
+    take_out[2].wait()
+    from_output(3)
+    share_output(3)
+    take_out[3].wait()
+    from_output(0)
+    part_y[y] = part_out[y]
+    take_proj.wait()
+    take_bias.wait()
     lanes = lax.broadcasted_iota(jnp.int32, (32, 128), 1)
     ranks = lax.broadcasted_iota(jnp.int32, (32, 128), 0)
     repeat = (lax.rem(lanes, 32) == ranks).astype(f32).astype(bf16)
@@ -198,7 +220,7 @@
     arrived(raw.at[c, three], raw_recv.at[c])
     for k in others:
         send(raw.at[c], raw.at[c], far_send, raw_recv.at[c], col=turn(y, k) * 4 + z)
-    for m in others:
+    for m in (1, 3, 2):
         slot = y * 4 + turn(z, m)
         arrived(raw.at[slot], raw_recv.at[slot])
         for k in others:
@@ -231,13 +253,6 @@
     for k in others:
         send(pre_x.at[r], pre_x.at[r], pre_send, pre_recv.at[r], row=turn(r, k))
     for k in others:
-        to = turn(i, k)
-        send(gathered.at[pl.ds(8 * to, 8)], acts.at[i], acts_send, acts_recv.at[i], batch=to)
-    mine = pltpu.make_async_copy(gathered.at[pl.ds(8 * i, 8)], acts.at[i], own_sem)
-    mine.start()
-    arrived(every_cot.at[across], cot_recv.at[across])
-    send(every_cot.at[across], every_cot.at[across], cot_send, cot_recv.at[across], batch=sibling)
-    for k in others:
         f = turn(r, k)
         arrived(part_x.at[f], px_recv.at[f])
     d_hidden = four(part_x)
@@ -253,9 +268,9 @@
 
     for k in others:
         send(hidden, hidden_all.at[:, lanes_of(c)], h_send, h_recv.at[c], col=y * 4 + turn(z, k))
-    for half in range(2):
-        for e in range(16):
-            part = contract_last(d_pre_b[...], w_in[half * 16 + e])
+    for half in range(4):
+        for e in range(8):
+            part = contract_last(d_pre_b[...], w_in[half * 8 + e])
             d_act[half, e] = part.reshape(16, 8, 128).astype(bf16)
         for k in others:
             to = turn(y, k)
@@ -266,29 +281,35 @@
     for k in others:
         send(hidden, hidden_all.at[:, lanes_of(c)], h_send, h_recv.at[c], col=turn(y, k) * 4 + z)
     hidden_all[:, lanes_of(c)] = hidden[...]
-    d_all[i] = d_pre_b[...]
     for k in others:
         to = turn(i, k)
-        send(d_pre_b, d_all.at[i], all_send, all_recv.at[i], batch=to)
         send(bias_all.at[i], bias_all.at[i], bias_send, bias_recv.at[i], batch=to)
-    for m in others:
+    arrived(every_cot.at[across], cot_recv.at[across])
+    send(every_cot.at[across], every_cot.at[across], cot_send, cot_recv.at[across], batch=sibling)
+    core = lax.rem(i, 2)
+    chip = i // 2
+    for h in range(2):
+        for e in range(16):
+            in_part[h, e] = contract_first(gathered[h * 16 + e].reshape(128, 128), d_pre_b[...])
+    send(in_part.at[1 - core], in_near, near_in_send, near_in_recv, batch=sibling)
+    for m in (1, 3, 2):
         slot = y * 4 + turn(z, m)
         place = hidden_all.at[:, lanes_of(slot)]
         arrived(place, h_recv.at[slot])
         for k in others:
             send(place, place, h_send, h_recv.at[slot], col=turn(y, k) * 4 + z)
-    undo = ordering(128, 16)
-    for half in range(2):
+    undo = ordering(64, 8)
+    for half in range(4):
         d_y[half, y] = d_act[half, :, pl.ds(4 * y, 4)]
         for k in others:
             f = turn(y, k)
             arrived(d_y.at[half, f], dy_recv.at[half, f])
         for q in range(4):
             part = four([d_y[half, f, :, q].astype(f32) for f in range(4)])
-            rows = contract_first(undo, part.reshape(128, 128).astype(bf16))
+            rows = contract_first(undo, part.reshape(64, 128).astype(bf16))
             for g in range(4):
                 d_z_out[half, q * 4 + g] = (
-                    rows[g * 32 : (g + 1) * 32].reshape(2, 16, 128).astype(bf16)
+                    rows[g * 16 : (g + 1) * 16].reshape(2, 8, 128).astype(bf16)
                 )
         d_z[half, plane] = d_z_out[half, plane]
 
@@ -301,6 +322,10 @@
             return 0
 
         lax.fori_loop(1, 16, hand, 0)
+        if half == 0:
+            arrived(in_near, near_in_recv)
+            in_both[chip] = (in_part[core] + in_near[...]).astype(bf16)
+            send(in_both.at[chip], in_both.at[chip], both_send, both_recv, batch=across)
     for m in others:
         for k in range(4):
             slot = turn(y, m) * 4 + k
@@ -312,24 +337,14 @@
             batch=to,
         )
     own_hidden[i] = hidden_all[:, lanes_of(i, 512)]
-    mine.wait()
-    for k in others:
-        f = turn(i, k)
-        arrived(d_all.at[f], all_recv.at[f])
-        arrived(acts.at[f], acts_recv.at[f])
-    for e in range(8):
-        part = four([contract_first(acts[f, e].reshape(128, 128), d_all[f]) for f in range(4)])
-        grad_in[i, e] = part.astype(bf16)
-    send(grad_in.at[i], grad_in.at[i], in_send, in_recv.at[i], batch=sibling)
-    send(grad_in.at[i], grad_in.at[i], in_send, in_recv.at[i], batch=across)
-    for half in range(2):
+    for half in range(4):
         arrived(d_z.at[half, pl.ds(0, 15)], dz_recv.at[half])
     for s in range(2):
         grad = jnp.concatenate(
             [
                 four([d_z[half, q * 4 + g, s].astype(f32) for q in range(4)])
                 for g in range(4)
-                for half in range(2)
+                for half in range(4)
             ],
             axis=0,
         )
@@ -370,8 +385,9 @@
     proj_z[z] = four([four([proj_x[q * 4 + g] for g in range(4)]) for q in range(4)])
     for k in others:
         send(proj_z.at[z], proj_z.at[z], gz_send, gz_recv.at[z], col=y * 4 + turn(z, k))
-    arrived(grad_in.at[across], in_recv.at[across])
-    send(grad_in.at[across], grad_in.at[across], in_send, in_recv.at[across], batch=sibling)
+    arrived(in_both.at[1 - chip], both_recv)
+    grad_in[core] = in_both[0].astype(f32) + in_both[1].astype(f32)
+    send(grad_in.at[core], grad_in.at[core], in_send, in_recv, batch=sibling)
     for k in others:
         f = turn(i, k)
         arrived(own_hidden.at[f], oh_recv.at[f])
@@ -402,8 +418,7 @@
         f = turn(i, k)
         arrived(proj_b.at[f], gb_recv.at[f])
     grad_proj[...] = four(proj_b)
-    arrived(grad_in.at[sibling], in_recv.at[sibling])
-    arrived(grad_in.at[diagonal], in_recv.at[diagonal])
+    arrived(grad_in.at[1 - core], in_recv)
     arrived(emb.at[pl.ds(0, 63)], emb_send)
     arrived(every_cot.at[three], cot_send)
     arrived(part_y.at[three], py_send)
@@ -416,9 +431,9 @@
     arrived(own_hidden.at[three], oh_send)
     arrived(d_act.at[:, :, pl.ds(0, 12)], dy_send)
     arrived(d_z.at[:, pl.ds(0, 15)], dz_send)
-    arrived(acts.at[three], acts_send)
-    arrived(d_all.at[three], all_send)
-    arrived(grad_in.at[three], in_send)
+    arrived(in_near, near_in_send)
+    arrived(in_both.at[chip], both_send)
+    arrived(grad_in.at[core], in_send)
     arrived(bias_all.at[three], bias_send)
     arrived(proj_x.at[pl.ds(0, 15)], gx_send)
     arrived(proj_z.at[three], gz_send)
@@ -435,15 +450,18 @@
         out_shape=(
             out((128, 8, 128), bf16),
             out((4096, 128), f32),
-            out((4, 8, 128, 128), bf16),
+            out((2, 16, 128, 128), f32),
             out((8, 128), f32),
             out((32, 128), f32),
         ),
-        in_specs=[far, near, far, near, far, near],
+        in_specs=[far] * 6,
         out_specs=[near] * 5,
         scratch_shapes=[
+            VMEM((32, 512), bf16),
             VMEM((32, 128, 128), bf16),
+            VMEM((1, 128), f32),
             VMEM((2048, 8, 128), bf16),
+            VMEM((128, 8, 128), bf16),
             VMEM((8, 2048, 128), bf16),
             VMEM((1024, 128), f32),
             VMEM((4, 8, 128, 128), bf16),
@@ -462,12 +480,13 @@
             VMEM((4, 128, 128), f32),
             VMEM((128, 128), bf16),
             VMEM((128, 128), bf16),
-            VMEM((2, 16, 16, 8, 128), bf16),
-            VMEM((2, 4, 16, 4, 8, 128), bf16),
-            VMEM((2, 16, 2, 16, 128), bf16),
-            VMEM((2, 16, 2, 16, 128), bf16),
             VMEM((4, 8, 16, 8, 128), bf16),
-            VMEM((4, 128, 128), bf16),
+            VMEM((4, 4, 8, 4, 8, 128), bf16),
+            VMEM((4, 16, 2, 8, 128), bf16),
+            VMEM((4, 16, 2, 8, 128), bf16),
+            VMEM((2, 16, 128, 128), f32),
+            VMEM((16, 128, 128), f32),
+            VMEM((2, 16, 128, 128), bf16),
             VMEM((4, 8, 128), f32),
             VMEM((128, 2048), bf16),
             VMEM((4, 128, 512), bf16),
@@ -476,18 +495,18 @@
             VMEM((16, 32, 128), f32),
             VMEM((4, 32, 128), f32),
             VMEM((4, 32, 128), f32),
-            DMA, DMA, DMA, DMA, *pair,
+            DMA, DMA((4,)), DMA, DMA, DMA, DMA, DMA, *pair,
             *pair, *pair, *pair,
             DMA, DMA, DMA((16,)), *pair,
-            DMA, DMA((16,)), *pair, DMA, DMA((2, 4)), DMA, DMA((2,)),
-            *pair, *pair, *pair, *pair,
-            DMA, DMA, *pair, *pair, DMA,
+            DMA, DMA((16,)), *pair, DMA, DMA((4, 4)), DMA, DMA((4,)),
+            DMA, DMA, DMA, DMA, DMA, DMA, *pair,
+            DMA, DMA, *pair, *pair,
         ],
         compiler_params=pltpu.CompilerParams(
             collective_id=0, has_side_effects=True, vmem_limit_bytes=49 << 20
         ),
         name="block",
-    )(emb, proj, w_in, bias, w_out, cot)
+    )(*[pltpu.with_memory_space_constraint(a, pltpu.HBM) for a in (emb, proj, w_in, bias, w_out, cot)])
 
 
 def local(embeddings, projection, w_in, bias, w_out, cotangent):
@@ -496,7 +515,7 @@
         bias.reshape(1, 128), w_out, cotangent,
     )
     return (
-        mixed, grad_out.reshape(512, 8, 128), grad_in.astype(f32).reshape(4096, 128),
+        mixed, grad_out.reshape(512, 8, 128), grad_in.reshape(4096, 128),
         grad_bias[0], grad_proj.T,
     )
 

time: 95.8 us -> 97.6 us (1.019)
  Pallas kernels: 85.7 us -> 92.4 us
  local copies, waits for them, and re-layouts: 7.67 us -> 4.46 us
  other arithmetic: 1.52 us -> 0 us
    pallas_call x1, Pallas kernels: 85.7 us -> 92.4 us  [everything(): pl.pallas_call(kernel, out_shape=(out((128, 8, 128), bf16), out((4096, 12...]
    unnamed x13 -> x4, local copies, waits for them, and re-layouts: 7.15 us -> 3.94 us
    reshape x1 -> x0, other arithmetic: 1.52 us -> none  [local(): grad_in.astype(f32).reshape(4096, 128)]
where the time goes in v5:
time: 97.6 us; the launch traced here: 97.5 us
  Pallas kernels  92.4 us (95%)
  local copies, waits for them, and re-layouts  4.46 us (5%)
    pallas_call x1, Pallas kernels, everything(): pl.pallas_call(kernel, out_shape=(out((128, 8, 128), bf16), out((4096, 12...  92.4 us
    unnamed x4, local copies, waits for them, and re-layouts  3.94 us

profile of v5, /device:TPU:1, one launch (start us, length us, event | category | flops | bytes accessed | tf_op | source)
XLA Modules:
  0.0 97.5 jit_solution(17195089154946972220)
XLA Ops:
  0.6 92.4 %block.1 = (bf16[128,8,128]{2,1,0:T(8,128)(2,1)S(1)}, f32[4096,128]{1,0:T(8,128)S(1)}, f32[2,16,128,128]{3,2,1,0:T(8,128)S(1)}, f32[8,128]{1,0:T(8,128)S(1)}, f32[32,128]{1,0:T(8,128)S(1)}) custom-call(bf16[64,2,8,128]{3,2,1,0:T(8,128)(2,1)} %bitcast.13, bf16[32,512]{1,0:T(8,128)(2,1)} %bitcast.14, bf16[32,128,128]{2,1,0:T(8,128)(2,1)} %bitcast.12, ...), custom_call_target="tpu_custom_call" | custom-call | tf_op jit(solution)/shard_map/block/pallas_call | solution.py:448
  93.0 0.5 slice_bitcast_fusion
  93.5 0.7 copy.15
  94.2 1.3 %copy.16 = f32[512,8,128]{2,1,0:T(8,128)} copy(f32[512,8,128]{2,1,0:T(8,128)S(1)} %bitcast.10) | data formatting | bytes 4194304
  95.6 1.3 %copy.17 = f32[4096,128]{1,0:T(8,128)} copy(f32[4096,128]{1,0:T(8,128)S(1)} %bitcast.9) | data formatting | bytes 4194304
  96.9 0.6 copy.18

commit v6 on v4

--- a/solution.py
+++ b/solution.py
@@ -67,14 +67,14 @@
 
 
 def kernel(
-    emb, proj, w_in_far, bias, w_out_far, cot,
+    emb, proj_far, w_in_far, bias_far, w_out_far, cot_far,
     mixed, grad_out, grad_in, grad_bias, grad_proj,
-    w_in, w_out, w_split, stage, every_cot, own_emb, folds, normed, inv,
+    proj, w_in, bias, w_out, cot, w_split, stage, every_cot, own_emb, folds, normed, inv,
     part_out, part_y, part_z_out, part_z, part_x,
     to_row, raw, gathered, pre_x, hidden, d_pre_b,
     d_act, d_y, d_z_out, d_z, acts, d_all, bias_all, hidden_all, own_hidden, hidden_t,
     proj_out, proj_x, proj_z, proj_b,
-    load_in, load_out, emb_send, emb_recv, cot_send, cot_recv,
+    load_in, load_out, load_cot, load_proj, load_bias, emb_send, emb_recv, cot_send, cot_recv,
     py_send, py_recv, pz_send, pz_recv, px_send, px_recv,
     near_send, far_send, raw_recv, pre_send, pre_recv,
     h_send, h_recv, oh_send, oh_recv, dy_send, dy_recv, dz_send, dz_recv,
@@ -104,13 +104,48 @@
     lax.fori_loop(1, 64, greet, 0)
     for k in others:
         pl.semaphore_signal(barrier, inc=1, device_id={"batch": turn(i, k)}, device_id_type=MESH)
-    take_out = pltpu.make_async_copy(w_out_far, w_out, load_out)
-    take_out.start()
+    take_cot = pltpu.make_async_copy(cot_far, cot, load_cot)
+    take_cot.start()
+    take_out = []
+    for k in (1, 2, 3, 0):
+        at = lanes_of(turn(y, k), 512)
+        take_out.append(pltpu.make_async_copy(w_out_far.at[at], w_out.at[at], load_out.at[k]))
+        take_out[-1].start()
+    take_proj = pltpu.make_async_copy(proj_far, proj, load_proj)
+    take_proj.start()
+    take_bias = pltpu.make_async_copy(bias_far, bias, load_bias)
+    take_bias.start()
     take_in = pltpu.make_async_copy(w_in_far, w_in, load_in)
     take_in.start()
+    take_cot.wait()
     stage[...] = cot[...].astype(f32).reshape(1024, 128)
     for d in range(8):
         every_cot[i, d] = stage[pl.ds(d, 128, stride=8), :].astype(bf16)
+
+    def from_output(k):
+        to = turn(y, k)
+
+        def divide(n, _):
+            at = pl.multiple_of(to * 512 + n * 128, 128)
+            stage[...] = w_out[pl.ds(at, 128)].astype(f32).reshape(1024, 128)
+            for d in range(8):
+                w_split[d, pl.ds(at, 128), :] = stage[pl.ds(d, 128, stride=8), :].astype(bf16)
+            return 0
+
+        lax.fori_loop(0, 4, divide, 0)
+        part = jnp.zeros((128, 512), f32)
+        for d in range(8):
+            part = part + contract_last(every_cot[i, d], w_split[d, lanes_of(to, 512), :])
+        for q in range(4):
+            part_out[to, q] = part[:, q * 128 : (q + 1) * 128].astype(bf16)
+
+    def share_output(k):
+        to = turn(y, k)
+        send(part_out.at[to], part_y.at[y], py_send, py_recv.at[y], col=to * 4 + z)
+
+    for n in (0, 1):
+        take_out[n].wait()
+        from_output(n + 1)
     pl.semaphore_wait(barrier, 66)
 
     keep = pltpu.make_async_copy(emb.at[me], own_emb.at[r, :, c], emb_recv)
@@ -125,29 +160,16 @@
         return 0
 
     lax.fori_loop(1, 64, give, 0)
-
-    take_out.wait()
-    for k in (1, 2, 3, 0):
-        to = turn(y, k)
-
-        def divide(n, _):
-            at = pl.multiple_of(to * 512 + n * 128, 128)
-            stage[...] = w_out[pl.ds(at, 128)].astype(f32).reshape(1024, 128)
-            for d in range(8):
-                w_split[d, pl.ds(at, 128), :] = stage[pl.ds(d, 128, stride=8), :].astype(bf16)
-            return 0
-
-        lax.fori_loop(0, 4, divide, 0)
-        part = jnp.zeros((128, 512), f32)
-        for d in range(8):
-            part = part + contract_last(every_cot[i, d], w_split[d, lanes_of(to, 512), :])
-        for q in range(4):
-            part_out[to, q] = part[:, q * 128 : (q + 1) * 128].astype(bf16)
-        if k:
-            send(part_out.at[to], part_y.at[y], py_send, py_recv.at[y], col=to * 4 + z)
-        else:
-            part_y[y] = part_out[y]
-
+    share_output(1)
+    share_output(2)
+    take_out[2].wait()
+    from_output(3)
+    share_output(3)
+    take_out[3].wait()
+    from_output(0)
+    part_y[y] = part_out[y]
+    take_proj.wait()
+    take_bias.wait()
     lanes = lax.broadcasted_iota(jnp.int32, (32, 128), 1)
     ranks = lax.broadcasted_iota(jnp.int32, (32, 128), 0)
     repeat = (lax.rem(lanes, 32) == ranks).astype(f32).astype(bf16)
@@ -198,7 +220,7 @@
     arrived(raw.at[c, three], raw_recv.at[c])
     for k in others:
         send(raw.at[c], raw.at[c], far_send, raw_recv.at[c], col=turn(y, k) * 4 + z)
-    for m in others:
+    for m in (1, 3, 2):
         slot = y * 4 + turn(z, m)
         arrived(raw.at[slot], raw_recv.at[slot])
         for k in others:
@@ -235,8 +257,6 @@
         send(gathered.at[pl.ds(8 * to, 8)], acts.at[i], acts_send, acts_recv.at[i], batch=to)
     mine = pltpu.make_async_copy(gathered.at[pl.ds(8 * i, 8)], acts.at[i], own_sem)
     mine.start()
-    arrived(every_cot.at[across], cot_recv.at[across])
-    send(every_cot.at[across], every_cot.at[across], cot_send, cot_recv.at[across], batch=sibling)
     for k in others:
         f = turn(r, k)
         arrived(part_x.at[f], px_recv.at[f])
@@ -277,6 +297,8 @@
         arrived(place, h_recv.at[slot])
         for k in others:
             send(place, place, h_send, h_recv.at[slot], col=turn(y, k) * 4 + z)
+    arrived(every_cot.at[across], cot_recv.at[across])
+    send(every_cot.at[across], every_cot.at[across], cot_send, cot_recv.at[across], batch=sibling)
     undo = ordering(128, 16)
     for half in range(2):
         d_y[half, y] = d_act[half, :, pl.ds(4 * y, 4)]
@@ -439,11 +461,14 @@
             out((8, 128), f32),
             out((32, 128), f32),
         ),
-        in_specs=[far, near, far, near, far, near],
+        in_specs=[far] * 6,
         out_specs=[near] * 5,
         scratch_shapes=[
+            VMEM((32, 512), bf16),
             VMEM((32, 128, 128), bf16),
+            VMEM((1, 128), f32),
             VMEM((2048, 8, 128), bf16),
+            VMEM((128, 8, 128), bf16),
             VMEM((8, 2048, 128), bf16),
             VMEM((1024, 128), f32),
             VMEM((4, 8, 128, 128), bf16),
@@ -476,7 +501,7 @@
             VMEM((16, 32, 128), f32),
             VMEM((4, 32, 128), f32),
             VMEM((4, 32, 128), f32),
-            DMA, DMA, DMA, DMA, *pair,
+            DMA, DMA((4,)), DMA, DMA, DMA, DMA, DMA, *pair,
             *pair, *pair, *pair,
             DMA, DMA, DMA((16,)), *pair,
             DMA, DMA((16,)), *pair, DMA, DMA((2, 4)), DMA, DMA((2,)),
@@ -487,7 +512,7 @@
             collective_id=0, has_side_effects=True, vmem_limit_bytes=49 << 20
         ),
         name="block",
-    )(emb, proj, w_in, bias, w_out, cot)
+    )(*[pltpu.with_memory_space_constraint(a, pltpu.HBM) for a in (emb, proj, w_in, bias, w_out, cot)])
 
 
 def local(embeddings, projection, w_in, bias, w_out, cotangent):

time: 95.8 us -> 92.7 us (0.968)
  local copies, waits for them, and re-layouts: 7.67 us -> 3.14 us
  Pallas kernels: 85.7 us -> 87.3 us
    unnamed x13 -> x3, local copies, waits for them, and re-layouts: 7.15 us -> 2.63 us
    pallas_call x1, Pallas kernels: 85.7 us -> 87.3 us  [everything(): pl.pallas_call(kernel, out_shape=(out((128, 8, 128), bf16), out((4096, 12...]
where the time goes in v6:
time: 92.7 us; the launch traced here: 92.6 us
  Pallas kernels  87.3 us (94%)
  local copies, waits for them, and re-layouts  3.14 us (3%)
  other arithmetic  1.52 us (2%)
    pallas_call x1, Pallas kernels, everything(): pl.pallas_call(kernel, out_shape=(out((128, 8, 128), bf16), out((4096, 12...  87.3 us
    unnamed x3, local copies, waits for them, and re-layouts  2.63 us

profile of v6, /device:TPU:1, one launch (start us, length us, event | category | flops | bytes accessed | tf_op | source)
XLA Modules:
  0.0 92.6 jit_solution(1682927535121310610)
XLA Ops:
  0.6 87.3 %block.1 = (bf16[128,8,128]{2,1,0:T(8,128)(2,1)S(1)}, f32[4096,128]{1,0:T(8,128)S(1)}, bf16[4,8,128,128]{3,2,1,0:T(8,128)(2,1)S(1)}, f32[8,128]{1,0:T(8,128)S(1)}, f32[32,128]{1,0:T(8,128)S(1)}) custom-call(bf16[64,2,8,128]{3,2,1,0:T(8,128)(2,1)} %bitcast.14, bf16[32,512]{1,0:T(8,128)(2,1)} %bitcast.15, bf16[32,128,128]{2,1,0:T(8,128)(2,1)} %bitcast.13, ...), custom_call_target="tpu_custom_call" | custom-call | tf_op jit(solution)/shard_map/block/pallas_call | solution.py:455
  88.0 0.5 slice_bitcast_fusion
  88.5 1.5 %bitcast_convert_fusion = f32[4096,128]{1,0:T(8,128)} fusion(bf16[4,8,128,128]{3,2,1,0:T(8,128)(2,1)S(1)} %get-tuple-element.12), kind=kLoop, calls=%fused_computation | loop fusion | flops 524288 | bytes 3145728 | tf_op jit(solution)/shard_map/reshape | solution.py:524
  90.0 0.7 copy.14
  90.7 1.3 %copy.15 = f32[512,8,128]{2,1,0:T(8,128)} copy(f32[512,8,128]{2,1,0:T(8,128)S(1)} %bitcast.11) | data formatting | bytes 4194304
  92.0 0.6 copy.16

commit v7 on v6

--- a/solution.py
+++ b/solution.py
@@ -12,6 +12,7 @@
 VMEM = pltpu.VMEM
 DMA = pltpu.SemaphoreType.DMA
 others = (1, 2, 3)
+pieces = ((0, 16), (16, 16))
 
 
 def contract_last(left, right):
@@ -72,7 +73,7 @@
     proj, w_in, bias, w_out, cot, w_split, stage, every_cot, own_emb, folds, normed, inv,
     part_out, part_y, part_z_out, part_z, part_x,
     to_row, raw, gathered, pre_x, hidden, d_pre_b,
-    d_act, d_y, d_z_out, d_z, acts, d_all, bias_all, hidden_all, own_hidden, hidden_t,
+    d_act, d_y, z_out, z_in, acts, d_all, bias_all, hidden_all, own_hidden, hidden_t,
     proj_out, proj_x, proj_z, proj_b,
     load_in, load_out, load_cot, load_proj, load_bias, emb_send, emb_recv, cot_send, cot_recv,
     py_send, py_recv, pz_send, pz_recv, px_send, px_recv,
@@ -273,15 +274,16 @@
 
     for k in others:
         send(hidden, hidden_all.at[:, lanes_of(c)], h_send, h_recv.at[c], col=y * 4 + turn(z, k))
-    for half in range(2):
-        for e in range(16):
-            part = contract_last(d_pre_b[...], w_in[half * 16 + e])
-            d_act[half, e] = part.reshape(16, 8, 128).astype(bf16)
+    for n, (first, size) in enumerate(pieces):
+        for e in range(first, first + size):
+            part = contract_last(d_pre_b[...], w_in[e])
+            d_act[e] = part.reshape(16, 8, 128).astype(bf16)
         for k in others:
             to = turn(y, k)
             send(
-                d_act.at[half, :, pl.ds(4 * to, 4)], d_y.at[half, y],
-                dy_send, dy_recv.at[half, y], col=to * 4 + z,
+                d_act.at[pl.ds(first, size), pl.ds(4 * to, 4)],
+                d_y.at[y, pl.ds(first, size)],
+                dy_send, dy_recv.at[n, y], col=to * 4 + z,
             )
     for k in others:
         send(hidden, hidden_all.at[:, lanes_of(c)], h_send, h_recv.at[c], col=turn(y, k) * 4 + z)
@@ -299,25 +301,27 @@
             send(place, place, h_send, h_recv.at[slot], col=turn(y, k) * 4 + z)
     arrived(every_cot.at[across], cot_recv.at[across])
     send(every_cot.at[across], every_cot.at[across], cot_send, cot_recv.at[across], batch=sibling)
-    undo = ordering(128, 16)
-    for half in range(2):
-        d_y[half, y] = d_act[half, :, pl.ds(4 * y, 4)]
+    for n, (first, size) in enumerate(pieces):
+        d_z_out, d_z = z_out[n], z_in[n]
+        undo = ordering(8 * size, size)
+        span = pl.ds(first, size)
+        d_y[y, span] = d_act[span, pl.ds(4 * y, 4)]
         for k in others:
             f = turn(y, k)
-            arrived(d_y.at[half, f], dy_recv.at[half, f])
+            arrived(d_y.at[f, span], dy_recv.at[n, f])
         for q in range(4):
-            part = four([d_y[half, f, :, q].astype(f32) for f in range(4)])
-            rows = contract_first(undo, part.reshape(128, 128).astype(bf16))
+            part = four([d_y[f, span, q].astype(f32) for f in range(4)])
+            rows = contract_first(undo, part.reshape(8 * size, 128).astype(bf16))
             for g in range(4):
-                d_z_out[half, q * 4 + g] = (
-                    rows[g * 32 : (g + 1) * 32].reshape(2, 16, 128).astype(bf16)
+                d_z_out[q * 4 + g] = (
+                    rows[g * 2 * size : (g + 1) * 2 * size].reshape(2, size, 128).astype(bf16)
                 )
-        d_z[half, plane] = d_z_out[half, plane]
+        d_z[plane] = d_z_out[plane]
 
         def hand(k, _):
             peer = lax.rem(plane + k, 16)
             send(
-                d_z_out.at[half, peer], d_z.at[half, plane], dz_send, dz_recv.at[half],
+                d_z_out.at[peer], d_z.at[plane], dz_send.at[n], dz_recv.at[n],
                 col=y * 4 + peer // 4, row=lax.rem(peer, 4),
             )
             return 0
@@ -344,14 +348,14 @@
         grad_in[i, e] = part.astype(bf16)
     send(grad_in.at[i], grad_in.at[i], in_send, in_recv.at[i], batch=sibling)
     send(grad_in.at[i], grad_in.at[i], in_send, in_recv.at[i], batch=across)
-    for half in range(2):
-        arrived(d_z.at[half, pl.ds(0, 15)], dz_recv.at[half])
+    for n in range(len(pieces)):
+        arrived(z_in[n].at[pl.ds(0, 15)], dz_recv.at[n])
     for s in range(2):
         grad = jnp.concatenate(
             [
-                four([d_z[half, q * 4 + g, s].astype(f32) for q in range(4)])
+                four([d_z[q * 4 + g, s].astype(f32) for q in range(4)])
                 for g in range(4)
-                for half in range(2)
+                for d_z in z_in
             ],
             axis=0,
         )
@@ -436,8 +440,9 @@
     arrived(pre_x.at[three], pre_send)
     arrived(hidden_all.at[:, pl.ds(0, 15 * 128)], h_send)
     arrived(own_hidden.at[three], oh_send)
-    arrived(d_act.at[:, :, pl.ds(0, 12)], dy_send)
-    arrived(d_z.at[:, pl.ds(0, 15)], dz_send)
+    arrived(d_act.at[:, pl.ds(0, 12)], dy_send)
+    for n in range(len(pieces)):
+        arrived(z_out[n].at[pl.ds(0, 15)], dz_send.at[n])
     arrived(acts.at[three], acts_send)
     arrived(d_all.at[three], all_send)
     arrived(grad_in.at[three], in_send)
@@ -450,6 +455,7 @@
 def everything(emb, proj, w_in, bias, w_out, cot):
     out = jax.ShapeDtypeStruct
     pair = [DMA, DMA((4,))]
+    count = len(pieces)
     far = pl.BlockSpec(memory_space=pltpu.HBM)
     near = pl.BlockSpec(memory_space=VMEM)
     return pl.pallas_call(
@@ -487,10 +493,10 @@
             VMEM((4, 128, 128), f32),
             VMEM((128, 128), bf16),
             VMEM((128, 128), bf16),
-            VMEM((2, 16, 16, 8, 128), bf16),
-            VMEM((2, 4, 16, 4, 8, 128), bf16),
-            VMEM((2, 16, 2, 16, 128), bf16),
-            VMEM((2, 16, 2, 16, 128), bf16),
+            VMEM((32, 16, 8, 128), bf16),
+            VMEM((4, 32, 4, 8, 128), bf16),
+            tuple(VMEM((16, 2, size, 128), bf16) for _, size in pieces),
+            tuple(VMEM((16, 2, size, 128), bf16) for _, size in pieces),
             VMEM((4, 8, 16, 8, 128), bf16),
             VMEM((4, 128, 128), bf16),
             VMEM((4, 8, 128), f32),
@@ -504,7 +510,7 @@
             DMA, DMA((4,)), DMA, DMA, DMA, DMA, DMA, *pair,
             *pair, *pair, *pair,
             DMA, DMA, DMA((16,)), *pair,
-            DMA, DMA((16,)), *pair, DMA, DMA((2, 4)), DMA, DMA((2,)),
+            DMA, DMA((16,)), *pair, DMA, DMA((count, 4)), DMA((count,)), DMA((count,)),
             *pair, *pair, *pair, *pair,
             DMA, DMA, *pair, *pair, DMA,
         ],
@@ -515,14 +521,56 @@
     )(*[pltpu.with_memory_space_constraint(a, pltpu.HBM) for a in (emb, proj, w_in, bias, w_out, cot)])
 
 
+def finish_kernel(
+    mixed, grad_out, grad_in, grad_bias, grad_proj,
+    mixed_far, grad_out_far, grad_in_far, grad_bias_far, grad_proj_far,
+    wide, sems,
+):
+    copies = [
+        pltpu.make_async_copy(grad_out, grad_out_far, sems.at[0]),
+        pltpu.make_async_copy(mixed, mixed_far, sems.at[1]),
+        pltpu.make_async_copy(grad_bias.at[pl.ds(0, 1)], grad_bias_far, sems.at[2]),
+        pltpu.make_async_copy(grad_proj, grad_proj_far, sems.at[3]),
+    ]
+    for copy in copies:
+        copy.start()
+    for f in range(4):
+        wide[f] = grad_in[f].astype(f32)
+        copies.append(pltpu.make_async_copy(wide.at[f], grad_in_far.at[f], sems.at[4 + f]))
+        copies[-1].start()
+    for copy in copies:
+        copy.wait()
+
+
+def finish(mixed, grad_out, grad_in, grad_bias, grad_proj):
+    near = pl.BlockSpec(memory_space=VMEM)
+    far = pl.BlockSpec(memory_space=pltpu.HBM)
+    return pl.pallas_call(
+        finish_kernel,
+        out_shape=(
+            pltpu.HBM((128, 8, 128), bf16),
+            pltpu.HBM((4096, 128), f32),
+            pltpu.HBM((4, 8, 128, 128), f32),
+            pltpu.HBM((1, 128), f32),
+            pltpu.HBM((32, 128), f32),
+        ),
+        in_specs=[near] * 5,
+        out_specs=[far] * 5,
+        scratch_shapes=[VMEM((4, 8, 128, 128), f32), DMA((8,))],
+        compiler_params=pltpu.CompilerParams(vmem_limit_bytes=16 << 20),
+        name="finish",
+    )(mixed, grad_out, grad_in, grad_bias, grad_proj)
+
+
 def local(embeddings, projection, w_in, bias, w_out, cotangent):
-    mixed, grad_out, grad_in, grad_bias, grad_proj = everything(
+    results = everything(
         embeddings.reshape(64, 2, 8, 128), projection.T, w_in.reshape(32, 128, 128),
         bias.reshape(1, 128), w_out, cotangent,
     )
+    mixed, grad_out, grad_in, grad_bias, grad_proj = finish(*results)
     return (
-        mixed, grad_out.reshape(512, 8, 128), grad_in.astype(f32).reshape(4096, 128),
-        grad_bias[0], grad_proj.T,
+        mixed, grad_out.reshape(512, 8, 128), grad_in.reshape(4096, 128),
+        grad_bias.reshape(128), grad_proj.T,
     )
 
 

time: 92.7 us -> 90.2 us (0.973)
  local copies, waits for them, and re-layouts: 3.14 us -> 0 us
  Pallas kernels: 87.3 us -> 89.5 us
  other arithmetic: 1.52 us -> 0 us
    unnamed x3 -> x0, local copies, waits for them, and re-layouts: 2.63 us -> none
    pallas_call x0 -> x1, Pallas kernels: none -> 2.17 us  [finish(): pl.pallas_call(finish_kernel, out_shape=(pltpu.HBM((128, 8, 128), bf16),...]
    reshape x1 -> x0, other arithmetic: 1.52 us -> none  [local(): grad_in.astype(f32).reshape(4096, 128)]
where the time goes in v7:
time: 90.2 us; the launch traced here: 90.1 us
  Pallas kernels  89.5 us (99%)
    pallas_call x1, Pallas kernels, everything(): pl.pallas_call(kernel, out_shape=(out((128, 8, 128), bf16), out((4096, 12...  87.3 us
    pallas_call x1, Pallas kernels, finish(): pl.pallas_call(finish_kernel, out_shape=(pltpu.HBM((128, 8, 128), bf16),...  2.17 us

profile of v7, /device:TPU:1, one launch (start us, length us, event | category | flops | bytes accessed | tf_op | source)
XLA Modules:
  0.0 90.1 jit_solution(1762928326103221513)
XLA Ops:
  0.6 87.3 %block.1 = (bf16[128,8,128]{2,1,0:T(8,128)(2,1)S(1)}, f32[4096,128]{1,0:T(8,128)S(1)}, bf16[4,8,128,128]{3,2,1,0:T(8,128)(2,1)S(1)}, f32[8,128]{1,0:T(8,128)S(1)}, f32[32,128]{1,0:T(8,128)S(1)}) custom-call(bf16[64,2,8,128]{3,2,1,0:T(8,128)(2,1)} %bitcast.9, bf16[32,512]{1,0:T(8,128)(2,1)} %bitcast.10, bf16[32,128,128]{2,1,0:T(8,128)(2,1)} %bitcast.8, ...), custom_call_target="tpu_custom_call" | custom-call | tf_op jit(solution)/shard_map/block/pallas_call | solution.py:461
  88.0 2.2 %finish.1 = (bf16[128,8,128]{2,1,0:T(8,128)(2,1)}, f32[4096,128]{1,0:T(8,128)}, f32[4,8,128,128]{3,2,1,0:T(8,128)}, f32[1,128]{1,0:T(1,128)}, f32[32,128]{1,0:T(8,128)}) custom-call(bf16[128,8,128]{2,1,0:T(8,128)(2,1)S(1)} %get-tuple-element.15.mixed, f32[4096,128]{1,0:T(8,128)S(1)} %get-tuple-element.16.grad_out, ...), custom_call_target="tpu_custom_call" | custom-call | tf_op jit(solution)/shard_map/finish/pallas_call | solution.py:548

commit v8 on v7

--- a/solution.py
+++ b/solution.py
@@ -11,7 +11,7 @@
 MESH = pl.DeviceIdType.MESH
 VMEM = pltpu.VMEM
 DMA = pltpu.SemaphoreType.DMA
-others = (1, 2, 3)
+others = (2, 1, 3)
 pieces = ((0, 16), (16, 16))
 
 
@@ -70,7 +70,7 @@
 def kernel(
     emb, proj_far, w_in_far, bias_far, w_out_far, cot_far,
     mixed, grad_out, grad_in, grad_bias, grad_proj,
-    proj, w_in, bias, w_out, cot, w_split, stage, every_cot, own_emb, folds, normed, inv,
+    proj, w_in, w_turned, bias, w_out, cot, w_split, stage, every_cot, own_emb, folds, normed, inv,
     part_out, part_y, part_z_out, part_z, part_x,
     to_row, raw, gathered, pre_x, hidden, d_pre_b,
     d_act, d_y, z_out, z_in, acts, d_all, bias_all, hidden_all, own_hidden, hidden_t,
@@ -95,7 +95,7 @@
     barrier = pltpu.get_barrier_semaphore()
 
     def greet(k, _):
-        peer = lax.rem(me + k, 64)
+        peer = lax.rem(me + 1 + lax.rem(k + 40, 63), 64)
         pl.semaphore_signal(
             barrier, inc=1, device_id={"col": peer // 4, "row": lax.rem(peer, 4)},
             device_id_type=MESH,
@@ -153,7 +153,7 @@
     keep.start()
 
     def give(k, _):
-        peer = lax.rem(me + k, 64)
+        peer = lax.rem(me + 1 + lax.rem(k + 40, 63), 64)
         send(
             emb.at[peer], own_emb.at[r, :, c], emb_send, emb_recv,
             col=peer // 4, row=lax.rem(peer, 4),
@@ -200,7 +200,7 @@
     plane = z * 4 + r
 
     def scatter(k, _):
-        peer = lax.rem(plane + k, 16)
+        peer = lax.rem(plane + 1 + lax.rem(k + 8, 15), 16)
         to_z = peer // 4
         to_r = lax.rem(peer, 4)
         send(to_row.at[to_r], raw.at[c, r], near_send, raw_recv.at[c], col=y * 4 + to_z, row=to_r)
@@ -242,6 +242,8 @@
     for k in others:
         send(part_x.at[r], part_x.at[r], px_send, px_recv.at[r], row=turn(r, k))
     take_in.wait()
+    for e in range(32):
+        w_turned[e] = jnp.transpose(w_in[e])
     for k in range(4):
         for m in others:
             slot = turn(y, m) * 4 + turn(z, k)
@@ -276,7 +278,7 @@
         send(hidden, hidden_all.at[:, lanes_of(c)], h_send, h_recv.at[c], col=y * 4 + turn(z, k))
     for n, (first, size) in enumerate(pieces):
         for e in range(first, first + size):
-            part = contract_last(d_pre_b[...], w_in[e])
+            part = dot(d_pre_b[...], w_turned[e])
             d_act[e] = part.reshape(16, 8, 128).astype(bf16)
         for k in others:
             to = turn(y, k)
@@ -319,7 +321,7 @@
         d_z[plane] = d_z_out[plane]
 
         def hand(k, _):
-            peer = lax.rem(plane + k, 16)
+            peer = lax.rem(plane + 1 + lax.rem(k + 8, 15), 16)
             send(
                 d_z_out.at[peer], d_z.at[plane], dz_send.at[n], dz_recv.at[n],
                 col=y * 4 + peer // 4, row=lax.rem(peer, 4),
@@ -331,12 +333,6 @@
         for k in range(4):
             slot = turn(y, m) * 4 + k
             arrived(hidden_all.at[:, lanes_of(slot)], h_recv.at[slot])
-    for k in others:
-        to = turn(i, k)
-        send(
-            hidden_all.at[:, lanes_of(to, 512)], own_hidden.at[i], oh_send, oh_recv.at[i],
-            batch=to,
-        )
     own_hidden[i] = hidden_all[:, lanes_of(i, 512)]
     mine.wait()
     for k in others:
@@ -350,6 +346,12 @@
     send(grad_in.at[i], grad_in.at[i], in_send, in_recv.at[i], batch=across)
     for n in range(len(pieces)):
         arrived(z_in[n].at[pl.ds(0, 15)], dz_recv.at[n])
+    for k in others:
+        to = turn(i, k)
+        send(
+            hidden_all.at[:, lanes_of(to, 512)], own_hidden.at[i], oh_send, oh_recv.at[i],
+            batch=to,
+        )
     for s in range(2):
         grad = jnp.concatenate(
             [
@@ -380,7 +382,7 @@
     proj_x[flat] = proj_out[r]
 
     def hand_on(k, _):
-        peer = lax.rem(flat + k, 16)
+        peer = lax.rem(flat + 1 + lax.rem(k + 8, 15), 16)
         to_r = lax.rem(peer, 4)
         send(
             proj_out.at[to_r], proj_x.at[flat], gx_send, gx_recv,
@@ -396,6 +398,12 @@
     proj_z[z] = four([four([proj_x[q * 4 + g] for g in range(4)]) for q in range(4)])
     for k in others:
         send(proj_z.at[z], proj_z.at[z], gz_send, gz_recv.at[z], col=y * 4 + turn(z, k))
+    for k in others:
+        f = turn(z, k)
+        arrived(proj_z.at[f], gz_recv.at[f])
+    proj_b[i] = four(proj_z)
+    for k in others:
+        send(proj_b.at[i], proj_b.at[i], gb_send, gb_recv.at[i], batch=turn(i, k))
     arrived(grad_in.at[across], in_recv.at[across])
     send(grad_in.at[across], grad_in.at[across], in_send, in_recv.at[across], batch=sibling)
     for k in others:
@@ -412,12 +420,6 @@
 
     for d in range(4):
         outer(d)
-    for k in others:
-        f = turn(z, k)
-        arrived(proj_z.at[f], gz_recv.at[f])
-    proj_b[i] = four(proj_z)
-    for k in others:
-        send(proj_b.at[i], proj_b.at[i], gb_send, gb_recv.at[i], batch=turn(i, k))
     for d in range(4, 8):
         outer(d)
     for k in others:
@@ -471,6 +473,7 @@
         out_specs=[near] * 5,
         scratch_shapes=[
             VMEM((32, 512), bf16),
+            VMEM((32, 128, 128), bf16),
             VMEM((32, 128, 128), bf16),
             VMEM((1, 128), f32),
             VMEM((2048, 8, 128), bf16),

time: 90.2 us -> 89.6 us (level)
  no operation moved by 1% of the time
where the time goes in v8:
time: 89.6 us; the launch traced here: 89.5 us
  Pallas kernels  88.9 us (99%)
    pallas_call x1, Pallas kernels, everything(): pl.pallas_call(kernel, out_shape=(out((128, 8, 128), bf16), out((4096, 12...  86.7 us
    pallas_call x1, Pallas kernels, finish(): pl.pallas_call(finish_kernel, out_shape=(pltpu.HBM((128, 8, 128), bf16),...  2.17 us

profile of v8, /device:TPU:1, one launch (start us, length us, event | category | flops | bytes accessed | tf_op | source)
XLA Modules:
  0.0 89.5 jit_solution(5307440975817904116)
XLA Ops:
  0.6 86.7 %block.1 = (bf16[128,8,128]{2,1,0:T(8,128)(2,1)S(1)}, f32[4096,128]{1,0:T(8,128)S(1)}, bf16[4,8,128,128]{3,2,1,0:T(8,128)(2,1)S(1)}, f32[8,128]{1,0:T(8,128)S(1)}, f32[32,128]{1,0:T(8,128)S(1)}) custom-call(bf16[64,2,8,128]{3,2,1,0:T(8,128)(2,1)} %bitcast.9, bf16[32,512]{1,0:T(8,128)(2,1)} %bitcast.10, bf16[32,128,128]{2,1,0:T(8,128)(2,1)} %bitcast.8, ...), custom_call_target="tpu_custom_call" | custom-call | tf_op jit(solution)/shard_map/block/pallas_call | solution.py:463
  87.3 2.2 %finish.1 = (bf16[128,8,128]{2,1,0:T(8,128)(2,1)}, f32[4096,128]{1,0:T(8,128)}, f32[4,8,128,128]{3,2,1,0:T(8,128)}, f32[1,128]{1,0:T(1,128)}, f32[32,128]{1,0:T(8,128)}) custom-call(bf16[128,8,128]{2,1,0:T(8,128)(2,1)S(1)} %get-tuple-element.15.mixed, f32[4096,128]{1,0:T(8,128)S(1)} %get-tuple-element.16.grad_out, ...), custom_call_target="tpu_custom_call" | custom-call | tf_op jit(solution)/shard_map/finish/pallas_call | solution.py:551

commit v9 on v8

--- a/solution.py
+++ b/solution.py
@@ -69,11 +69,11 @@
 
 def kernel(
     emb, proj_far, w_in_far, bias_far, w_out_far, cot_far,
-    mixed, grad_out, grad_in, grad_bias, grad_proj,
+    mixed, grad_out, grad_wide, grad_bias, grad_proj,
     proj, w_in, w_turned, bias, w_out, cot, w_split, stage, every_cot, own_emb, folds, normed, inv,
     part_out, part_y, part_z_out, part_z, part_x,
     to_row, raw, gathered, pre_x, hidden, d_pre_b,
-    d_act, d_y, z_out, z_in, acts, d_all, bias_all, hidden_all, own_hidden, hidden_t,
+    d_act, d_y, z_out, z_in, grad_in, acts, d_all, bias_all, hidden_all, own_hidden, hidden_t,
     proj_out, proj_x, proj_z, proj_b,
     load_in, load_out, load_cot, load_proj, load_bias, emb_send, emb_recv, cot_send, cot_recv,
     py_send, py_recv, pz_send, pz_recv, px_send, px_recv,
@@ -344,6 +344,7 @@
         grad_in[i, e] = part.astype(bf16)
     send(grad_in.at[i], grad_in.at[i], in_send, in_recv.at[i], batch=sibling)
     send(grad_in.at[i], grad_in.at[i], in_send, in_recv.at[i], batch=across)
+    grad_wide[i] = grad_in[i].astype(f32)
     for n in range(len(pieces)):
         arrived(z_in[n].at[pl.ds(0, 15)], dz_recv.at[n])
     for k in others:
@@ -406,6 +407,9 @@
         send(proj_b.at[i], proj_b.at[i], gb_send, gb_recv.at[i], batch=turn(i, k))
     arrived(grad_in.at[across], in_recv.at[across])
     send(grad_in.at[across], grad_in.at[across], in_send, in_recv.at[across], batch=sibling)
+    grad_wide[across] = grad_in[across].astype(f32)
+    arrived(grad_in.at[sibling], in_recv.at[sibling])
+    grad_wide[sibling] = grad_in[sibling].astype(f32)
     for k in others:
         f = turn(i, k)
         arrived(own_hidden.at[f], oh_recv.at[f])
@@ -430,8 +434,8 @@
         f = turn(i, k)
         arrived(proj_b.at[f], gb_recv.at[f])
     grad_proj[...] = four(proj_b)
-    arrived(grad_in.at[sibling], in_recv.at[sibling])
     arrived(grad_in.at[diagonal], in_recv.at[diagonal])
+    grad_wide[diagonal] = grad_in[diagonal].astype(f32)
     arrived(emb.at[pl.ds(0, 63)], emb_send)
     arrived(every_cot.at[three], cot_send)
     arrived(part_y.at[three], py_send)
@@ -465,7 +469,7 @@
         out_shape=(
             out((128, 8, 128), bf16),
             out((4096, 128), f32),
-            out((4, 8, 128, 128), bf16),
+            out((4, 8, 128, 128), f32),
             out((8, 128), f32),
             out((32, 128), f32),
         ),
@@ -500,6 +504,7 @@
             VMEM((4, 32, 4, 8, 128), bf16),
             tuple(VMEM((16, 2, size, 128), bf16) for _, size in pieces),
             tuple(VMEM((16, 2, size, 128), bf16) for _, size in pieces),
+            VMEM((4, 8, 128, 128), bf16),
             VMEM((4, 8, 16, 8, 128), bf16),
             VMEM((4, 128, 128), bf16),
             VMEM((4, 8, 128), f32),
@@ -527,20 +532,17 @@
 def finish_kernel(
     mixed, grad_out, grad_in, grad_bias, grad_proj,
     mixed_far, grad_out_far, grad_in_far, grad_bias_far, grad_proj_far,
-    wide, sems,
+    sems,
 ):
     copies = [
         pltpu.make_async_copy(grad_out, grad_out_far, sems.at[0]),
+        pltpu.make_async_copy(grad_in, grad_in_far, sems.at[4]),
         pltpu.make_async_copy(mixed, mixed_far, sems.at[1]),
         pltpu.make_async_copy(grad_bias.at[pl.ds(0, 1)], grad_bias_far, sems.at[2]),
         pltpu.make_async_copy(grad_proj, grad_proj_far, sems.at[3]),
     ]
     for copy in copies:
         copy.start()
-    for f in range(4):
-        wide[f] = grad_in[f].astype(f32)
-        copies.append(pltpu.make_async_copy(wide.at[f], grad_in_far.at[f], sems.at[4 + f]))
-        copies[-1].start()
     for copy in copies:
         copy.wait()
 
@@ -559,7 +561,7 @@
         ),
         in_specs=[near] * 5,
         out_specs=[far] * 5,
-        scratch_shapes=[VMEM((4, 8, 128, 128), f32), DMA((8,))],
+        scratch_shapes=[DMA((5,))],
         compiler_params=pltpu.CompilerParams(vmem_limit_bytes=16 << 20),
         name="finish",
     )(mixed, grad_out, grad_in, grad_bias, grad_proj)

time: 89.6 us -> 89.6 us (level)
  no operation moved by 1% of the time
where the time goes in v9:
time: 89.6 us; the launch traced here: 89.5 us
  Pallas kernels  88.9 us (99%)
    pallas_call x1, Pallas kernels, everything(): pl.pallas_call(kernel, out_shape=(out((128, 8, 128), bf16), out((4096, 12...  86.7 us
    pallas_call x1, Pallas kernels, finish(): pl.pallas_call(finish_kernel, out_shape=(pltpu.HBM((128, 8, 128), bf16),...  2.13 us

profile of v9, /device:TPU:1, one launch (start us, length us, event | category | flops | bytes accessed | tf_op | source)
XLA Modules:
  0.0 89.5 jit_solution(14349585580587848998)
XLA Ops:
  0.6 86.7 %block.1 = (bf16[128,8,128]{2,1,0:T(8,128)(2,1)S(1)}, f32[4096,128]{1,0:T(8,128)S(1)}, f32[4,8,128,128]{3,2,1,0:T(8,128)S(1)}, f32[8,128]{1,0:T(8,128)S(1)}, f32[32,128]{1,0:T(8,128)S(1)}) custom-call(bf16[64,2,8,128]{3,2,1,0:T(8,128)(2,1)} %bitcast.9, bf16[32,512]{1,0:T(8,128)(2,1)} %bitcast.10, bf16[32,128,128]{2,1,0:T(8,128)(2,1)} %bitcast.8, ...), custom_call_target="tpu_custom_call" | custom-call | tf_op jit(solution)/shard_map/block/pallas_call | solution.py:467
  87.4 2.1 %finish.1 = (bf16[128,8,128]{2,1,0:T(8,128)(2,1)}, f32[4096,128]{1,0:T(8,128)}, f32[4,8,128,128]{3,2,1,0:T(8,128)}, f32[1,128]{1,0:T(1,128)}, f32[32,128]{1,0:T(8,128)}) custom-call(bf16[128,8,128]{2,1,0:T(8,128)(2,1)S(1)} %get-tuple-element.15.mixed, f32[4096,128]{1,0:T(8,128)S(1)} %get-tuple-element.16.grad_out, ...), custom_call_target="tpu_custom_call" | custom-call | tf_op jit(solution)/shard_map/finish/pallas_call | solution.py:553

commit v10 on v8

--- a/solution.py
+++ b/solution.py
@@ -334,6 +334,9 @@
             slot = turn(y, m) * 4 + k
             arrived(hidden_all.at[:, lanes_of(slot)], h_recv.at[slot])
     own_hidden[i] = hidden_all[:, lanes_of(i, 512)]
+    for d in range(8):
+        stage[pl.ds(d, 128, stride=8), :] = dot(hidden_all[...], w_split[d])
+    mixed[...] = stage[...].reshape(128, 8, 128).astype(bf16)
     mine.wait()
     for k in others:
         f = turn(i, k)
@@ -391,9 +394,6 @@
         return 0
 
     lax.fori_loop(1, 16, hand_on, 0)
-    for d in range(8):
-        stage[pl.ds(d, 128, stride=8), :] = dot(hidden_all[...], w_split[d])
-    mixed[...] = stage[...].reshape(128, 8, 128).astype(bf16)
     arrived(proj_x.at[pl.ds(0, 15)], gx_recv)
     proj_z[z] = four([four([proj_x[q * 4 + g] for g in range(4)]) for q in range(4)])
     for k in others:

time: 89.6 us -> 89.4 us (level)
  no operation moved by 1% of the time
where the time goes in v10:
time: 89.4 us; the launch traced here: 88.8 us
  Pallas kernels  88.1 us (99%)
    pallas_call x1, Pallas kernels, everything(): pl.pallas_call(kernel, out_shape=(out((128, 8, 128), bf16), out((4096, 12...  86 us
    pallas_call x1, Pallas kernels, finish(): pl.pallas_call(finish_kernel, out_shape=(pltpu.HBM((128, 8, 128), bf16),...  2.17 us

profile of v10, /device:TPU:1, one launch (start us, length us, event | category | flops | bytes accessed | tf_op | source)
XLA Modules:
  0.0 88.8 jit_solution(760255558248397401)
XLA Ops:
  0.6 86.0 %block.1 = (bf16[128,8,128]{2,1,0:T(8,128)(2,1)S(1)}, f32[4096,128]{1,0:T(8,128)S(1)}, bf16[4,8,128,128]{3,2,1,0:T(8,128)(2,1)S(1)}, f32[8,128]{1,0:T(8,128)S(1)}, f32[32,128]{1,0:T(8,128)S(1)}) custom-call(bf16[64,2,8,128]{3,2,1,0:T(8,128)(2,1)} %bitcast.9, bf16[32,512]{1,0:T(8,128)(2,1)} %bitcast.10, bf16[32,128,128]{2,1,0:T(8,128)(2,1)} %bitcast.8, ...), custom_call_target="tpu_custom_call" | custom-call | tf_op jit(solution)/shard_map/block/pallas_call | solution.py:463
  86.6 2.2 %finish.1 = (bf16[128,8,128]{2,1,0:T(8,128)(2,1)}, f32[4096,128]{1,0:T(8,128)}, f32[4,8,128,128]{3,2,1,0:T(8,128)}, f32[1,128]{1,0:T(1,128)}, f32[32,128]{1,0:T(8,128)}) custom-call(bf16[128,8,128]{2,1,0:T(8,128)(2,1)S(1)} %get-tuple-element.15.mixed, f32[4096,128]{1,0:T(8,128)S(1)} %get-tuple-element.16.grad_out, ...), custom_call_target="tpu_custom_call" | custom-call | tf_op jit(solution)/shard_map/finish/pallas_call | solution.py:551
